TPU v7x, 32 devices: a whole 2x2x4 slice. The times are simulated.
32 devices in a mesh: row: 16 (over z, y, x), col: 2 (over core).
Axes of the slice: x: 2, y: 2, z: 4, core: 2. Of those that a mesh axis runs over, the one named last changes fastest.
Arguments:
- panel: bfloat16 [4096, 256], P('row', 'col'), may hold values from -0.1875 to 0.1875
- trailing: bfloat16 [4096, 4096], P('row', 'col'), may hold values from -6 to 6
- tile_mask: int32 [16, 16], P('row', 'col'), may hold values 0 or 1
Outputs:
- r_factor: float32 [256, 256], replicated
- coupling: bfloat16 [256, 4096], P(None, 'col')
- updated: bfloat16 [4096, 4096], P('row', 'col')
All inputs are finite; a program needn't handle non-finite values. No bound on the sum of `tile_mask` on one device may be relied on, other than what follows from the above.
Results may differ from a plain program's by a relative error of at most 0.0023.
Values may be sent and summed in bfloat16 or wider, within the bound.
No kernel may reach another device: no remote copies, remote signals or barrier semaphores. Data moves between devices by JAX's collectives and lax.ppermute only.
A program may use at most 128 MiB of HBM per device.

v0:
```python
import jax
import jax.numpy as jnp
from jax import lax
from jax.sharding import PartitionSpec as P

TILE = 256


damping_total = 0.5


def inner_product(left, right):
    return lax.dot_general(
        left, right, (((0,), (0,)), ((), ())), preferred_element_type=jnp.float32
    )


def small_pair(gram):
    order = gram.shape[0]
    places = jnp.arange(order, dtype=jnp.int32)
    rows_list = []
    for index in range(order):
        values = gram[index, :]
        if index > 0:
            done = jnp.stack(rows_list, axis=0)
            values = values - jnp.dot(done[:, index], done, precision=lax.Precision.HIGHEST)
        pivot = jnp.sqrt(values[index])
        rows_list.append(jnp.where(places >= index, values / pivot, jnp.zeros_like(values)))
    factor = jnp.stack(rows_list, axis=0)
    inv_rows = [None] * order
    for index in range(order - 1, -1, -1):
        unit = (places == index).astype(gram.dtype)
        if index < order - 1:
            later = jnp.stack(inv_rows[index + 1 :], axis=0)
            unit = unit - jnp.dot(
                factor[index, index + 1 :], later, precision=lax.Precision.HIGHEST
            )
        inv_rows[index] = unit / factor[index, index]
    return (factor, jnp.stack(inv_rows, axis=0))


def cholesky_pair(gram):
    order = gram.shape[0]
    if order <= 16:
        return small_pair(gram)
    half = order // 2
    upper_a, inverse_a = cholesky_pair(gram[:half, :half])
    upper_b = jnp.dot(inverse_a.T, gram[:half, half:], precision=lax.Precision.HIGHEST)
    schur = gram[half:, half:] - jnp.dot(upper_b.T, upper_b, precision=lax.Precision.HIGHEST)
    upper_c, inverse_c = cholesky_pair(schur)
    inverse_b = -jnp.dot(
        jnp.dot(inverse_a, upper_b, precision=lax.Precision.HIGHEST),
        inverse_c,
        precision=lax.Precision.HIGHEST,
    )
    lower_zero = jnp.zeros((order - half, half), gram.dtype)
    factor = jnp.concatenate(
        [
            jnp.concatenate([upper_a, upper_b], axis=1),
            jnp.concatenate([lower_zero, upper_c], axis=1),
        ],
        axis=0,
    )
    inverse = jnp.concatenate(
        [
            jnp.concatenate([inverse_a, inverse_b], axis=1),
            jnp.concatenate([lower_zero, inverse_c], axis=1),
        ],
        axis=0,
    )
    return (factor, inverse)


def apply_inverse(inverse, values):
    return jnp.dot(inverse.T, values, precision=lax.Precision.HIGHEST)


def local(panel, trailing, tile_mask):
    gathered = lax.all_gather(panel, "col", axis=1, tiled=True)
    local_rows = trailing.shape[0]
    local_cols = trailing.shape[1]
    tiles = trailing.reshape(local_rows // TILE, TILE, local_cols // TILE, TILE)
    masked = (tiles * tile_mask.astype(jnp.bfloat16)[:, None, :, None]).reshape(
        local_rows, local_cols
    )
    identity = jnp.eye(gathered.shape[1], dtype=jnp.float32)
    gram_local = inner_product(gathered, gathered)
    cross_terms = inner_product(gathered, masked)
    gram_total, summed = lax.psum((gram_local, cross_terms), "row")
    upper_factor, inverse = cholesky_pair(gram_total + damping_total * identity)
    coupling = apply_inverse(inverse, summed).astype(jnp.bfloat16)
    basis_t = apply_inverse(inverse, gathered.astype(jnp.float32).T).astype(jnp.bfloat16)
    removed = inner_product(basis_t, coupling)
    updated = (masked.astype(jnp.float32) - removed).astype(jnp.bfloat16)
    return (upper_factor, coupling, updated)


def solution(mesh):
    placed = (P("row", "col"), P("row", "col"), P("row", "col"))
    return jax.shard_map(
        local,
        mesh=mesh,
        in_specs=placed,
        out_specs=(P(), P(None, "col"), P("row", "col")),
        check_vma=False,
    )
```

profile of v0, /device:TPU:0, one launch (start us, length us, event | category | flops | bytes accessed | tf_op | source)
XLA Modules:
  0.0 979.8 jit_solution(17785703045218473414)
XLA Ops:
  8.0 2.2 all_gather.3
  10.2 0.9 fusion.2087
  11.1 3.0 convolution_bitcast_fusion
  14.2 134.3 %all-reduce.33.cloned.1.call-done = (f32[256,256]{1,0:T(8,128)}, f32[256,2048]{0,1:T(8,128)}) async-done(((f32[256,256]{1,0:T(8,128)}, f32[256,2048]{0,1:T(8,128)}), (f32[256,256]{1,0:T(8,128)}, f32[256,2048]{0,1:T(8,128)})) %all-reduce.33.cloned.1.call-update) | async-done | bytes 2359312 | tf_op jit(solution)/shard_map/psum | solution.py:89
  148.5 1.0 select_add_fusion
  186.3 1.2 divide_bitcast_fusion.15
  188.3 0.9 fusion.457
  190.9 0.9 fusion.466
  191.8 0.9 fusion.469
  237.0 1.2 divide_bitcast_fusion.14
  239.1 0.9 fusion.481
  241.7 0.9 fusion.490
  242.6 0.9 fusion.493
  287.9 1.2 divide_bitcast_fusion.13
  290.0 0.9 fusion.505
  292.6 0.9 fusion.514
  293.5 0.9 fusion.517
  338.8 1.2 divide_bitcast_fusion.12
  340.9 0.9 fusion.529
  343.5 0.9 fusion.538
  344.4 0.9 fusion.541
  390.3 1.2 divide_bitcast_fusion.11
  395.0 0.9 fusion.562
  395.9 0.9 fusion.565
  441.1 1.2 divide_bitcast_fusion.10
  445.8 0.9 fusion.586
  446.7 0.9 fusion.589
  492.0 1.2 divide_bitcast_fusion.9
  496.6 0.9 fusion.610
  497.6 0.9 fusion.613
  543.2 1.2 divide_bitcast_fusion.8
  545.2 0.9 fusion.625
  547.8 0.9 fusion.634
  548.7 0.9 fusion.637
  594.8 1.2 divide_bitcast_fusion.7
  596.9 0.9 fusion.649
  599.5 0.9 fusion.658
  600.4 0.9 fusion.661
  645.5 1.2 divide_bitcast_fusion.6
  650.2 0.9 fusion.682
  651.1 0.9 fusion.685
  696.4 1.2 divide_bitcast_fusion.5
  698.5 0.9 fusion.697
  701.1 0.9 fusion.706
  702.0 0.9 fusion.709
  747.4 1.2 divide_bitcast_fusion.4
  752.0 0.9 fusion.730
  753.0 0.9 fusion.733
  798.7 1.2 divide_bitcast_fusion.3
  803.4 0.9 fusion.754
  804.3 0.9 fusion.757
  849.5 1.2 divide_bitcast_fusion.2
  851.6 0.9 fusion.769
  854.2 0.9 fusion.778
  855.1 0.9 fusion.781
  900.5 1.2 divide_bitcast_fusion.1
  902.6 0.9 fusion.793
  905.2 0.9 fusion.802
  906.1 0.9 fusion.805
  952.1 1.2 divide_bitcast_fusion
  956.8 0.9 fusion.826
  957.7 0.9 fusion.829
  966.9 2.9 convolution_convert_fusion
  970.1 1.4 fusion
  (1958 shorter events, 572.0 us)
Async XLA Ops:
  7.2 141.3 %all-reduce.33.cloned.1.call-start = ((), (), s32[]{:S(2)}) async-start(), calls=%async_computation | async-start | bytes 4718592 | tf_op jit(solution)/shard_map/psum | solution.py:89
  898.3 68.6 %copy-start.2 = (f32[256,2048]{0,1:T(8,128)S(1)}, f32[256,2048]{0,1:T(8,128)}, u32[]{:S(2)}) copy-start(f32[256,2048]{0,1:T(8,128)} %get-tuple-element.4) | copy-start | bytes 6291460
  966.9 3.2 copy-start.1
  969.8 2.9 copy-start
Sparse Core Ops, SparseCore 0:
  14.4 134.0 all-reduce.32
where the time goes:
time: 994 us; the launch traced here: 980 us
  local copies, waits for them, and re-layouts  366 us (37%)
  matrix products  235 us (24%)
  between operations  207 us (21%)
  waiting for transfers between devices  134 us (13%)
  other arithmetic  35.1 us (4%)
    dot_general x224, matrix products, small_pair(): jnp.dot(factor[index, index + 1:], later, precision=lax.Precision.HIGHEST)  186 us
    slice x256, local copies, waits for them, and re-layouts, small_pair(): pivot = jnp.sqrt(values[index])  152 us
    slice x240, local copies, waits for them, and re-layouts, small_pair(): inv_rows[index] = unit / factor[index, index]  147 us
    psum x1, waiting for transfers between devices, local(): gram_total, summed = lax.psum((gram_local, cross_terms), 'row')  134 us
    slice x224, local copies, waits for them, and re-layouts, small_pair(): done[:, index]  41.7 us
    dot_general x224, matrix products, small_pair(): jnp.dot(done[:, index], done, precision=lax.Precision.HIGHEST)  29 us
  transfers between devices with their start and end apart: 1, of which 1 were waited for; matrix products, arithmetic and copies ran while one was open for 0% of the time, Pallas kernels for 0%

commit v1 on v0

v1 whole, which is shorter than its diff:
```python
import functools

import jax
import jax.numpy as jnp
from jax import lax
from jax.experimental import pallas as pl
from jax.experimental.pallas import tpu as pltpu
from jax.sharding import PartitionSpec as P

TILE = 256
BLOCK = 64
HIGHEST = lax.Precision.HIGHEST


damping_total = 0.5


def inner_product(left, right):
    return lax.dot_general(
        left, right, (((0,), (0,)), ((), ())), preferred_element_type=jnp.float32
    )


def eliminate(groups, base, lane):
    sub = lax.broadcasted_iota(jnp.int32, (8, 1), 0)
    for step in range(0, 8 * len(groups), 2):
        g, r = divmod(step, 8)
        j = base + step
        row0 = groups[g][r : r + 1, :]
        row1 = groups[g][r + 1 : r + 2, :]
        a = row0[:, j : j + 1]
        b = row0[:, j + 1 : j + 2]
        c = row1[:, j + 1 : j + 2]
        inv_a = 1.0 / a
        inv_d = a / (a * c - b * b)
        l = b * inv_a
        at0 = lane == j
        at1 = lane == j + 1
        q0 = (row0 + jnp.where(at0, 1.0, 0.0)) * inv_a
        row1 = jnp.where(at0, -l, row1 - l * row0)
        q1 = (row1 + jnp.where(at1, 1.0, 0.0)) * inv_d
        for i in range(g, len(groups)):
            m0 = groups[i][:, j : j + 1]
            m1 = groups[i][:, j + 1 : j + 2] - l * m0
            if i == g:
                m0 = jnp.where(sub > r, m0, 0.0)
                m1 = jnp.where(sub > r + 1, m1, 0.0)
            groups[i] = groups[i] - m0 * q0 - m1 * q1
    return groups


def factor_kernel(gram_ref, factor_ref, inverse_t_ref, work):
    order = gram_ref.shape[0]
    work[...] = gram_ref[...]
    lane = lax.broadcasted_iota(jnp.int32, (1, order), 1)
    for base in range(0, order, BLOCK):
        end = base + BLOCK
        groups = [work[base + i : base + i + 8, :] for i in range(0, BLOCK, 8)]
        block = jnp.concatenate(eliminate(groups, base, lane), axis=0)
        rows = base + lax.broadcasted_iota(jnp.int32, (BLOCK, order), 0)
        cols = lax.broadcasted_iota(jnp.int32, (BLOCK, order), 1)
        pivots = jnp.sum(jnp.where(rows == cols, block, 0.0), axis=1, keepdims=True)
        scale = lax.rsqrt(pivots)
        scaled = block * scale
        lower = jnp.where(cols < rows, scaled, jnp.where(cols == rows, scale, 0.0))
        factor_ref[base:end, :] = jnp.where(cols >= rows, scaled, 0.0)
        inverse_t_ref[base:end, :] = lower
        if end < order:
            rest = jnp.where((lane >= base) & (lane < end), 0.0, work[end:, :])
            work[end:, :] = rest - lax.dot_general(
                scaled[:, end:],
                jnp.where(cols < end, lower, scaled),
                (((0,), (0,)), ((), ())),
                precision=HIGHEST,
                preferred_element_type=jnp.float32,
            )


def cholesky_pair(gram):
    order = gram.shape[0]
    out = jax.ShapeDtypeStruct((order, order), jnp.float32)
    return pl.pallas_call(
        factor_kernel,
        out_shape=[out, out],
        scratch_shapes=[pltpu.VMEM((order, order), jnp.float32)],
        name="factor",
    )(gram)


def local(panel, trailing, tile_mask):
    gathered = lax.all_gather(panel, "col", axis=1, tiled=True)
    local_rows = trailing.shape[0]
    local_cols = trailing.shape[1]
    tiles = trailing.reshape(local_rows // TILE, TILE, local_cols // TILE, TILE)
    masked = (tiles * tile_mask.astype(jnp.bfloat16)[:, None, :, None]).reshape(
        local_rows, local_cols
    )
    identity = jnp.eye(gathered.shape[1], dtype=jnp.float32)
    gram_local = inner_product(gathered, gathered)
    cross_terms = inner_product(gathered, masked)
    gram_total, summed = lax.psum((gram_local, cross_terms), "row")
    upper_factor, inverse_t = cholesky_pair(gram_total + damping_total * identity)
    coupling = jnp.dot(inverse_t, summed, precision=HIGHEST).astype(jnp.bfloat16)
    basis_t = jnp.dot(
        inverse_t, gathered.astype(jnp.float32).T, precision=HIGHEST
    ).astype(jnp.bfloat16)
    removed = inner_product(basis_t, coupling)
    updated = (masked.astype(jnp.float32) - removed).astype(jnp.bfloat16)
    return (upper_factor, coupling, updated)


def solution(mesh):
    placed = (P("row", "col"), P("row", "col"), P("row", "col"))
    return jax.shard_map(
        local,
        mesh=mesh,
        in_specs=placed,
        out_specs=(P(), P(None, "col"), P("row", "col")),
        check_vma=False,
    )
```

time: 994 us -> 188 us (0.19); the launches traced: 980 us -> 187 us
  local copies, waits for them, and re-layouts: 366 us -> 0.09 us
  matrix products: 235 us -> 10.3 us
  between operations: 207 us -> 14.1 us
  other arithmetic: 35.1 us -> 2.33 us
  Pallas kernels: 0 us -> 23.9 us
    slice x736 -> x0, local copies, waits for them, and re-layouts: 350 us -> none  [the longest x256 152 us: small_pair(): pivot = jnp.sqrt(values[index])]
    dot_general x510 -> x2, matrix products: 230 us -> 4.91 us  [the longest x1 3.62 us: local(): jnp.dot(inverse_t, summed, precision=HIGHEST).astype(jnp.bfloat16)]
    pallas_call x0 -> x1, Pallas kernels: none -> 23.9 us  [cholesky_pair(): pl.pallas_call(factor_kernel, out_shape=[out, out], scratch_shapes=[pltpu...]
    another operation x304 -> x0, other arithmetic: 20.9 us -> none  [the longest x16 19.2 us: small_pair(): later = jnp.stack(inv_rows[index + 1:], axis=0)]
    another operation x384 -> x0, local copies, waits for them, and re-layouts: 15.7 us -> none  [the longest x176 7.45 us: small_pair(): later = jnp.stack(inv_rows[index + 1:], axis=0)]
    sub x16 -> x0, other arithmetic: 10.4 us -> none  [small_pair(): values - jnp.dot(done[:, index], done, precision=lax.Precision.HIGHEST)]
where the time goes in v1:
time: 188 us; the launch traced here: 187 us
  waiting for transfers between devices  134 us (71%)
  Pallas kernels  23.9 us (13%)
  between operations  14.1 us (8%)
  matrix products  10.3 us (5%)
  other arithmetic  2.33 us (1%)
  blocking collectives  2.25 us (1%)
    psum x1, waiting for transfers between devices, local(): gram_total, summed = lax.psum((gram_local, cross_terms), 'row')  134 us
    pallas_call x1, Pallas kernels, cholesky_pair(): pl.pallas_call(factor_kernel, out_shape=[out, out], scratch_shapes=[pltpu...  23.9 us
    dot_general x3, matrix products, inner_product(): lax.dot_general(left, right, (((0,), (0,)), ((), ())), preferred_element_...  5.38 us
  transfers between devices with their start and end apart: 1, of which 1 were waited for; matrix products, arithmetic and copies ran while one was open for 0% of the time, Pallas kernels for 0%

profile of v1, /device:TPU:0, one launch (start us, length us, event | category | flops | bytes accessed | tf_op | source)
XLA Modules:
  0.0 187.3 jit_solution(171199227614835032)
XLA Ops:
  7.2 0.0 all-reduce.3.cloned.1.call-start
  7.2 0.7 convert_bitcast_fusion
  7.9 0.1 broadcast_bitcast_fusion
  8.0 2.2 %all_gather.3 = bf16[256,256]{1,0:T(8,128)(2,1)S(1)} all-gather(bf16[256,128]{1,0:T(8,128)(2,1)} %param.3), channel_id=1, replica_groups=mesh['row'=16,'col'=2] {'col'}, dimensions={1}, use_global_device_ids=true | all-gather | bytes 196608 | tf_op jit(solution)/shard_map/all_gather | solution.py:91
  10.2 0.9 fusion.3
  11.1 3.0 %convolution_bitcast_fusion = f32[256,2048]{0,1:T(8,128)} fusion(bf16[256,256]{1,0:T(8,128)(2,1)S(1)} %all_gather.3, bf16[256,2048]{1,0:T(8,128)(2,1)} %param.4, bf16[2048]{0:T(1024)(128)(2,1)S(1)} %bitcast.16), kind=kOutput, calls=%fused_computation | convolution fusion | flops 268959744 | bytes 3280896 | tf_op jit(solution)/shard_map/dot_general | solution.py:19
  14.1 0.0 all-reduce.3.cloned.1.call-update
  14.2 134.3 %all-reduce.3.cloned.1.call-done = (f32[256,256]{1,0:T(8,128)}, f32[256,2048]{0,1:T(8,128)}) async-done(((f32[256,256]{1,0:T(8,128)}, f32[256,2048]{0,1:T(8,128)}), (f32[256,256]{1,0:T(8,128)}, f32[256,2048]{0,1:T(8,128)})) %all-reduce.3.cloned.1.call-update) | async-done | bytes 2359312 | tf_op jit(solution)/shard_map/psum | solution.py:101
  148.5 1.7 select_add_fusion.gram_ref
  150.1 0.0 copy-start
  150.1 23.9 %factor.1 = (f32[256,256]{1,0:T(8,128)}, f32[256,256]{1,0:T(8,128)}) custom-call(f32[256,256]{1,0:T(8,128)} %select_add_fusion.gram_ref), custom_call_target="tpu_custom_call" | custom-call | tf_op jit(solution)/shard_map/factor/pallas_call | solution.py:82
  174.1 1.3 convolution_convert_fusion.1
  175.4 3.6 %convolution_convert_fusion = bf16[256,2048]{1,0:T(8,128)(2,1)S(1)} fusion(f32[256,256]{1,0:T(8,128)} %get-tuple-element.6, f32[256,2048]{0,1:T(8,128)} %get-tuple-element.8), kind=kOutput, calls=%fused_computation.2 | convolution fusion | flops 1611137024 | bytes 3407872 | tf_op jit(solution)/shard_map/dot_general | solution.py:103
  179.0 0.0 copy-done
  179.0 0.0 copy-start.1
  179.0 1.4 fusion
  180.4 0.0 copy-done.1
  (1 shorter events, 0.0 us)
Async XLA Ops:
  7.2 141.3 %all-reduce.3.cloned.1.call-start = ((), (), s32[]{:S(2)}) async-start(), calls=%async_computation | async-start | bytes 4718592 | tf_op jit(solution)/shard_map/psum | solution.py:101
  150.1 28.8 %copy-start = (bf16[256,2048]{1,0:T(8,128)(2,1)S(1)}, bf16[256,2048]{1,0:T(8,128)(2,1)}, u32[]{:S(2)}) copy-start(bf16[256,2048]{1,0:T(8,128)(2,1)} %param.4) | copy-start | bytes 3145732
  179.0 1.5 copy-start.1
Sparse Core Ops, SparseCore 0:
  14.4 134.0 all-reduce.2

commit v2 on v1

--- a/solution.py
+++ b/solution.py
@@ -19,6 +19,35 @@
     return lax.dot_general(
         left, right, (((0,), (0,)), ((), ())), preferred_element_type=jnp.float32
     )
+
+
+def tree_sum(terms):
+    while len(terms) > 1:
+        terms = [terms[i] + terms[i + 1] for i in range(0, len(terms), 2)]
+    return terms[0]
+
+
+class Groups:
+    def __init__(self, rows, cols):
+        self.rows, self.cols = rows, cols
+        bits = rows.bit_length() - 1
+        self.near = 1 << ((bits + 1) // 2)
+        self.far = rows // self.near
+
+    def near_index(self):
+        return lax.rem(lax.axis_index("row"), self.near)
+
+    def far_index(self):
+        return lax.div(lax.axis_index("row"), self.near)
+
+    def swap(self, value, offset):
+        return lax.ppermute(value, "row", [(i, i ^ offset) for i in range(self.rows)])
+
+    def near_swap(self, value, offset):
+        return self.swap(value, offset)
+
+    def far_swap(self, value, offset):
+        return self.swap(value, offset * self.near)
 
 
 def eliminate(groups, base, lane):
@@ -49,9 +78,16 @@
     return groups
 
 
-def factor_kernel(gram_ref, factor_ref, inverse_t_ref, work):
-    order = gram_ref.shape[0]
-    work[...] = gram_ref[...]
+def factor_kernel(own_ref, other_ref, factor_ref, inverse_t_ref, work):
+    order = own_ref.shape[0]
+    half = order // 2
+    side = lax.rem(lax.axis_index("col"), 2)
+    work[:, pl.ds(pl.multiple_of(side * half, half), half)] = own_ref[...]
+    work[:, pl.ds(pl.multiple_of((1 - side) * half, half), half)] = other_ref[...]
+    diagonal = lax.broadcasted_iota(jnp.int32, (order, order), 0) == lax.broadcasted_iota(
+        jnp.int32, (order, order), 1
+    )
+    work[...] += jnp.where(diagonal, damping_total, 0.0)
     lane = lax.broadcasted_iota(jnp.int32, (1, order), 1)
     for base in range(0, order, BLOCK):
         end = base + BLOCK
@@ -76,31 +112,114 @@
             )
 
 
-def cholesky_pair(gram):
-    order = gram.shape[0]
+def cholesky_pair(own, other):
+    order = own.shape[0]
     out = jax.ShapeDtypeStruct((order, order), jnp.float32)
     return pl.pallas_call(
         factor_kernel,
         out_shape=[out, out],
         scratch_shapes=[pltpu.VMEM((order, order), jnp.float32)],
+        cost_estimate=pl.CostEstimate(
+            flops=8 * order**3, bytes_accessed=48 * order * order, transcendentals=order
+        ),
         name="factor",
-    )(gram)
-
-
-def local(panel, trailing, tile_mask):
+    )(own, other)
+
+
+def gram_kernel(count, *refs):
+    out_ref = refs[count]
+    half = out_ref.shape[1]
+    side = lax.rem(lax.axis_index("col"), 2)
+    own = pl.ds(pl.multiple_of(side * half, half), half)
+    out_ref[...] = tree_sum(
+        [inner_product(ref[...], ref[:, own]) for ref in refs[:count]]
+    )
+
+
+def gram_part(panels):
+    order = panels[0].shape[1]
+    return pl.pallas_call(
+        functools.partial(gram_kernel, len(panels)),
+        out_shape=jax.ShapeDtypeStruct((order, order // 2), jnp.float32),
+        name="gram_part",
+    )(*panels)
+
+
+def cross_kernel(near, far, *refs):
+    panels, tiles, outs = refs[:near], refs[near : 2 * near], refs[2 * near :]
+    index = lax.div(lax.axis_index("row"), near)
+    width = outs[0].shape[1]
+    left = jnp.concatenate([ref[...] for ref in panels], axis=0)
+    for k in range(far):
+        cols = pl.ds(pl.multiple_of((index ^ k) * width, width), width)
+        right = jnp.concatenate([ref[:, cols] for ref in tiles], axis=0)
+        outs[k][...] = inner_product(left, right)
+
+
+def cross_part(groups, panels, tiles):
+    width = tiles[0].shape[1] // groups.far
+    out = jax.ShapeDtypeStruct((panels[0].shape[1], width), jnp.float32)
+    if width % 128:
+        whole = inner_product(jnp.concatenate(panels, 0), jnp.concatenate(tiles, 0))
+        return [
+            lax.dynamic_slice_in_dim(whole, (groups.far_index() ^ k) * width, width, 1)
+            for k in range(groups.far)
+        ]
+    return pl.pallas_call(
+        functools.partial(cross_kernel, groups.near, groups.far),
+        out_shape=[out] * groups.far,
+        name="cross_part",
+    )(*panels, *tiles)
+
+
+def gather_columns(groups, shard):
+    near, far = groups.near, groups.far
+    width = shard.shape[1]
+    wide = jnp.concatenate(
+        [shard] + [groups.far_swap(shard, k) for k in range(1, far)], axis=1
+    )
+    slots = [wide] + [groups.near_swap(wide, k) for k in range(1, near)]
+    out = jnp.zeros((shard.shape[0], width * near * far), shard.dtype)
+    for i, slot in enumerate(slots):
+        for k in range(far):
+            start = ((groups.near_index() ^ i) * far + (groups.far_index() ^ k)) * width
+            part = slot[:, k * width : (k + 1) * width]
+            out = lax.dynamic_update_slice_in_dim(out, part, start, 1)
+    return out
+
+
+def local(groups, panel, trailing, tile_mask):
+    near, far = groups.near, groups.far
     gathered = lax.all_gather(panel, "col", axis=1, tiled=True)
+    panels = [gathered] + [groups.near_swap(gathered, k) for k in range(1, near)]
+
     local_rows = trailing.shape[0]
     local_cols = trailing.shape[1]
     tiles = trailing.reshape(local_rows // TILE, TILE, local_cols // TILE, TILE)
     masked = (tiles * tile_mask.astype(jnp.bfloat16)[:, None, :, None]).reshape(
         local_rows, local_cols
     )
-    identity = jnp.eye(gathered.shape[1], dtype=jnp.float32)
-    gram_local = inner_product(gathered, gathered)
-    cross_terms = inner_product(gathered, masked)
-    gram_total, summed = lax.psum((gram_local, cross_terms), "row")
-    upper_factor, inverse_t = cholesky_pair(gram_total + damping_total * identity)
-    coupling = jnp.dot(inverse_t, summed, precision=HIGHEST).astype(jnp.bfloat16)
+    chunk = local_cols // near
+    chunks = [
+        lax.dynamic_slice_in_dim(masked, (groups.near_index() ^ k) * chunk, chunk, 1)
+        for k in range(near)
+    ]
+    chunks = chunks[:1] + [groups.near_swap(chunks[k], k) for k in range(1, near)]
+
+    gram_terms = gram_part(panels)
+    gram_own = tree_sum(
+        [gram_terms] + [groups.far_swap(gram_terms, k) for k in range(1, far)]
+    )
+    gram_other = lax.ppermute(gram_own, "col", [(i, i ^ 1) for i in range(groups.cols)])
+
+    cross_terms = cross_part(groups, panels, chunks)
+    summed = tree_sum(
+        [cross_terms[0]] + [groups.far_swap(cross_terms[k], k) for k in range(1, far)]
+    )
+
+    upper_factor, inverse_t = cholesky_pair(gram_own, gram_other)
+    shard = jnp.dot(inverse_t, summed, precision=HIGHEST).astype(jnp.bfloat16)
+    coupling = gather_columns(groups, shard)
     basis_t = jnp.dot(
         inverse_t, gathered.astype(jnp.float32).T, precision=HIGHEST
     ).astype(jnp.bfloat16)
@@ -111,8 +230,9 @@
 
 def solution(mesh):
     placed = (P("row", "col"), P("row", "col"), P("row", "col"))
+    groups = Groups(mesh.shape["row"], mesh.shape["col"])
     return jax.shard_map(
-        local,
+        functools.partial(local, groups),
         mesh=mesh,
         in_specs=placed,
         out_specs=(P(), P(None, "col"), P("row", "col")),

time: 188 us -> 94.1 us (0.50)
  waiting for transfers between devices: 134 us -> 24.4 us
  starting transfers between devices: 0.04 us -> 24.7 us
  between operations: 14.1 us -> 1.02 us
  local copies, waits for them, and re-layouts: 0.09 us -> 7.39 us
  matrix products: 10.3 us -> 3.22 us
  Pallas kernels: 23.9 us -> 28.8 us
    psum x1 -> x0, waiting for transfers between devices: 134 us -> none  [local(): gram_total, summed = lax.psum((gram_local, cross_terms), 'row')]
    ppermute x0 -> x19, starting transfers between devices: none -> 24.7 us  [the longest x18 24.7 us: swap(): lax.ppermute(value, 'row', [(i, i ^ offset) for i in range(self.rows)])]
    ppermute x0 -> x19, waiting for transfers between devices: none -> 24.4 us  [the longest x18 24.4 us: swap(): lax.ppermute(value, 'row', [(i, i ^ offset) for i in range(self.rows)])]
    pallas_call x0 -> x2, Pallas kernels: none -> 4.91 us  [the longest x1 2.81 us: cross_part(): pl.pallas_call(functools.partial(cross_kernel, groups.near, groups.far),...]
    dot_general x3 -> x1, matrix products: 5.38 us -> 1.43 us  [inner_product(): lax.dot_general(left, right, (((0,), (0,)), ((), ())), preferred_element_...]
    slice x0 -> x15, local copies, waits for them, and re-layouts: none -> 2.9 us  [gather_columns(): part = slot[:, k * width:(k + 1) * width]]
    unnamed x6 -> x28, local copies, waits for them, and re-layouts: 0.09 us -> 2.74 us
    dot_general x1, matrix products: 3.62 us -> 1.45 us  [local(): shard = jnp.dot(inverse_t, summed, precision=HIGHEST).astype(jnp.bfloat16)]
  transfers between devices with their start and end apart: 1 -> 19, of which waited for: 1 -> 10; matrix products, arithmetic and copies ran while one was open for 0% -> 7% of each run, Pallas kernels for 0% -> 28%
where the time goes in v2:
time: 94.1 us; the launch traced here: 93.8 us
  Pallas kernels  28.8 us (31%)
  starting transfers between devices  24.7 us (26%)
  waiting for transfers between devices  24.4 us (26%)
  local copies, waits for them, and re-layouts  7.39 us (8%)
  matrix products  3.22 us (3%)
  blocking collectives  2.26 us (2%)
  other arithmetic  2 us (2%)
  between operations  1.02 us (1%)
    ppermute x18, starting transfers between devices, swap(): lax.ppermute(value, 'row', [(i, i ^ offset) for i in range(self.rows)])  24.7 us
    ppermute x18, waiting for transfers between devices, swap(): lax.ppermute(value, 'row', [(i, i ^ offset) for i in range(self.rows)])  24.4 us
    pallas_call x1, Pallas kernels, cholesky_pair(): pl.pallas_call(factor_kernel, out_shape=[out, out], scratch_shapes=[pltpu...  23.9 us
    slice x15, local copies, waits for them, and re-layouts, gather_columns(): part = slot[:, k * width:(k + 1) * width]  2.9 us
    pallas_call x1, Pallas kernels, cross_part(): pl.pallas_call(functools.partial(cross_kernel, groups.near, groups.far),...  2.81 us
    unnamed x28, local copies, waits for them, and re-layouts  2.74 us
    all_gather x1, blocking collectives, local(): gathered = lax.all_gather(panel, 'col', axis=1, tiled=True)  2.26 us
    pallas_call x1, Pallas kernels, gram_part(): pl.pallas_call(functools.partial(gram_kernel, len(panels)), out_shape=jax...  2.1 us
  transfers between devices with their start and end apart: 19, of which 10 were waited for; matrix products, arithmetic and copies ran while one was open for 7% of the time, Pallas kernels for 28%

profile of v2, /device:TPU:0, one launch (start us, length us, event | category | flops | bytes accessed | tf_op | source)
XLA Modules:
  0.0 93.8 jit_solution(10047247806904284853)
XLA Ops:
  0.6 2.3 %all_gather.3.refs_0_ = bf16[256,256]{1,0:T(8,128)(2,1)S(1)} all-gather(bf16[256,128]{1,0:T(8,128)(2,1)} %param.3), channel_id=1, replica_groups=mesh['row'=16,'col'=2] {'col'}, dimensions={1}, use_global_device_ids=true | all-gather | bytes 196608 | tf_op jit(solution)/shard_map/all_gather | solution.py:193
  2.9 2.8 %collective-permute-start = (bf16[256,256]{1,0:T(8,128)(2,1)S(1)}, bf16[256,256]{1,0:T(8,128)(2,1)S(1)}, u32[]{:S(2)}, u32[]{:S(2)}) collective-permute-start(bf16[256,256]{1,0:T(8,128)(2,1)S(1)} %all_gather.3.refs_0_), channel_id=1, source_target_pairs={{0,2},{2,0},{4,6},{6,4},{8,10},{10,8},{12,14},{14,12},{16,18},{18,... | collective-permute-start | bytes 393224 | tf_op jit(solution)/shard_map/ppermute | solution.py:44
  5.7 1.5 %collective-permute-start.1 = (bf16[256,256]{1,0:T(8,128)(2,1)S(1)}, bf16[256,256]{1,0:T(8,128)(2,1)S(1)}, u32[]{:S(2)}, u32[]{:S(2)}) collective-permute-start(bf16[256,256]{1,0:T(8,128)(2,1)S(1)} %all_gather.3.refs_0_), channel_id=1, source_target_pairs={{0,4},{2,6},{4,0},{6,2},{8,12},{10,14},{12,8},{14,10},{16,20},{18,... | collective-permute-start | bytes 393224 | tf_op jit(solution)/shard_map/ppermute | solution.py:44
  7.3 0.0 collective-permute-start.2
  7.3 0.7 convert_bitcast_fusion
  7.9 0.1 broadcast_bitcast_fusion
  8.0 1.3 %broadcast_multiply_fusion = bf16[256,2048]{1,0:T(8,128)(2,1)S(1)} fusion(bf16[256,2048]{1,0:T(8,128)(2,1)} %param.4, bf16[2048]{0:T(1024)(128)(2,1)S(1)} %bitcast.10), kind=kLoop, calls=%fused_computation.4 | loop fusion | flops 524288 | bytes 2101248 | tf_op jit(solution)/shard_map/mul | solution.py:199
  9.4 0.3 collective-permute-done.refs_1_
  9.6 4.2 %collective-permute-done.1.refs_2_ = bf16[256,256]{1,0:T(8,128)(2,1)S(1)} collective-permute-done((bf16[256,256]{1,0:T(8,128)(2,1)S(1)}, bf16[256,256]{1,0:T(8,128)(2,1)S(1)}, u32[]{:S(2)}, u32[]{:S(2)}) %collective-permute-start.1) | collective-permute-done | bytes 131104 | tf_op jit(solution)/shard_map/ppermute | solution.py:44
  13.8 0.6 copy-done.5
  14.5 0.6 copy-done.6
  15.1 2.1 %gram_part.1 = f32[256,128]{1,0:T(8,128)} custom-call(bf16[256,256]{1,0:T(8,128)(2,1)} %copy-done.1, bf16[256,256]{1,0:T(8,128)(2,1)} %copy-done.4, bf16[256,256]{1,0:T(8,128)(2,1)} %copy-done.5, bf16[256,256]{1,0:T(8,128)(2,1)} %copy-done.6), custom_call_target="tpu_custom_call" | custom-call | tf_op jit(solution)/shard_map/gram_part/pallas_call | solution.py:141
  17.2 1.6 %collective-permute-start.3 = (f32[256,128]{1,0:T(8,128)}, f32[256,128]{1,0:T(8,128)S(1)}, u32[]{:S(2)}, u32[]{:S(2)}) collective-permute-start(f32[256,128]{1,0:T(8,128)} %gram_part.1), channel_id=1, source_target_pairs={{0,8},{2,10},{4,12},{6,14},{8,0},{10,2},{12,4},{14,6},{16,24},{18,... | collective-permute-start | bytes 393224 | tf_op jit(solution)/shard_map/ppermute | solution.py:44
  18.8 2.6 %collective-permute-start.4 = (f32[256,128]{1,0:T(8,128)}, f32[256,128]{1,0:T(8,128)S(1)}, u32[]{:S(2)}, u32[]{:S(2)}) collective-permute-start(f32[256,128]{1,0:T(8,128)} %gram_part.1), channel_id=1, source_target_pairs={{0,16},{2,18},{4,20},{6,22},{8,24},{10,26},{12,28},{14,30},{16,0},... | collective-permute-start | bytes 393224 | tf_op jit(solution)/shard_map/ppermute | solution.py:44
  21.4 0.2 collective-permute-start.5
  21.6 0.8 constant_dynamic-slice_fusion
  22.4 0.6 collective-permute-start.7
  23.0 1.5 %collective-permute-start.8 = (bf16[256,512]{1,0:T(8,128)(2,1)S(1)}, bf16[256,512]{1,0:T(8,128)(2,1)S(1)}, u32[]{:S(2)}, u32[]{:S(2)}) collective-permute-start(bf16[256,512]{1,0:T(8,128)(2,1)S(1)} %get-tuple-element.16), channel_id=1, source_target_pairs={{0,4},{2,6},{4,0},{6,2},{8,12},{10,14},{12,8},{14,10},{16,20},{18,... | collective-permute-start | bytes 786440 | tf_op jit(solution)/shard_map/ppermute | solution.py:44
  24.5 0.0 collective-permute-done.3
  24.5 1.4 %collective-permute-start.9 = (bf16[256,512]{1,0:T(8,128)(2,1)S(1)}, bf16[256,512]{1,0:T(8,128)(2,1)S(1)}, u32[]{:S(2)}, u32[]{:S(2)}) collective-permute-start(bf16[256,512]{1,0:T(8,128)(2,1)S(1)} %get-tuple-element.15), channel_id=1, source_target_pairs={{0,6},{2,4},{4,2},{6,0},{8,14},{10,12},{12,10},{14,8},{16,22},{18,... | collective-permute-start | bytes 786440 | tf_op jit(solution)/shard_map/ppermute | solution.py:44
  25.9 4.4 %collective-permute-done.4 = f32[256,128]{1,0:T(8,128)S(1)} collective-permute-done((f32[256,128]{1,0:T(8,128)}, f32[256,128]{1,0:T(8,128)S(1)}, u32[]{:S(2)}, u32[]{:S(2)}) %collective-permute-start.4) | collective-permute-done | bytes 131104 | tf_op jit(solution)/shard_map/ppermute | solution.py:44
  30.4 0.1 collective-permute-start.6
  30.5 0.5 collective-permute-done.7.refs_5_
  30.9 2.6 %collective-permute-done.8.refs_6_ = bf16[256,512]{1,0:T(8,128)(2,1)S(1)} collective-permute-done((bf16[256,512]{1,0:T(8,128)(2,1)S(1)}, bf16[256,512]{1,0:T(8,128)(2,1)S(1)}, u32[]{:S(2)}, u32[]{:S(2)}) %collective-permute-start.8) | collective-permute-done | bytes 262176 | tf_op jit(solution)/shard_map/ppermute | solution.py:44
  33.5 1.9 %collective-permute-done.9.refs_7_ = bf16[256,512]{1,0:T(8,128)(2,1)S(1)} collective-permute-done((bf16[256,512]{1,0:T(8,128)(2,1)S(1)}, bf16[256,512]{1,0:T(8,128)(2,1)S(1)}, u32[]{:S(2)}, u32[]{:S(2)}) %collective-permute-start.9) | collective-permute-done | bytes 262176 | tf_op jit(solution)/shard_map/ppermute | solution.py:44
  35.4 0.7 copy-done.10
  36.1 2.8 %cross_part.1 = (f32[256,128]{1,0:T(8,128)}, f32[256,128]{1,0:T(8,128)}, f32[256,128]{1,0:T(8,128)}, f32[256,128]{1,0:T(8,128)}) custom-call(bf16[256,256]{1,0:T(8,128)(2,1)} %copy-done.1, bf16[256,256]{1,0:T(8,128)(2,1)} %copy-done.4, bf16[256,256]{1,0:T(8,128)(2,1)} %copy-done.5, bf16[256,256]{1,0:T(8,128)(2,1)} %copy-done.6, ...), custom_call_target="tpu_custom_call" | custom-call | tf_op jit(solution)/shard_map/cross_part/pallas_call | solution.py:168
  38.9 0.6 collective-permute-start.10
  39.6 3.5 %collective-permute-start.11 = (f32[256,128]{1,0:T(8,128)}, f32[256,128]{1,0:T(8,128)S(1)}, u32[]{:S(2)}, u32[]{:S(2)}) collective-permute-start(f32[256,128]{1,0:T(8,128)} %get-tuple-element.13), channel_id=1, source_target_pairs={{0,16},{2,18},{4,20},{6,22},{8,24},{10,26},{12,28},{14,30},{16,0},... | collective-permute-start | bytes 393224 | tf_op jit(solution)/shard_map/ppermute | solution.py:44
  43.0 0.3 collective-permute-start.12
  43.3 0.7 copy-done.12
  44.0 23.9 %factor.1 = (f32[256,256]{1,0:T(8,128)}, f32[256,256]{1,0:T(8,128)}) custom-call(f32[256,128]{1,0:T(8,128)} %copy-done.11, f32[256,128]{1,0:T(8,128)} %copy-done.12), custom_call_target="tpu_custom_call" | custom-call | flops 134217728 | bytes 3145728 | tf_op jit(solution)/shard_map/factor/pallas_call | solution.py:118
  67.9 1.4 %convolution_convert_fusion.1 = bf16[256,128]{0,1:T(8,128)(2,1)S(1)} fusion(f32[256,256]{1,0:T(8,128)} %get-tuple-element.10, f32[256,128]{1,0:T(8,128)S(1)} %collective-permute-done.11, f32[256,128]{1,0:T(8,128)S(1)} %collective-permute-done.12, f32[256,128]{1,0:T(8,128)} %get-tuple-element.11, f32[256,128]{1,0:T(8,128)S(1)} %collective-permute-done.10), kind=kOutput, calls=%fused_computation.3 | convolution fusion | flops 100794368 | bytes 851968 | tf_op jit(solution)/shard_map/dot_general | solution.py:221
  69.3 0.4 collective-permute-start.13
  69.7 3.8 %collective-permute-start.14 = (bf16[256,128]{0,1:T(8,128)(2,1)S(1)}, bf16[256,128]{0,1:T(8,128)(2,1)S(1)}, u32[]{:S(2)}, u32[]{:S(2)}) collective-permute-start(bf16[256,128]{0,1:T(8,128)(2,1)S(1)} %convolution_convert_fusion.1), channel_id=1, source_target_pairs={{0,16},{2,18},{4,20},{6,22},{8,24},{10,26},{12,28},{14,30},{16,0},... | collective-permute-start | bytes 196616 | tf_op jit(solution)/shard_map/ppermute | solution.py:44
  73.5 0.3 collective-permute-start.15
  73.8 0.1 copy.6
  73.9 0.3 convolution_convert_fusion
  74.3 0.1 broadcast_in_dim.4
  74.4 2.0 %collective-permute-done.14 = bf16[256,128]{0,1:T(8,128)(2,1)S(1)} collective-permute-done((bf16[256,128]{0,1:T(8,128)(2,1)S(1)}, bf16[256,128]{0,1:T(8,128)(2,1)S(1)}, u32[]{:S(2)}, u32[]{:S(2)}) %collective-permute-start.14) | collective-permute-done | bytes 65568 | tf_op jit(solution)/shard_map/ppermute | solution.py:44
  76.4 3.1 %collective-permute-done.15 = bf16[256,128]{0,1:T(8,128)(2,1)S(1)} collective-permute-done((bf16[256,128]{0,1:T(8,128)(2,1)S(1)}, bf16[256,128]{0,1:T(8,128)(2,1)S(1)}, u32[]{:S(2)}, u32[]{:S(2)}) %collective-permute-start.15) | collective-permute-done | bytes 65568 | tf_op jit(solution)/shard_map/ppermute | solution.py:44
  79.6 0.7 collective-permute-start.16
  80.3 1.7 %collective-permute-start.17 = (bf16[256,512]{0,1:T(8,128)(2,1)S(1)}, bf16[256,512]{0,1:T(8,128)(2,1)S(1)}, u32[]{:S(2)}, u32[]{:S(2)}) collective-permute-start(bf16[256,512]{0,1:T(8,128)(2,1)S(1)} %pad_maximum_fusion), channel_id=1, source_target_pairs={{0,4},{2,6},{4,0},{6,2},{8,12},{10,14},{12,8},{14,10},{16,20},{18,... | collective-permute-start | bytes 786440 | tf_op jit(solution)/shard_map/ppermute | solution.py:44
  82.0 1.1 %collective-permute-start.18 = (bf16[256,512]{0,1:T(8,128)(2,1)S(1)}, bf16[256,512]{0,1:T(8,128)(2,1)S(1)}, u32[]{:S(2)}, u32[]{:S(2)}) collective-permute-start(bf16[256,512]{0,1:T(8,128)(2,1)S(1)} %pad_maximum_fusion), channel_id=1, source_target_pairs={{0,6},{2,4},{4,2},{6,0},{8,14},{10,12},{12,10},{14,8},{16,22},{18,... | collective-permute-start | bytes 786440 | tf_op jit(solution)/shard_map/ppermute | solution.py:44
  83.1 0.1 copy.7
  83.3 0.1 copy.8
  83.4 0.1 copy.9
  83.6 2.4 %collective-permute-done.16 = bf16[256,512]{0,1:T(8,128)(2,1)S(1)} collective-permute-done((bf16[256,512]{0,1:T(8,128)(2,1)S(1)}, bf16[256,512]{0,1:T(8,128)(2,1)S(1)}, u32[]{:S(2)}, u32[]{:S(2)}) %collective-permute-start.16) | collective-permute-done | bytes 262176 | tf_op jit(solution)/shard_map/ppermute | solution.py:44
  86.0 0.1 copy.10
  86.2 0.1 copy.11
  86.3 0.1 copy.12
  86.4 0.1 copy.13
  86.5 3.0 %collective-permute-done.17 = bf16[256,512]{0,1:T(8,128)(2,1)S(1)} collective-permute-done((bf16[256,512]{0,1:T(8,128)(2,1)S(1)}, bf16[256,512]{0,1:T(8,128)(2,1)S(1)}, u32[]{:S(2)}, u32[]{:S(2)}) %collective-permute-start.17) | collective-permute-done | bytes 262176 | tf_op jit(solution)/shard_map/ppermute | solution.py:44
  89.5 0.6 fusion.5
  90.1 0.9 %copy.14 = bf16[256,128]{1,0:T(8,128)(2,1)S(1)} copy(bf16[256,128]{0,1:T(8,128)(2,1)} %get-tuple-element.26) | data formatting | bytes 131072 | tf_op jit(solution)/shard_map/slice | solution.py:186
  91.1 0.1 copy.15
  91.2 0.1 copy.16
  91.3 0.1 copy.17
  91.5 0.1 copy.18
  91.6 0.1 copy.19
  91.7 0.1 copy.20
  91.9 0.1 copy.21
  92.3 0.0 copy-start
  92.4 1.4 %fusion = bf16[256,2048]{1,0:T(8,128)(2,1)} fusion(bf16[256,256]{1,0:T(8,128)(2,1)S(1)} %convolution_convert_fusion, bf16[256,2048]{1,0:T(8,128)(2,1)S(1)} %constant_dynamic-update-slice_fusion, bf16[256,2048]{1,0:T(8,128)(2,1)S(1)} %broadcast_multiply_fusion), kind=kOutput, calls=%fused_computation.1 | convolution fusion | flops 270008320 | bytes 3276800 | tf_op jit(solution)/shard_map/dot_general | solution.py:19
  (50 shorter events, 0.5 us)
Async XLA Ops:
  2.9 6.4 %copy-start.1 = (bf16[256,256]{1,0:T(8,128)(2,1)}, bf16[256,256]{1,0:T(8,128)(2,1)S(1)}, u32[]{:S(2)}) copy-start(bf16[256,256]{1,0:T(8,128)(2,1)S(1)} %all_gather.3.refs_0_) | copy-start | bytes 393220
  2.9 6.7 %collective-permute-start = (bf16[256,256]{1,0:T(8,128)(2,1)S(1)}, bf16[256,256]{1,0:T(8,128)(2,1)S(1)}, u32[]{:S(2)}, u32[]{:S(2)}) collective-permute-start(bf16[256,256]{1,0:T(8,128)(2,1)S(1)} %all_gather.3.refs_0_), channel_id=1, source_target_pairs={{0,2},{2,0},{4,6},{6,4},{8,10},{10,8},{12,14},{14,12},{16,18},{18,... | collective-permute-start | bytes 393224 | tf_op jit(solution)/shard_map/ppermute | solution.py:44
  5.7 8.1 %collective-permute-start.1 = (bf16[256,256]{1,0:T(8,128)(2,1)S(1)}, bf16[256,256]{1,0:T(8,128)(2,1)S(1)}, u32[]{:S(2)}, u32[]{:S(2)}) collective-permute-start(bf16[256,256]{1,0:T(8,128)(2,1)S(1)} %all_gather.3.refs_0_), channel_id=1, source_target_pairs={{0,4},{2,6},{4,0},{6,2},{8,12},{10,14},{12,8},{14,10},{16,20},{18,... | collective-permute-start | bytes 393224 | tf_op jit(solution)/shard_map/ppermute | solution.py:44
  7.3 6.6 %collective-permute-start.2 = (bf16[256,256]{1,0:T(8,128)(2,1)S(1)}, bf16[256,256]{1,0:T(8,128)(2,1)S(1)}, u32[]{:S(2)}, u32[]{:S(2)}) collective-permute-start(bf16[256,256]{1,0:T(8,128)(2,1)S(1)} %all_gather.3.refs_0_), channel_id=1, source_target_pairs={{0,6},{2,4},{4,2},{6,0},{8,14},{10,12},{12,10},{14,8},{16,22},{18,... | collective-permute-start | bytes 393224 | tf_op jit(solution)/shard_map/ppermute | solution.py:44
  9.6 4.2 %copy-start.4 = (bf16[256,256]{1,0:T(8,128)(2,1)}, bf16[256,256]{1,0:T(8,128)(2,1)S(1)}, u32[]{:S(2)}) copy-start(bf16[256,256]{1,0:T(8,128)(2,1)S(1)} %collective-permute-done.refs_1_) | copy-start | bytes 393220
  13.8 0.6 copy-start.5
  14.5 0.7 copy-start.6
  17.2 13.1 %copy-start.7 = (f32[256,128]{1,0:T(8,128)S(1)}, f32[256,128]{1,0:T(8,128)}, u32[]{:S(2)}) copy-start(f32[256,128]{1,0:T(8,128)} %gram_part.1) | copy-start | bytes 393220
  17.2 7.3 %collective-permute-start.3 = (f32[256,128]{1,0:T(8,128)}, f32[256,128]{1,0:T(8,128)S(1)}, u32[]{:S(2)}, u32[]{:S(2)}) collective-permute-start(f32[256,128]{1,0:T(8,128)} %gram_part.1), channel_id=1, source_target_pairs={{0,8},{2,10},{4,12},{6,14},{8,0},{10,2},{12,4},{14,6},{16,24},{18,... | collective-permute-start | bytes 393224 | tf_op jit(solution)/shard_map/ppermute | solution.py:44
  18.8 11.5 %collective-permute-start.4 = (f32[256,128]{1,0:T(8,128)}, f32[256,128]{1,0:T(8,128)S(1)}, u32[]{:S(2)}, u32[]{:S(2)}) collective-permute-start(f32[256,128]{1,0:T(8,128)} %gram_part.1), channel_id=1, source_target_pairs={{0,16},{2,18},{4,20},{6,22},{8,24},{10,26},{12,28},{14,30},{16,0},... | collective-permute-start | bytes 393224 | tf_op jit(solution)/shard_map/ppermute | solution.py:44
  21.4 8.9 %collective-permute-start.5 = (f32[256,128]{1,0:T(8,128)}, f32[256,128]{1,0:T(8,128)S(1)}, u32[]{:S(2)}, u32[]{:S(2)}) collective-permute-start(f32[256,128]{1,0:T(8,128)} %gram_part.1), channel_id=1, source_target_pairs={{0,24},{2,26},{4,28},{6,30},{8,16},{10,18},{12,20},{14,22},{16,8},... | collective-permute-start | bytes 393224 | tf_op jit(solution)/shard_map/ppermute | solution.py:44
  22.4 8.5 %collective-permute-start.7 = (bf16[256,512]{1,0:T(8,128)(2,1)S(1)}, bf16[256,512]{1,0:T(8,128)(2,1)S(1)}, u32[]{:S(2)}, u32[]{:S(2)}) collective-permute-start(bf16[256,512]{1,0:T(8,128)(2,1)S(1)} %get-tuple-element.17), channel_id=1, source_target_pairs={{0,2},{2,0},{4,6},{6,4},{8,10},{10,8},{12,14},{14,12},{16,18},{18,... | collective-permute-start | bytes 786440 | tf_op jit(solution)/shard_map/ppermute | solution.py:44
  23.0 10.5 %collective-permute-start.8 = (bf16[256,512]{1,0:T(8,128)(2,1)S(1)}, bf16[256,512]{1,0:T(8,128)(2,1)S(1)}, u32[]{:S(2)}, u32[]{:S(2)}) collective-permute-start(bf16[256,512]{1,0:T(8,128)(2,1)S(1)} %get-tuple-element.16), channel_id=1, source_target_pairs={{0,4},{2,6},{4,0},{6,2},{8,12},{10,14},{12,8},{14,10},{16,20},{18,... | collective-permute-start | bytes 786440 | tf_op jit(solution)/shard_map/ppermute | solution.py:44
  24.5 11.0 %collective-permute-start.9 = (bf16[256,512]{1,0:T(8,128)(2,1)S(1)}, bf16[256,512]{1,0:T(8,128)(2,1)S(1)}, u32[]{:S(2)}, u32[]{:S(2)}) collective-permute-start(bf16[256,512]{1,0:T(8,128)(2,1)S(1)} %get-tuple-element.15), channel_id=1, source_target_pairs={{0,6},{2,4},{4,2},{6,0},{8,14},{10,12},{12,10},{14,8},{16,22},{18,... | collective-permute-start | bytes 786440 | tf_op jit(solution)/shard_map/ppermute | solution.py:44
  30.4 13.0 %copy-start.11 = (f32[256,128]{1,0:T(8,128)}, f32[256,128]{1,0:T(8,128)S(1)}, u32[]{:S(2)}) copy-start(f32[256,128]{1,0:T(8,128)S(1)} %add_add_fusion.own_ref) | copy-start | bytes 393220
  30.4 13.0 %collective-permute-start.6 = (f32[256,128]{1,0:T(8,128)S(1)}, f32[256,128]{1,0:T(8,128)S(1)}, u32[]{:S(2)}, u32[]{:S(2)}) collective-permute-start(f32[256,128]{1,0:T(8,128)S(1)} %add_add_fusion.own_ref), channel_id=1, source_target_pairs={{0,1},{1,0},{2,3},{3,2},{4,5},{5,4},{6,7},{7,6},{8,9},{9,8},{10,11... | collective-permute-start | bytes 393224 | tf_op jit(solution)/shard_map/ppermute | solution.py:213
  30.9 4.5 %copy-start.8 = (bf16[256,512]{1,0:T(8,128)(2,1)}, bf16[256,512]{1,0:T(8,128)(2,1)S(1)}, u32[]{:S(2)}) copy-start(bf16[256,512]{1,0:T(8,128)(2,1)S(1)} %collective-permute-done.7.refs_5_) | copy-start | bytes 786436
  33.5 1.9 %copy-start.9 = (bf16[256,512]{1,0:T(8,128)(2,1)}, bf16[256,512]{1,0:T(8,128)(2,1)S(1)}, u32[]{:S(2)}) copy-start(bf16[256,512]{1,0:T(8,128)(2,1)S(1)} %collective-permute-done.8.refs_6_) | copy-start | bytes 786436
  35.4 0.7 copy-start.10
  38.9 35.0 %copy-start.2 = (bf16[256,256]{1,0:T(8,128)(2,1)S(1)}, bf16[256,256]{1,0:T(8,128)(2,1)}, u32[]{:S(2)}) copy-start(bf16[256,256]{1,0:T(8,128)(2,1)} %copy-done.1) | copy-start | bytes 393220
  38.9 28.9 %collective-permute-start.10 = (f32[256,128]{1,0:T(8,128)}, f32[256,128]{1,0:T(8,128)S(1)}, u32[]{:S(2)}, u32[]{:S(2)}) collective-permute-start(f32[256,128]{1,0:T(8,128)} %get-tuple-element.12), channel_id=1, source_target_pairs={{0,8},{2,10},{4,12},{6,14},{8,0},{10,2},{12,4},{14,6},{16,24},{18,... | collective-permute-start | bytes 393224 | tf_op jit(solution)/shard_map/ppermute | solution.py:44
  39.6 28.3 %collective-permute-start.11 = (f32[256,128]{1,0:T(8,128)}, f32[256,128]{1,0:T(8,128)S(1)}, u32[]{:S(2)}, u32[]{:S(2)}) collective-permute-start(f32[256,128]{1,0:T(8,128)} %get-tuple-element.13), channel_id=1, source_target_pairs={{0,16},{2,18},{4,20},{6,22},{8,24},{10,26},{12,28},{14,30},{16,0},... | collective-permute-start | bytes 393224 | tf_op jit(solution)/shard_map/ppermute | solution.py:44
  43.0 24.8 %collective-permute-start.12 = (f32[256,128]{1,0:T(8,128)}, f32[256,128]{1,0:T(8,128)S(1)}, u32[]{:S(2)}, u32[]{:S(2)}) collective-permute-start(f32[256,128]{1,0:T(8,128)} %get-tuple-element.14), channel_id=1, source_target_pairs={{0,24},{2,26},{4,28},{6,30},{8,16},{10,18},{12,20},{14,22},{16,8},... | collective-permute-start | bytes 393224 | tf_op jit(solution)/shard_map/ppermute | solution.py:44
  43.3 0.7 copy-start.12
  67.8 6.1 %copy-start.3 = (f32[256,256]{1,0:T(8,128)S(1)}, f32[256,256]{1,0:T(8,128)}, u32[]{:S(2)}) copy-start(f32[256,256]{1,0:T(8,128)} %get-tuple-element.10) | copy-start | bytes 786436
  69.3 5.1 %collective-permute-start.13 = (bf16[256,128]{0,1:T(8,128)(2,1)S(1)}, bf16[256,128]{0,1:T(8,128)(2,1)S(1)}, u32[]{:S(2)}, u32[]{:S(2)}) collective-permute-start(bf16[256,128]{0,1:T(8,128)(2,1)S(1)} %convolution_convert_fusion.1), channel_id=1, source_target_pairs={{0,8},{2,10},{4,12},{6,14},{8,0},{10,2},{12,4},{14,6},{16,24},{18,... | collective-permute-start | bytes 196616 | tf_op jit(solution)/shard_map/ppermute | solution.py:44
  69.7 6.8 %collective-permute-start.14 = (bf16[256,128]{0,1:T(8,128)(2,1)S(1)}, bf16[256,128]{0,1:T(8,128)(2,1)S(1)}, u32[]{:S(2)}, u32[]{:S(2)}) collective-permute-start(bf16[256,128]{0,1:T(8,128)(2,1)S(1)} %convolution_convert_fusion.1), channel_id=1, source_target_pairs={{0,16},{2,18},{4,20},{6,22},{8,24},{10,26},{12,28},{14,30},{16,0},... | collective-permute-start | bytes 196616 | tf_op jit(solution)/shard_map/ppermute | solution.py:44
  73.5 6.1 %collective-permute-start.15 = (bf16[256,128]{0,1:T(8,128)(2,1)S(1)}, bf16[256,128]{0,1:T(8,128)(2,1)S(1)}, u32[]{:S(2)}, u32[]{:S(2)}) collective-permute-start(bf16[256,128]{0,1:T(8,128)(2,1)S(1)} %convolution_convert_fusion.1), channel_id=1, source_target_pairs={{0,24},{2,26},{4,28},{6,30},{8,16},{10,18},{12,20},{14,22},{16,8},... | collective-permute-start | bytes 196616 | tf_op jit(solution)/shard_map/ppermute | solution.py:44
  79.6 6.4 %collective-permute-start.16 = (bf16[256,512]{0,1:T(8,128)(2,1)S(1)}, bf16[256,512]{0,1:T(8,128)(2,1)S(1)}, u32[]{:S(2)}, u32[]{:S(2)}) collective-permute-start(bf16[256,512]{0,1:T(8,128)(2,1)S(1)} %pad_maximum_fusion), channel_id=1, source_target_pairs={{0,2},{2,0},{4,6},{6,4},{8,10},{10,8},{12,14},{14,12},{16,18},{18,... | collective-permute-start | bytes 786440 | tf_op jit(solution)/shard_map/ppermute | solution.py:44
  80.3 9.2 %collective-permute-start.17 = (bf16[256,512]{0,1:T(8,128)(2,1)S(1)}, bf16[256,512]{0,1:T(8,128)(2,1)S(1)}, u32[]{:S(2)}, u32[]{:S(2)}) collective-permute-start(bf16[256,512]{0,1:T(8,128)(2,1)S(1)} %pad_maximum_fusion), channel_id=1, source_target_pairs={{0,4},{2,6},{4,0},{6,2},{8,12},{10,14},{12,8},{14,10},{16,20},{18,... | collective-permute-start | bytes 786440 | tf_op jit(solution)/shard_map/ppermute | solution.py:44
  82.0 9.4 %collective-permute-start.18 = (bf16[256,512]{0,1:T(8,128)(2,1)S(1)}, bf16[256,512]{0,1:T(8,128)(2,1)S(1)}, u32[]{:S(2)}, u32[]{:S(2)}) collective-permute-start(bf16[256,512]{0,1:T(8,128)(2,1)S(1)} %pad_maximum_fusion), channel_id=1, source_target_pairs={{0,6},{2,4},{4,2},{6,0},{8,14},{10,12},{12,10},{14,8},{16,22},{18,... | collective-permute-start | bytes 786440 | tf_op jit(solution)/shard_map/ppermute | solution.py:44
  92.3 1.4 %copy-start = (bf16[256,2048]{1,0:T(8,128)(2,1)}, bf16[256,2048]{1,0:T(8,128)(2,1)S(1)}, u32[]{:S(2)}) copy-start(bf16[256,2048]{1,0:T(8,128)(2,1)S(1)} %constant_dynamic-update-slice_fusion) | copy-start | bytes 3145732

commit v3 on v2

v3 whole, which is shorter than its diff:
```python
import functools

import jax
import jax.numpy as jnp
from jax import lax
from jax.experimental import pallas as pl
from jax.experimental.pallas import tpu as pltpu
from jax.sharding import PartitionSpec as P

TILE = 256
BLOCK = 64
STEP = 8
HIGHEST = lax.Precision.HIGHEST


damping_total = 0.5


def inner_product(left, right):
    return lax.dot_general(
        left, right, (((0,), (0,)), ((), ())), preferred_element_type=jnp.float32
    )


def tree_sum(terms):
    while len(terms) > 1:
        terms = [terms[i] + terms[i + 1] for i in range(0, len(terms), 2)]
    return terms[0]


class Groups:
    def __init__(self, rows, cols):
        self.rows, self.cols = rows, cols
        bits = rows.bit_length() - 1
        self.near = 1 << ((bits + 1) // 2)
        self.far = rows // self.near

    def near_index(self):
        return lax.rem(lax.axis_index("row"), self.near)

    def far_index(self):
        return lax.div(lax.axis_index("row"), self.near)

    def swap(self, value, offset):
        return lax.ppermute(value, "row", [(i, i ^ offset) for i in range(self.rows)])

    def near_swap(self, value, offset):
        return self.swap(value, offset)

    def far_swap(self, value, offset):
        return self.swap(value, offset * self.near)


VMEM = pl.BlockSpec(memory_space=pltpu.VMEM)
PARAMS = pltpu.CompilerParams(vmem_limit_bytes=8 * 2**20)


def spread(value):
    return jnp.broadcast_to(value, (STEP, 128))


def pivot_block(d):
    d = [list(row) for row in d]
    low = [[None] * STEP for _ in range(STEP)]
    inv = [[None] * STEP for _ in range(STEP)]
    pivots, recips = [], []
    for t in range(STEP):
        pivots.append(d[t][t])
        recips.append(1.0 / d[t][t])
        for r in range(t + 1, STEP):
            low[r][t] = d[r][t] * recips[t]
            for s in range(t + 1, r + 1):
                d[r][s] = d[r][s] - low[r][t] * d[s][t]
    for s in range(STEP):
        for r in range(s + 1, STEP):
            total = -low[r][s]
            for t in range(s + 1, r):
                total = total - low[r][t] * inv[t][s]
            inv[r][s] = total
    return pivots, recips, inv


def block_inverse(recips, inv):
    scaled = [[inv[r][s] * recips[r] for s in range(r)] + [recips[r]] for r in range(STEP)]
    out = [[None] * STEP for _ in range(STEP)]
    for s in range(STEP):
        for t in range(s + 1):
            total = scaled[s][t]
            for r in range(s + 1, STEP):
                total = total + inv[r][s] * scaled[r][t]
            out[s][t] = out[t][s] = total
    return out


def weighted(weights, rows):
    total = weights[0] * rows[0]
    for weight, row in zip(weights[1:], rows[1:]):
        total = total + weight * row
    return total


def factor_rows(work, factor_ref, inverse_t_ref, base):
    halves = range(work.shape[1] // 128)
    lane = lax.broadcasted_iota(jnp.int32, (STEP, 128), 1)
    sub = lax.broadcasted_iota(jnp.int32, (STEP, 128), 0)
    steps = range(STEP)
    count = BLOCK // STEP
    rows = [
        [work[base + STEP * i : base + STEP * (i + 1), 128 * h : 128 * (h + 1)] for h in halves]
        for i in range(count)
    ]
    for g in range(count):
        j = base + STEP * g
        home, first = divmod(j, 128)
        columns = [
            [spread(rows[i][home][:, first + s : first + s + 1]) for s in steps]
            for i in range(g, count)
        ]
        block = [[spread(columns[0][s][r : r + 1, :]) for s in range(r + 1)] for r in steps]
        pivots, recips, inv = pivot_block(block)
        own = [[spread(rows[g][h][t : t + 1, :]) for t in steps] for h in halves]

        roots = [lax.rsqrt(pivot) for pivot in pivots]
        scaled_inv = []
        for s in steps:
            column = jnp.where(sub == s, roots[s], 0.0)
            for t in range(s + 1, STEP):
                column = jnp.where(sub == t, inv[t][s] * roots[t], column)
            scaled_inv.append(column)
        corner = jnp.zeros((STEP, 128), jnp.float32)
        for s in steps:
            corner = jnp.where(lane == first + s, scaled_inv[s], corner)
        for h in halves:
            scaled = weighted(scaled_inv, own[h])
            col = lane + 128 * h
            place = (slice(j, j + STEP), slice(128 * h, 128 * (h + 1)))
            factor_ref[place] = jnp.where(col >= j + sub, scaled, 0.0)
            inverse_t_ref[place] = jnp.where(col < j, scaled, corner if h == home else 0.0)

        if g + 1 < count:
            solve = block_inverse(recips, inv)
            pulls = []
            for h in halves:
                pulls.append([weighted(solve[s], own[h]) for s in steps])
                if h == home:
                    for s in steps:
                        for t in steps:
                            entry = solve[s][t] + 1.0 if s == t else solve[s][t]
                            pulls[h][s] = jnp.where(lane == first + t, entry, pulls[h][s])
            for i in range(g + 1, count):
                for h in halves:
                    for s in steps:
                        rows[i][h] = rows[i][h] - columns[i - g][s] * pulls[h][s]


def factor_kernel(own_ref, other_ref, factor_ref, inverse_t_ref, work):
    order = factor_ref.shape[0]
    half = order // 2
    first = lax.rem(lax.axis_index("col"), 2) == 0
    own, other = own_ref[...], other_ref[...]
    packed = jnp.where(first, own, other)
    corner = jnp.where(first, other, own)[:half, :]
    square = packed[:half, :]
    flipped = square.T
    row = lax.broadcasted_iota(jnp.int32, (half, half), 0)
    col = lax.broadcasted_iota(jnp.int32, (half, half), 1)
    damping = jnp.where(row == col, damping_total, 0.0)
    work[:half, :half] = jnp.where(row <= col, square, flipped) + damping
    work[:half, half:] = corner
    work[half:, :half] = corner.T
    last = jnp.where(row == col, packed[half : half + 1, :], jnp.where(row > col, square, flipped))
    work[half:, half:] = last + damping
    for base in range(0, order, BLOCK):
        end = base + BLOCK
        factor_rows(work, factor_ref, inverse_t_ref, base)
        if end < order:
            lane = lax.broadcasted_iota(jnp.int32, (1, order), 1)
            upper = factor_ref[base:end, :]
            rest = jnp.where((lane >= base) & (lane < end), 0.0, work[end:, :])
            work[end:, :] = rest - lax.dot_general(
                upper[:, end:],
                jnp.where(lane < end, inverse_t_ref[base:end, :], upper),
                (((0,), (0,)), ((), ())),
                precision=HIGHEST,
                preferred_element_type=jnp.float32,
            )


def cholesky_pair(own, other):
    order = 2 * own.shape[1]
    out = jax.ShapeDtypeStruct((order, order), jnp.float32)
    return pl.pallas_call(
        factor_kernel,
        out_shape=[out, out],
        in_specs=[VMEM] * 2,
        out_specs=[VMEM] * 2,
        scratch_shapes=[pltpu.VMEM((order, order), jnp.float32)],
        cost_estimate=pl.CostEstimate(
            flops=8 * order**3, bytes_accessed=48 * order * order, transcendentals=order
        ),
        compiler_params=PARAMS,
        name="factor",
    )(own, other)


def gram_kernel(count, panel_ref, out_ref, turned_ref):
    half = out_ref.shape[1]
    rows = panel_ref.shape[0] // count
    grams = []
    for k in range(count):
        part = panel_ref[rows * k : rows * (k + 1), :]
        turned = part.T
        turned_ref[:, rows * k : rows * (k + 1)] = turned
        grams.append(jnp.dot(turned, part, preferred_element_type=jnp.float32))
    gram = tree_sum(grams)
    row = lax.broadcasted_iota(jnp.int32, (half, half), 0)
    col = lax.broadcasted_iota(jnp.int32, (half, half), 1)
    last = gram[half:, half:]
    packed = jnp.where(row <= col, gram[:half, :half], last)
    first = lax.rem(lax.axis_index("col"), 2) == 0
    out_ref[:half, :] = jnp.where(first, packed, gram[:half, half:])
    diagonal = jnp.sum(jnp.where(row == col, last, 0.0), axis=0, keepdims=True)
    out_ref[half:, :] = jnp.broadcast_to(diagonal, (8, half))


def gram_part(count, panel):
    rows, order = panel.shape
    half = order // 2
    return pl.pallas_call(
        functools.partial(gram_kernel, count),
        out_shape=[
            jax.ShapeDtypeStruct((half + 8, half), jnp.float32),
            jax.ShapeDtypeStruct((order, rows), panel.dtype),
        ],
        in_specs=[VMEM],
        out_specs=[VMEM] * 2,
        compiler_params=PARAMS,
        name="gram_part",
    )(panel)


def cross_kernel(near, far, turned_ref, *refs):
    tiles, outs, whole = refs[:near], refs[near : near + far], refs[near + far]
    index = lax.div(lax.axis_index("row"), near)
    width = outs[0].shape[1]
    rows = tiles[0].shape[0]
    total = None
    for k, ref in enumerate(tiles):
        term = jnp.dot(
            turned_ref[:, rows * k : rows * (k + 1)], ref[...], preferred_element_type=jnp.float32
        )
        total = term if total is None else total + term
    whole[...] = total
    for k in range(far):
        start = pl.multiple_of((index ^ k) * width, width)
        outs[k][...] = whole[:, pl.ds(start, width)]


def cross_part(groups, turned, tiles):
    order = turned.shape[0]
    width = tiles[0].shape[1] // groups.far
    if width % 128:
        whole = jnp.dot(
            turned, jnp.concatenate(tiles, 0), preferred_element_type=jnp.float32
        )
        return [
            lax.dynamic_slice_in_dim(whole, (groups.far_index() ^ k) * width, width, 1)
            for k in range(groups.far)
        ]
    return pl.pallas_call(
        functools.partial(cross_kernel, groups.near, groups.far),
        out_shape=[jax.ShapeDtypeStruct((order, width), jnp.float32)] * groups.far,
        in_specs=[VMEM] * (1 + groups.near),
        out_specs=[VMEM] * groups.far,
        scratch_shapes=[pltpu.VMEM((order, tiles[0].shape[1]), jnp.float32)],
        compiler_params=PARAMS,
        name="cross_part",
    )(turned, *tiles)


def update_kernel(near, far, basis_ref, masked_ref, *refs):
    slots, (coupling_ref, updated_ref) = refs[:near], refs[near:]
    index = lax.axis_index("row")
    near_index, far_index = lax.rem(index, near), lax.div(index, near)
    basis = basis_ref[...]
    width = slots[0].shape[1] // far
    for i, slot in enumerate(slots):
        removed = jnp.dot(basis, slot[...], preferred_element_type=jnp.float32)
        for k in range(far):
            start = ((near_index ^ i) * far + (far_index ^ k)) * width
            cols = pl.ds(pl.multiple_of(start, width), width)
            part = slice(k * width, (k + 1) * width)
            coupling_ref[:, cols] = slot[:, part]
            left = masked_ref[:, cols].astype(jnp.float32) - removed[:, part]
            updated_ref[:, cols] = left.astype(updated_ref.dtype)


def update(groups, basis, masked, slots):
    near, far = groups.near, groups.far
    rows, cols = masked.shape
    width = slots[0].shape[1] // far
    if width % 128:
        coupling = jnp.zeros((slots[0].shape[0], cols), slots[0].dtype)
        for i, slot in enumerate(slots):
            for k in range(far):
                start = ((groups.near_index() ^ i) * far + (groups.far_index() ^ k)) * width
                part = slot[:, k * width : (k + 1) * width]
                coupling = lax.dynamic_update_slice_in_dim(coupling, part, start, 1)
        removed = jnp.dot(basis, coupling, preferred_element_type=jnp.float32)
        return coupling, (masked.astype(jnp.float32) - removed).astype(masked.dtype)
    return pl.pallas_call(
        functools.partial(update_kernel, near, far),
        out_shape=[
            jax.ShapeDtypeStruct((slots[0].shape[0], cols), slots[0].dtype),
            jax.ShapeDtypeStruct((rows, cols), masked.dtype),
        ],
        in_specs=[VMEM] * (2 + near),
        out_specs=[VMEM] * 2,
        compiler_params=PARAMS,
        name="update",
    )(basis, masked, *slots)


def gather_slots(groups, shard):
    far = range(1, groups.far)
    wide = jnp.concatenate([shard] + [groups.far_swap(shard, k) for k in far], axis=1)
    return [wide] + [groups.near_swap(wide, k) for k in range(1, groups.near)]


def local(groups, panel, trailing, tile_mask):
    near, far = groups.near, groups.far
    stacked = jnp.concatenate(
        [panel] + [groups.near_swap(panel, k) for k in range(1, near)], axis=0
    )
    gathered = lax.all_gather(stacked, "col", axis=1, tiled=True)

    local_rows = trailing.shape[0]
    local_cols = trailing.shape[1]
    tiles = trailing.reshape(local_rows // TILE, TILE, local_cols // TILE, TILE)
    masked = (tiles * tile_mask.astype(jnp.bfloat16)[:, None, :, None]).reshape(
        local_rows, local_cols
    )
    chunk = local_cols // near
    chunks = [
        lax.dynamic_slice_in_dim(masked, (groups.near_index() ^ k) * chunk, chunk, 1)
        for k in range(near)
    ]
    chunks = chunks[:1] + [groups.near_swap(chunks[k], k) for k in range(1, near)]

    gram_terms, turned = gram_part(near, gathered)
    gram_own = tree_sum(
        [gram_terms] + [groups.far_swap(gram_terms, k) for k in range(1, far)]
    )
    gram_other = lax.ppermute(gram_own, "col", [(i, i ^ 1) for i in range(groups.cols)])

    cross_terms = cross_part(groups, turned, chunks)
    summed = tree_sum(
        [cross_terms[0]] + [groups.far_swap(cross_terms[k], k) for k in range(1, far)]
    )

    upper_factor, inverse_t = cholesky_pair(gram_own, gram_other)
    shard = jnp.dot(inverse_t, summed, precision=HIGHEST).astype(jnp.bfloat16)
    slots = gather_slots(groups, shard)
    basis = lax.dot_general(
        gathered[: panel.shape[0], :].astype(jnp.float32), inverse_t, (((1,), (1,)), ((), ())), precision=HIGHEST
    ).astype(jnp.bfloat16)
    coupling, updated = update(groups, basis, masked, slots)
    return (upper_factor, coupling, updated)


def solution(mesh):
    placed = (P("row", "col"), P("row", "col"), P("row", "col"))
    groups = Groups(mesh.shape["row"], mesh.shape["col"])
    return jax.shard_map(
        functools.partial(local, groups),
        mesh=mesh,
        in_specs=placed,
        out_specs=(P(), P(None, "col"), P("row", "col")),
        check_vma=False,
    )
```

time: 94.1 us -> 65.2 us (0.69)
  Pallas kernels: 28.8 us -> 14.2 us
  local copies, waits for them, and re-layouts: 7.39 us -> 0.86 us
  waiting for transfers between devices: 24.4 us -> 18.2 us
  matrix products: 3.22 us -> 0.71 us
  starting transfers between devices: 24.7 us -> 26.8 us
    pallas_call x2 -> x3, Pallas kernels: 26 us -> 13.7 us  [the longest x1 11 us: cholesky_pair(): pl.pallas_call(factor_kernel, out_shape=[out, out], in_specs=[VMEM] * 2,...]
    ppermute x18, waiting for transfers between devices: 24.4 us -> 17 us  [swap(): lax.ppermute(value, 'row', [(i, i ^ offset) for i in range(self.rows)])]
    slice x15 -> x0, local copies, waits for them, and re-layouts: 2.9 us -> none  [gather_columns(): part = slot[:, k * width:(k + 1) * width]]
    pallas_call x1, Pallas kernels: 2.81 us -> 0.5 us  [cross_part(): pl.pallas_call(functools.partial(cross_kernel, groups.near, groups.far),...]
    ppermute x18, starting transfers between devices: 24.7 us -> 26.7 us  [swap(): lax.ppermute(value, 'row', [(i, i ^ offset) for i in range(self.rows)])]
    unnamed x28 -> x6, local copies, waits for them, and re-layouts: 2.74 us -> 0.74 us
    dot_general x2 -> x1, matrix products: 1.78 us -> 0.33 us  [local(): lax.dot_general(gathered[:panel.shape[0], :].astype(jnp.float32), inverse...]
    ppermute x1, waiting for transfers between devices: 0.01 us -> 1.25 us  [local(): lax.ppermute(gram_own, 'col', [(i, i ^ 1) for i in range(groups.cols)])]
  transfers between devices with their start and end apart: 19 -> 19, of which waited for: 10 -> 7; matrix products, arithmetic and copies ran while one was open for 7% -> 3% of each run, Pallas kernels for 28% -> 18%
where the time goes in v3:
time: 65.2 us; the launch traced here: 65 us
  starting transfers between devices  26.8 us (41%)
  waiting for transfers between devices  18.2 us (28%)
  Pallas kernels  14.2 us (22%)
  blocking collectives  2.18 us (3%)
  other arithmetic  1.37 us (2%)
  local copies, waits for them, and re-layouts  0.86 us (1%)
  between operations  0.73 us (1%)
  matrix products  0.71 us (1%)
    ppermute x18, starting transfers between devices, swap(): lax.ppermute(value, 'row', [(i, i ^ offset) for i in range(self.rows)])  26.7 us
    ppermute x18, waiting for transfers between devices, swap(): lax.ppermute(value, 'row', [(i, i ^ offset) for i in range(self.rows)])  17 us
    pallas_call x1, Pallas kernels, cholesky_pair(): pl.pallas_call(factor_kernel, out_shape=[out, out], in_specs=[VMEM] * 2,...  11 us
    pallas_call x1, Pallas kernels, update(): pl.pallas_call(functools.partial(update_kernel, near, far), out_shape=[ja...  2.34 us
    all_gather x1, blocking collectives, local(): gathered = lax.all_gather(stacked, 'col', axis=1, tiled=True)  2.18 us
  transfers between devices with their start and end apart: 19, of which 7 were waited for; matrix products, arithmetic and copies ran while one was open for 3% of the time, Pallas kernels for 18%

profile of v3, /device:TPU:0, one launch (start us, length us, event | category | flops | bytes accessed | tf_op | source)
XLA Modules:
  0.0 65.0 jit_solution(14002741258972599868)
XLA Ops:
  0.6 3.0 %collective-permute-start.1 = (bf16[256,128]{1,0:T(8,128)(2,1)}, bf16[256,128]{1,0:T(8,128)(2,1)S(1)}, u32[]{:S(2)}, u32[]{:S(2)}) collective-permute-start(bf16[256,128]{1,0:T(8,128)(2,1)} %param.3), channel_id=1, source_target_pairs={{0,4},{2,6},{4,0},{6,2},{8,12},{10,14},{12,8},{14,10},{16,20},{18,... | collective-permute-start | bytes 196616 | tf_op jit(solution)/shard_map/ppermute | solution.py:45
  3.7 1.5 %collective-permute-start = (bf16[256,128]{1,0:T(8,128)(2,1)}, bf16[256,128]{1,0:T(8,128)(2,1)S(1)}, u32[]{:S(2)}, u32[]{:S(2)}) collective-permute-start(bf16[256,128]{1,0:T(8,128)(2,1)} %param.3), channel_id=1, source_target_pairs={{0,2},{2,0},{4,6},{6,4},{8,10},{10,8},{12,14},{14,12},{16,18},{18,... | collective-permute-start | bytes 196616 | tf_op jit(solution)/shard_map/ppermute | solution.py:45
  5.2 0.1 collective-permute-start.2
  5.2 0.0 copy-start.1
  5.2 0.7 %copy-done.1 = s32[1,8]{1,0:T(1,128)S(1)} copy-done((s32[1,8]{1,0:T(1,128)S(1)}, s32[1,8]{1,0:T(1,128)}, u32[]{:S(2)}) %copy-start.1) | copy-done | bytes 56
  5.9 0.1 broadcast_bitcast_fusion
  6.0 1.3 %broadcast_multiply_fusion.masked_ref = bf16[256,2048]{1,0:T(8,128)(2,1)S(1)} fusion(bf16[256,2048]{1,0:T(8,128)(2,1)} %param.4, bf16[2048]{0:T(1024)(128)(2,1)S(1)} %bitcast.7), kind=kLoop, calls=%fused_computation.2 | loop fusion | flops 524288 | bytes 2101248 | tf_op jit(solution)/shard_map/mul | solution.py:340
  7.2 0.0 copy-start
  7.3 0.1 constant_dynamic-slice_fusion
  7.4 2.9 %collective-permute-start.9 = (bf16[256,512]{1,0:T(8,128)(2,1)S(1)}, bf16[256,512]{1,0:T(8,128)(2,1)S(1)}, u32[]{:S(2)}, u32[]{:S(2)}) collective-permute-start(bf16[256,512]{1,0:T(8,128)(2,1)S(1)} %get-tuple-element.23), channel_id=1, source_target_pairs={{0,6},{2,4},{4,2},{6,0},{8,14},{10,12},{12,10},{14,8},{16,22},{18,... | collective-permute-start | bytes 786440 | tf_op jit(solution)/shard_map/ppermute | solution.py:45
  10.3 0.5 collective-permute-start.8
  10.8 0.0 collective-permute-done.1
  10.8 0.1 collective-permute-start.7
  11.0 0.0 collective-permute-done
  11.0 0.0 collective-permute-done.2
  11.0 0.0 copy-done
  11.0 2.2 %all_gather.3.panel_ref = bf16[1024,256]{1,0:T(8,128)(2,1)S(1)} all-gather(bf16[1024,128]{1,0:T(8,128)(2,1)S(1)} %pad_maximum_fusion), channel_id=1, replica_groups=mesh['row'=16,'col'=2] {'col'}, dimensions={1}, use_global_device_ids=true | all-gather | bytes 786432 | tf_op jit(solution)/shard_map/all_gather | solution.py:335
  13.2 0.4 gram_part.1
  13.6 4.1 %collective-permute-start.5 = (f32[136,128]{1,0:T(8,128)S(1)}, f32[136,128]{1,0:T(8,128)S(1)}, u32[]{:S(2)}, u32[]{:S(2)}) collective-permute-start(f32[136,128]{1,0:T(8,128)S(1)} %get-tuple-element.13), channel_id=1, source_target_pairs={{0,24},{2,26},{4,28},{6,30},{8,16},{10,18},{12,20},{14,22},{16,8},... | collective-permute-start | bytes 208904 | tf_op jit(solution)/shard_map/ppermute | solution.py:45
  17.6 0.0 collective-permute-start.4
  17.6 0.0 collective-permute-done.9.refs_3_
  17.6 2.0 %collective-permute-start.3 = (f32[136,128]{1,0:T(8,128)S(1)}, f32[136,128]{1,0:T(8,128)S(1)}, u32[]{:S(2)}, u32[]{:S(2)}) collective-permute-start(f32[136,128]{1,0:T(8,128)S(1)} %get-tuple-element.13), channel_id=1, source_target_pairs={{0,8},{2,10},{4,12},{6,14},{8,0},{10,2},{12,4},{14,6},{16,24},{18,... | collective-permute-start | bytes 208904 | tf_op jit(solution)/shard_map/ppermute | solution.py:45
  19.6 2.1 %collective-permute-done.8.refs_2_ = bf16[256,512]{1,0:T(8,128)(2,1)S(1)} collective-permute-done((bf16[256,512]{1,0:T(8,128)(2,1)S(1)}, bf16[256,512]{1,0:T(8,128)(2,1)S(1)}, u32[]{:S(2)}, u32[]{:S(2)}) %collective-permute-start.8) | collective-permute-done | bytes 262176 | tf_op jit(solution)/shard_map/ppermute | solution.py:45
  21.8 0.0 collective-permute-done.7.refs_1_
  21.8 0.5 cross_part.1
  22.3 1.6 %collective-permute-start.10 = (f32[256,128]{1,0:T(8,128)S(1)}, f32[256,128]{1,0:T(8,128)S(1)}, u32[]{:S(2)}, u32[]{:S(2)}) collective-permute-start(f32[256,128]{1,0:T(8,128)S(1)} %get-tuple-element.18), channel_id=1, source_target_pairs={{0,8},{2,10},{4,12},{6,14},{8,0},{10,2},{12,4},{14,6},{16,24},{18,... | collective-permute-start | bytes 393224 | tf_op jit(solution)/shard_map/ppermute | solution.py:45
  23.9 2.6 %collective-permute-start.11 = (f32[256,128]{1,0:T(8,128)S(1)}, f32[256,128]{1,0:T(8,128)S(1)}, u32[]{:S(2)}, u32[]{:S(2)}) collective-permute-start(f32[256,128]{1,0:T(8,128)S(1)} %get-tuple-element.19), channel_id=1, source_target_pairs={{0,16},{2,18},{4,20},{6,22},{8,24},{10,26},{12,28},{14,30},{16,0},... | collective-permute-start | bytes 393224 | tf_op jit(solution)/shard_map/ppermute | solution.py:45
  26.5 0.0 collective-permute-done.5
  26.5 0.2 collective-permute-start.12
  26.7 0.0 collective-permute-done.4
  26.7 0.0 collective-permute-done.3
  26.8 0.1 collective-permute-start.6
  26.8 1.2 %collective-permute-done.6.other_ref = f32[136,128]{1,0:T(8,128)S(1)} collective-permute-done((f32[136,128]{1,0:T(8,128)S(1)}, f32[136,128]{1,0:T(8,128)S(1)}, u32[]{:S(2)}, u32[]{:S(2)}) %collective-permute-start.6) | collective-permute-done | bytes 69664 | tf_op jit(solution)/shard_map/ppermute | solution.py:354
  28.1 11.0 %factor.1 = (f32[256,256]{1,0:T(8,128)}, f32[256,256]{1,0:T(8,128)S(1)}) custom-call(f32[136,128]{1,0:T(8,128)S(1)} %add_add_fusion.own_ref, f32[136,128]{1,0:T(8,128)S(1)} %collective-permute-done.6.other_ref), custom_call_target="tpu_custom_call" | custom-call | flops 134217728 | bytes 3145728 | tf_op jit(solution)/shard_map/factor/pallas_call | solution.py:192
  39.1 0.0 collective-permute-done.10
  39.1 0.0 collective-permute-done.11
  39.1 0.0 collective-permute-done.12
  39.1 0.4 convolution_convert_fusion.1
  39.5 3.7 %collective-permute-start.15 = (bf16[256,128]{1,0:T(8,128)(2,1)S(1)}, bf16[256,128]{1,0:T(8,128)(2,1)S(1)}, u32[]{:S(2)}, u32[]{:S(2)}) collective-permute-start(bf16[256,128]{1,0:T(8,128)(2,1)S(1)} %convolution_convert_fusion.1), channel_id=1, source_target_pairs={{0,24},{2,26},{4,28},{6,30},{8,16},{10,18},{12,20},{14,22},{16,8},... | collective-permute-start | bytes 196616 | tf_op jit(solution)/shard_map/ppermute | solution.py:45
  43.1 0.0 collective-permute-start.14
  43.1 0.8 %collective-permute-start.13 = (bf16[256,128]{1,0:T(8,128)(2,1)S(1)}, bf16[256,128]{1,0:T(8,128)(2,1)S(1)}, u32[]{:S(2)}, u32[]{:S(2)}) collective-permute-start(bf16[256,128]{1,0:T(8,128)(2,1)S(1)} %convolution_convert_fusion.1), channel_id=1, source_target_pairs={{0,8},{2,10},{4,12},{6,14},{8,0},{10,2},{12,4},{14,6},{16,24},{18,... | collective-permute-start | bytes 196616 | tf_op jit(solution)/shard_map/ppermute | solution.py:45
  43.9 2.3 %collective-permute-done.15 = bf16[256,128]{1,0:T(8,128)(2,1)S(1)} collective-permute-done((bf16[256,128]{1,0:T(8,128)(2,1)S(1)}, bf16[256,128]{1,0:T(8,128)(2,1)S(1)}, u32[]{:S(2)}, u32[]{:S(2)}) %collective-permute-start.15) | collective-permute-done | bytes 65568 | tf_op jit(solution)/shard_map/ppermute | solution.py:45
  46.2 2.2 %collective-permute-done.14 = bf16[256,128]{1,0:T(8,128)(2,1)S(1)} collective-permute-done((bf16[256,128]{1,0:T(8,128)(2,1)S(1)}, bf16[256,128]{1,0:T(8,128)(2,1)S(1)}, u32[]{:S(2)}, u32[]{:S(2)}) %collective-permute-start.14) | collective-permute-done | bytes 65568 | tf_op jit(solution)/shard_map/ppermute | solution.py:45
  48.4 0.4 collective-permute-done.13
  48.8 1.6 %collective-permute-start.18 = (bf16[256,512]{1,0:T(8,128)(2,1)S(1)}, bf16[256,512]{1,0:T(8,128)(2,1)S(1)}, u32[]{:S(2)}, u32[]{:S(2)}) collective-permute-start(bf16[256,512]{1,0:T(8,128)(2,1)S(1)} %pad_maximum_fusion.1.refs_0_), channel_id=1, source_target_pairs={{0,6},{2,4},{4,2},{6,0},{8,14},{10,12},{12,10},{14,8},{16,22},{18,... | collective-permute-start | bytes 786440 | tf_op jit(solution)/shard_map/ppermute | solution.py:45
  50.5 1.3 %collective-permute-start.17 = (bf16[256,512]{1,0:T(8,128)(2,1)S(1)}, bf16[256,512]{1,0:T(8,128)(2,1)S(1)}, u32[]{:S(2)}, u32[]{:S(2)}) collective-permute-start(bf16[256,512]{1,0:T(8,128)(2,1)S(1)} %pad_maximum_fusion.1.refs_0_), channel_id=1, source_target_pairs={{0,4},{2,6},{4,0},{6,2},{8,12},{10,14},{12,8},{14,10},{16,20},{18,... | collective-permute-start | bytes 786440 | tf_op jit(solution)/shard_map/ppermute | solution.py:45
  51.8 0.6 collective-permute-start.16
  52.4 0.3 convolution_convert_fusion.basis_ref
  52.7 6.4 %collective-permute-done.18.refs_3_ = bf16[256,512]{1,0:T(8,128)(2,1)S(1)} collective-permute-done((bf16[256,512]{1,0:T(8,128)(2,1)S(1)}, bf16[256,512]{1,0:T(8,128)(2,1)S(1)}, u32[]{:S(2)}, u32[]{:S(2)}) %collective-permute-start.18) | collective-permute-done | bytes 262176 | tf_op jit(solution)/shard_map/ppermute | solution.py:45
  59.1 3.6 %collective-permute-done.17.refs_2_ = bf16[256,512]{1,0:T(8,128)(2,1)S(1)} collective-permute-done((bf16[256,512]{1,0:T(8,128)(2,1)S(1)}, bf16[256,512]{1,0:T(8,128)(2,1)S(1)}, u32[]{:S(2)}, u32[]{:S(2)}) %collective-permute-start.17) | collective-permute-done | bytes 262176 | tf_op jit(solution)/shard_map/ppermute | solution.py:45
  62.6 0.0 collective-permute-done.16.refs_1_
  62.6 2.3 %update.1 = (bf16[256,2048]{1,0:T(8,128)(2,1)}, bf16[256,2048]{1,0:T(8,128)(2,1)}) custom-call(bf16[256,256]{1,0:T(8,128)(2,1)S(1)} %convolution_convert_fusion.basis_ref, bf16[256,2048]{1,0:T(8,128)(2,1)S(1)} %broadcast_multiply_fusion.masked_ref, bf16[256,512]{1,0:T(8,128)(2,1)S(1)} %pad_maximum_fusion.1.refs_0_, ...), custom_call_target="tpu_custom_call" | custom-call | tf_op jit(solution)/shard_map/update/pallas_call | solution.py:311
  (5 shorter events, 0.1 us)
Async XLA Ops:
  0.6 10.2 %collective-permute-start.1 = (bf16[256,128]{1,0:T(8,128)(2,1)}, bf16[256,128]{1,0:T(8,128)(2,1)S(1)}, u32[]{:S(2)}, u32[]{:S(2)}) collective-permute-start(bf16[256,128]{1,0:T(8,128)(2,1)} %param.3), channel_id=1, source_target_pairs={{0,4},{2,6},{4,0},{6,2},{8,12},{10,14},{12,8},{14,10},{16,20},{18,... | collective-permute-start | bytes 196616 | tf_op jit(solution)/shard_map/ppermute | solution.py:45
  3.7 7.3 %collective-permute-start = (bf16[256,128]{1,0:T(8,128)(2,1)}, bf16[256,128]{1,0:T(8,128)(2,1)S(1)}, u32[]{:S(2)}, u32[]{:S(2)}) collective-permute-start(bf16[256,128]{1,0:T(8,128)(2,1)} %param.3), channel_id=1, source_target_pairs={{0,2},{2,0},{4,6},{6,4},{8,10},{10,8},{12,14},{14,12},{16,18},{18,... | collective-permute-start | bytes 196616 | tf_op jit(solution)/shard_map/ppermute | solution.py:45
  5.2 5.8 %collective-permute-start.2 = (bf16[256,128]{1,0:T(8,128)(2,1)}, bf16[256,128]{1,0:T(8,128)(2,1)S(1)}, u32[]{:S(2)}, u32[]{:S(2)}) collective-permute-start(bf16[256,128]{1,0:T(8,128)(2,1)} %param.3), channel_id=1, source_target_pairs={{0,6},{2,4},{4,2},{6,0},{8,14},{10,12},{12,10},{14,8},{16,22},{18,... | collective-permute-start | bytes 196616 | tf_op jit(solution)/shard_map/ppermute | solution.py:45
  5.2 0.7 %copy-start.1 = (s32[1,8]{1,0:T(1,128)S(1)}, s32[1,8]{1,0:T(1,128)}, u32[]{:S(2)}) copy-start(s32[1,8]{1,0:T(1,128)} %param.5) | copy-start | bytes 100
  7.2 3.7 %copy-start = (bf16[256,128]{1,0:T(8,128)(2,1)S(1)}, bf16[256,128]{1,0:T(8,128)(2,1)}, u32[]{:S(2)}) copy-start(bf16[256,128]{1,0:T(8,128)(2,1)} %param.3) | copy-start | bytes 196612
  7.4 10.3 %collective-permute-start.9 = (bf16[256,512]{1,0:T(8,128)(2,1)S(1)}, bf16[256,512]{1,0:T(8,128)(2,1)S(1)}, u32[]{:S(2)}, u32[]{:S(2)}) collective-permute-start(bf16[256,512]{1,0:T(8,128)(2,1)S(1)} %get-tuple-element.23), channel_id=1, source_target_pairs={{0,6},{2,4},{4,2},{6,0},{8,14},{10,12},{12,10},{14,8},{16,22},{18,... | collective-permute-start | bytes 786440 | tf_op jit(solution)/shard_map/ppermute | solution.py:45
  10.3 11.4 %collective-permute-start.8 = (bf16[256,512]{1,0:T(8,128)(2,1)S(1)}, bf16[256,512]{1,0:T(8,128)(2,1)S(1)}, u32[]{:S(2)}, u32[]{:S(2)}) collective-permute-start(bf16[256,512]{1,0:T(8,128)(2,1)S(1)} %get-tuple-element.24), channel_id=1, source_target_pairs={{0,4},{2,6},{4,0},{6,2},{8,12},{10,14},{12,8},{14,10},{16,20},{18,... | collective-permute-start | bytes 786440 | tf_op jit(solution)/shard_map/ppermute | solution.py:45
  10.8 10.9 %collective-permute-start.7 = (bf16[256,512]{1,0:T(8,128)(2,1)S(1)}, bf16[256,512]{1,0:T(8,128)(2,1)S(1)}, u32[]{:S(2)}, u32[]{:S(2)}) collective-permute-start(bf16[256,512]{1,0:T(8,128)(2,1)S(1)} %get-tuple-element.25), channel_id=1, source_target_pairs={{0,2},{2,0},{4,6},{6,4},{8,10},{10,8},{12,14},{14,12},{16,18},{18,... | collective-permute-start | bytes 786440 | tf_op jit(solution)/shard_map/ppermute | solution.py:45
  13.6 13.0 %collective-permute-start.5 = (f32[136,128]{1,0:T(8,128)S(1)}, f32[136,128]{1,0:T(8,128)S(1)}, u32[]{:S(2)}, u32[]{:S(2)}) collective-permute-start(f32[136,128]{1,0:T(8,128)S(1)} %get-tuple-element.13), channel_id=1, source_target_pairs={{0,24},{2,26},{4,28},{6,30},{8,16},{10,18},{12,20},{14,22},{16,8},... | collective-permute-start | bytes 208904 | tf_op jit(solution)/shard_map/ppermute | solution.py:45
  17.6 9.1 %collective-permute-start.4 = (f32[136,128]{1,0:T(8,128)S(1)}, f32[136,128]{1,0:T(8,128)S(1)}, u32[]{:S(2)}, u32[]{:S(2)}) collective-permute-start(f32[136,128]{1,0:T(8,128)S(1)} %get-tuple-element.13), channel_id=1, source_target_pairs={{0,16},{2,18},{4,20},{6,22},{8,24},{10,26},{12,28},{14,30},{16,0},... | collective-permute-start | bytes 208904 | tf_op jit(solution)/shard_map/ppermute | solution.py:45
  17.6 9.1 %collective-permute-start.3 = (f32[136,128]{1,0:T(8,128)S(1)}, f32[136,128]{1,0:T(8,128)S(1)}, u32[]{:S(2)}, u32[]{:S(2)}) collective-permute-start(f32[136,128]{1,0:T(8,128)S(1)} %get-tuple-element.13), channel_id=1, source_target_pairs={{0,8},{2,10},{4,12},{6,14},{8,0},{10,2},{12,4},{14,6},{16,24},{18,... | collective-permute-start | bytes 208904 | tf_op jit(solution)/shard_map/ppermute | solution.py:45
  22.3 16.8 %collective-permute-start.10 = (f32[256,128]{1,0:T(8,128)S(1)}, f32[256,128]{1,0:T(8,128)S(1)}, u32[]{:S(2)}, u32[]{:S(2)}) collective-permute-start(f32[256,128]{1,0:T(8,128)S(1)} %get-tuple-element.18), channel_id=1, source_target_pairs={{0,8},{2,10},{4,12},{6,14},{8,0},{10,2},{12,4},{14,6},{16,24},{18,... | collective-permute-start | bytes 393224 | tf_op jit(solution)/shard_map/ppermute | solution.py:45
  23.9 15.1 %collective-permute-start.11 = (f32[256,128]{1,0:T(8,128)S(1)}, f32[256,128]{1,0:T(8,128)S(1)}, u32[]{:S(2)}, u32[]{:S(2)}) collective-permute-start(f32[256,128]{1,0:T(8,128)S(1)} %get-tuple-element.19), channel_id=1, source_target_pairs={{0,16},{2,18},{4,20},{6,22},{8,24},{10,26},{12,28},{14,30},{16,0},... | collective-permute-start | bytes 393224 | tf_op jit(solution)/shard_map/ppermute | solution.py:45
  26.5 12.6 %collective-permute-start.12 = (f32[256,128]{1,0:T(8,128)S(1)}, f32[256,128]{1,0:T(8,128)S(1)}, u32[]{:S(2)}, u32[]{:S(2)}) collective-permute-start(f32[256,128]{1,0:T(8,128)S(1)} %get-tuple-element.20), channel_id=1, source_target_pairs={{0,24},{2,26},{4,28},{6,30},{8,16},{10,18},{12,20},{14,22},{16,8},... | collective-permute-start | bytes 393224 | tf_op jit(solution)/shard_map/ppermute | solution.py:45
  26.8 1.3 %collective-permute-start.6 = (f32[136,128]{1,0:T(8,128)S(1)}, f32[136,128]{1,0:T(8,128)S(1)}, u32[]{:S(2)}, u32[]{:S(2)}) collective-permute-start(f32[136,128]{1,0:T(8,128)S(1)} %add_add_fusion.own_ref), channel_id=1, source_target_pairs={{0,1},{1,0},{2,3},{3,2},{4,5},{5,4},{6,7},{7,6},{8,9},{9,8},{10,11... | collective-permute-start | bytes 208904 | tf_op jit(solution)/shard_map/ppermute | solution.py:354
  39.5 6.8 %collective-permute-start.15 = (bf16[256,128]{1,0:T(8,128)(2,1)S(1)}, bf16[256,128]{1,0:T(8,128)(2,1)S(1)}, u32[]{:S(2)}, u32[]{:S(2)}) collective-permute-start(bf16[256,128]{1,0:T(8,128)(2,1)S(1)} %convolution_convert_fusion.1), channel_id=1, source_target_pairs={{0,24},{2,26},{4,28},{6,30},{8,16},{10,18},{12,20},{14,22},{16,8},... | collective-permute-start | bytes 196616 | tf_op jit(solution)/shard_map/ppermute | solution.py:45
  43.1 5.3 %collective-permute-start.14 = (bf16[256,128]{1,0:T(8,128)(2,1)S(1)}, bf16[256,128]{1,0:T(8,128)(2,1)S(1)}, u32[]{:S(2)}, u32[]{:S(2)}) collective-permute-start(bf16[256,128]{1,0:T(8,128)(2,1)S(1)} %convolution_convert_fusion.1), channel_id=1, source_target_pairs={{0,16},{2,18},{4,20},{6,22},{8,24},{10,26},{12,28},{14,30},{16,0},... | collective-permute-start | bytes 196616 | tf_op jit(solution)/shard_map/ppermute | solution.py:45
  43.1 5.7 %collective-permute-start.13 = (bf16[256,128]{1,0:T(8,128)(2,1)S(1)}, bf16[256,128]{1,0:T(8,128)(2,1)S(1)}, u32[]{:S(2)}, u32[]{:S(2)}) collective-permute-start(bf16[256,128]{1,0:T(8,128)(2,1)S(1)} %convolution_convert_fusion.1), channel_id=1, source_target_pairs={{0,8},{2,10},{4,12},{6,14},{8,0},{10,2},{12,4},{14,6},{16,24},{18,... | collective-permute-start | bytes 196616 | tf_op jit(solution)/shard_map/ppermute | solution.py:45
  48.8 10.2 %collective-permute-start.18 = (bf16[256,512]{1,0:T(8,128)(2,1)S(1)}, bf16[256,512]{1,0:T(8,128)(2,1)S(1)}, u32[]{:S(2)}, u32[]{:S(2)}) collective-permute-start(bf16[256,512]{1,0:T(8,128)(2,1)S(1)} %pad_maximum_fusion.1.refs_0_), channel_id=1, source_target_pairs={{0,6},{2,4},{4,2},{6,0},{8,14},{10,12},{12,10},{14,8},{16,22},{18,... | collective-permute-start | bytes 786440 | tf_op jit(solution)/shard_map/ppermute | solution.py:45
  50.5 12.2 %collective-permute-start.17 = (bf16[256,512]{1,0:T(8,128)(2,1)S(1)}, bf16[256,512]{1,0:T(8,128)(2,1)S(1)}, u32[]{:S(2)}, u32[]{:S(2)}) collective-permute-start(bf16[256,512]{1,0:T(8,128)(2,1)S(1)} %pad_maximum_fusion.1.refs_0_), channel_id=1, source_target_pairs={{0,4},{2,6},{4,0},{6,2},{8,12},{10,14},{12,8},{14,10},{16,20},{18,... | collective-permute-start | bytes 786440 | tf_op jit(solution)/shard_map/ppermute | solution.py:45
  51.8 10.9 %collective-permute-start.16 = (bf16[256,512]{1,0:T(8,128)(2,1)S(1)}, bf16[256,512]{1,0:T(8,128)(2,1)S(1)}, u32[]{:S(2)}, u32[]{:S(2)}) collective-permute-start(bf16[256,512]{1,0:T(8,128)(2,1)S(1)} %pad_maximum_fusion.1.refs_0_), channel_id=1, source_target_pairs={{0,2},{2,0},{4,6},{6,4},{8,10},{10,8},{12,14},{14,12},{16,18},{18,... | collective-permute-start | bytes 786440 | tf_op jit(solution)/shard_map/ppermute | solution.py:45

commit v4 on v3

--- a/solution.py
+++ b/solution.py
@@ -8,7 +8,7 @@
 from jax.sharding import PartitionSpec as P
 
 TILE = 256
-BLOCK = 64
+BLOCK = 128
 STEP = 8
 HIGHEST = lax.Precision.HIGHEST
 
@@ -64,13 +64,20 @@
     low = [[None] * STEP for _ in range(STEP)]
     inv = [[None] * STEP for _ in range(STEP)]
     pivots, recips = [], []
-    for t in range(STEP):
-        pivots.append(d[t][t])
-        recips.append(1.0 / d[t][t])
-        for r in range(t + 1, STEP):
-            low[r][t] = d[r][t] * recips[t]
-            for s in range(t + 1, r + 1):
-                d[r][s] = d[r][s] - low[r][t] * d[s][t]
+    for t in range(0, STEP, 2):
+        a, b, c = d[t][t], d[t + 1][t], d[t + 1][t + 1]
+        det = a * c - b * b
+        recip_a, recip_det = 1.0 / a, 1.0 / det
+        pivots += [a, det * recip_a]
+        recips += [recip_a, a * recip_det]
+        low[t + 1][t] = b * recip_a
+        for r in range(t + 2, STEP):
+            u, v = d[r][t], d[r][t + 1]
+            x, y = c * u - b * v, a * v - b * u
+            low[r][t] = u * recip_a
+            low[r][t + 1] = y * recip_det
+            for s in range(t + 2, r + 1):
+                d[r][s] = d[r][s] - (x * d[s][t] + y * d[s][t + 1]) * recip_det
     for s in range(STEP):
         for r in range(s + 1, STEP):
             total = -low[r][s]
@@ -80,23 +87,20 @@
     return pivots, recips, inv
 
 
-def block_inverse(recips, inv):
-    scaled = [[inv[r][s] * recips[r] for s in range(r)] + [recips[r]] for r in range(STEP)]
-    out = [[None] * STEP for _ in range(STEP)]
-    for s in range(STEP):
-        for t in range(s + 1):
-            total = scaled[s][t]
-            for r in range(s + 1, STEP):
-                total = total + inv[r][s] * scaled[r][t]
-            out[s][t] = out[t][s] = total
+def pick(value, index):
+    where = jnp.full((STEP, 128), index, jnp.int32)
+    return jnp.take_along_axis(value, where, axis=1, mode="promise_in_bounds")
+
+
+def stack(sub, values):
+    out = values[0]
+    for i in range(1, STEP):
+        out = jnp.where(sub == i, values[i], out)
     return out
 
 
 def weighted(weights, rows):
-    total = weights[0] * rows[0]
-    for weight, row in zip(weights[1:], rows[1:]):
-        total = total + weight * row
-    return total
+    return tree_sum([weight * row for weight, row in zip(weights, rows)])
 
 
 def factor_rows(work, factor_ref, inverse_t_ref, base):
@@ -113,44 +117,39 @@
         j = base + STEP * g
         home, first = divmod(j, 128)
         columns = [
-            [spread(rows[i][home][:, first + s : first + s + 1]) for s in steps]
+            [pick(rows[i][home], first + s) for s in steps]
             for i in range(g, count)
         ]
         block = [[spread(columns[0][s][r : r + 1, :]) for s in range(r + 1)] for r in steps]
         pivots, recips, inv = pivot_block(block)
         own = [[spread(rows[g][h][t : t + 1, :]) for t in steps] for h in halves]
 
-        roots = [lax.rsqrt(pivot) for pivot in pivots]
-        scaled_inv = []
-        for s in steps:
-            column = jnp.where(sub == s, roots[s], 0.0)
-            for t in range(s + 1, STEP):
-                column = jnp.where(sub == t, inv[t][s] * roots[t], column)
-            scaled_inv.append(column)
+        down = [stack(sub, [inv[t][s] if t > s else float(t == s) for t in steps]) for s in steps]
+        across = [stack(sub, [inv[r][s] if r > s else float(r == s) for s in steps]) for r in steps]
+        root = lax.rsqrt(stack(sub, pivots))
         corner = jnp.zeros((STEP, 128), jnp.float32)
         for s in steps:
-            corner = jnp.where(lane == first + s, scaled_inv[s], corner)
+            corner = jnp.where(lane == first + s, down[s], corner)
+        solved = [weighted(down, own[h]) for h in halves]
         for h in halves:
-            scaled = weighted(scaled_inv, own[h])
             col = lane + 128 * h
             place = (slice(j, j + STEP), slice(128 * h, 128 * (h + 1)))
-            factor_ref[place] = jnp.where(col >= j + sub, scaled, 0.0)
-            inverse_t_ref[place] = jnp.where(col < j, scaled, corner if h == home else 0.0)
+            edge = corner * root if h == home else 0.0
+            factor_ref[place] = jnp.where(col >= j + sub, solved[h] * root, 0.0)
+            inverse_t_ref[place] = jnp.where(col < j, solved[h] * root, edge)
 
         if g + 1 < count:
-            solve = block_inverse(recips, inv)
-            pulls = []
+            inside = (lane >= first) & (lane < first + STEP)
+            unit = jnp.where(lane == first + sub, 1.0, 0.0)
+            across = [across[r] * recips[r] for r in steps]
             for h in halves:
-                pulls.append([weighted(solve[s], own[h]) for s in steps])
+                full = jnp.where(inside, corner, solved[h]) if h == home else solved[h]
+                pull = weighted(across, [spread(full[t : t + 1, :]) for t in steps])
                 if h == home:
-                    for s in steps:
-                        for t in steps:
-                            entry = solve[s][t] + 1.0 if s == t else solve[s][t]
-                            pulls[h][s] = jnp.where(lane == first + t, entry, pulls[h][s])
-            for i in range(g + 1, count):
-                for h in halves:
-                    for s in steps:
-                        rows[i][h] = rows[i][h] - columns[i - g][s] * pulls[h][s]
+                    pull = pull + unit
+                pulls = [spread(pull[s : s + 1, :]) for s in steps]
+                for i in range(g + 1, count):
+                    rows[i][h] = rows[i][h] - weighted(columns[i - g], pulls)
 
 
 def factor_kernel(own_ref, other_ref, factor_ref, inverse_t_ref, work):
@@ -278,53 +277,135 @@
     )(turned, *tiles)
 
 
-def update_kernel(near, far, basis_ref, masked_ref, *refs):
-    slots, (coupling_ref, updated_ref) = refs[:near], refs[near:]
+def chunk_kernel(near, mask_hbm, trailing_hbm, *refs):
+    outs, (mask, held, sems) = refs[:near], refs[near:]
+    index = lax.rem(lax.axis_index("row"), near)
+    rows, width = outs[0].shape
+    first = pltpu.make_async_copy(mask_hbm, mask, sems.at[near])
+    first.start()
+    copies = []
+    for k in [*range(1, near), 0]:
+        cols = pl.ds(pl.multiple_of((index ^ k) * width, width), width)
+        copies.append(pltpu.make_async_copy(trailing_hbm.at[:, cols], held.at[k], sems.at[k]))
+        copies[-1].start()
+    first.wait()
+    for k, copy in zip([*range(1, near), 0], copies):
+        copy.wait()
+        for i in range(rows // TILE):
+            for j in range(width // TILE):
+                place = (slice(i * TILE, (i + 1) * TILE), slice(j * TILE, (j + 1) * TILE))
+                tile = held[(k, *place)]
+                present = mask[i, (index ^ k) * (width // TILE) + j] != 0
+                outs[k][place] = jnp.where(present, tile, jnp.zeros_like(tile))
+
+
+def masked_chunks(groups, trailing, tile_mask):
+    rows, cols = trailing.shape
+    width = cols // groups.near
+    out = jax.ShapeDtypeStruct((rows, width), trailing.dtype)
+    return pl.pallas_call(
+        functools.partial(chunk_kernel, groups.near),
+        out_shape=[out] * groups.near,
+        in_specs=[pl.BlockSpec(memory_space=pltpu.HBM)] * 2,
+        out_specs=[VMEM] * groups.near,
+        scratch_shapes=[
+            pltpu.SMEM(tile_mask.shape, tile_mask.dtype),
+            pltpu.VMEM((groups.near, rows, width), trailing.dtype),
+            pltpu.SemaphoreType.DMA((groups.near + 1,)),
+        ],
+        compiler_params=PARAMS,
+        name="chunks",
+    )(
+        pltpu.with_memory_space_constraint(tile_mask, pltpu.HBM),
+        pltpu.with_memory_space_constraint(trailing, pltpu.HBM),
+    )
+
+
+def update_kernel(near, far, basis_ref, *refs):
+    chunks, firsts, rests = refs[:near], refs[near : 2 * near], refs[2 * near : 3 * near]
+    coupling_ref, updated_ref, work, sems = refs[3 * near :]
     index = lax.axis_index("row")
     near_index, far_index = lax.rem(index, near), lax.div(index, near)
-    basis = basis_ref[...]
-    width = slots[0].shape[1] // far
-    for i, slot in enumerate(slots):
-        removed = jnp.dot(basis, slot[...], preferred_element_type=jnp.float32)
+    width = firsts[0].shape[1]
+    copies = []
+
+    def send(source, target, cols):
+        copy = pltpu.make_async_copy(source, target.at[:, cols], sems.at[len(copies)])
+        copy.start()
+        copies.append(copy)
+
+    for i in range(near):
         for k in range(far):
+            source = firsts[i] if k == 0 else rests[i].at[:, (k - 1) * width : k * width]
             start = ((near_index ^ i) * far + (far_index ^ k)) * width
-            cols = pl.ds(pl.multiple_of(start, width), width)
-            part = slice(k * width, (k + 1) * width)
-            coupling_ref[:, cols] = slot[:, part]
-            left = masked_ref[:, cols].astype(jnp.float32) - removed[:, part]
-            updated_ref[:, cols] = left.astype(updated_ref.dtype)
-
-
-def update(groups, basis, masked, slots):
+            send(source, coupling_ref, pl.ds(pl.multiple_of(start, width), width))
+    for i in range(near):
+        for part in (firsts, rests):
+            removed = jnp.dot(basis_ref[...], part[i][...], preferred_element_type=jnp.float32)
+            for k in range(part[i].shape[1] // width):
+                slot = k if part is firsts else k + 1
+                inner = (far_index ^ slot) * width
+                left = chunks[i][:, pl.ds(pl.multiple_of(inner, width), width)]
+                place = (i * far + slot) * width
+                result = left.astype(jnp.float32) - removed[:, k * width : (k + 1) * width]
+                work[:, place : place + width] = result.astype(work.dtype)
+                start = (near_index ^ i) * far * width + inner
+                cols = pl.ds(pl.multiple_of(start, width), width)
+                send(work.at[:, place : place + width], updated_ref, cols)
+    for copy in copies:
+        copy.wait()
+
+
+def update(groups, basis, chunks, firsts, rests):
     near, far = groups.near, groups.far
-    rows, cols = masked.shape
-    width = slots[0].shape[1] // far
-    if width % 128:
-        coupling = jnp.zeros((slots[0].shape[0], cols), slots[0].dtype)
-        for i, slot in enumerate(slots):
-            for k in range(far):
-                start = ((groups.near_index() ^ i) * far + (groups.far_index() ^ k)) * width
-                part = slot[:, k * width : (k + 1) * width]
-                coupling = lax.dynamic_update_slice_in_dim(coupling, part, start, 1)
-        removed = jnp.dot(basis, coupling, preferred_element_type=jnp.float32)
-        return coupling, (masked.astype(jnp.float32) - removed).astype(masked.dtype)
+    rows, width = chunks[0].shape
+    cols = width * near
+    dtype = chunks[0].dtype
+    if (width // far) % 128:
+        return update_plain(groups, basis, chunks, firsts, rests)
+    hbm = pl.BlockSpec(memory_space=pltpu.HBM)
     return pl.pallas_call(
         functools.partial(update_kernel, near, far),
         out_shape=[
-            jax.ShapeDtypeStruct((slots[0].shape[0], cols), slots[0].dtype),
-            jax.ShapeDtypeStruct((rows, cols), masked.dtype),
+            jax.ShapeDtypeStruct((firsts[0].shape[0], cols), dtype),
+            jax.ShapeDtypeStruct((rows, cols), dtype),
         ],
-        in_specs=[VMEM] * (2 + near),
-        out_specs=[VMEM] * 2,
+        in_specs=[VMEM] * (1 + 3 * near),
+        out_specs=[hbm] * 2,
+        scratch_shapes=[
+            pltpu.VMEM((rows, cols), dtype),
+            pltpu.SemaphoreType.DMA((2 * near * far,)),
+        ],
         compiler_params=PARAMS,
         name="update",
-    )(basis, masked, *slots)
+    )(basis, *chunks, *firsts, *rests)
+
+
+def update_plain(groups, basis, chunks, firsts, rests):
+    near, far = groups.near, groups.far
+    rows, chunk = chunks[0].shape
+    width = firsts[0].shape[1]
+    coupling = jnp.zeros((firsts[0].shape[0], chunk * near), firsts[0].dtype)
+    masked = jnp.zeros((rows, chunk * near), chunks[0].dtype)
+    for i in range(near):
+        base = (groups.near_index() ^ i) * chunk
+        masked = lax.dynamic_update_slice_in_dim(masked, chunks[i], base, 1)
+        slot = jnp.concatenate([firsts[i], rests[i]], axis=1)
+        for k in range(far):
+            start = base + (groups.far_index() ^ k) * width
+            part = slot[:, k * width : (k + 1) * width]
+            coupling = lax.dynamic_update_slice_in_dim(coupling, part, start, 1)
+    removed = jnp.dot(basis, coupling, preferred_element_type=jnp.float32)
+    return coupling, (masked.astype(jnp.float32) - removed).astype(masked.dtype)
 
 
 def gather_slots(groups, shard):
-    far = range(1, groups.far)
-    wide = jnp.concatenate([shard] + [groups.far_swap(shard, k) for k in far], axis=1)
-    return [wide] + [groups.near_swap(wide, k) for k in range(1, groups.near)]
+    near = range(1, groups.near)
+    rest = [groups.far_swap(shard, k) for k in range(1, groups.far)]
+    rest[1], later = lax.optimization_barrier((rest[1], shard))
+    firsts = [shard] + [groups.near_swap(later, k) for k in near]
+    rest = jnp.concatenate(rest, axis=1)
+    return firsts, [rest] + [groups.near_swap(rest, k) for k in near]
 
 
 def local(groups, panel, trailing, tile_mask):
@@ -334,18 +415,8 @@
     )
     gathered = lax.all_gather(stacked, "col", axis=1, tiled=True)
 
-    local_rows = trailing.shape[0]
-    local_cols = trailing.shape[1]
-    tiles = trailing.reshape(local_rows // TILE, TILE, local_cols // TILE, TILE)
-    masked = (tiles * tile_mask.astype(jnp.bfloat16)[:, None, :, None]).reshape(
-        local_rows, local_cols
-    )
-    chunk = local_cols // near
-    chunks = [
-        lax.dynamic_slice_in_dim(masked, (groups.near_index() ^ k) * chunk, chunk, 1)
-        for k in range(near)
-    ]
-    chunks = chunks[:1] + [groups.near_swap(chunks[k], k) for k in range(1, near)]
+    chunks = masked_chunks(groups, trailing, tile_mask)
+    tiles = [chunks[0]] + [groups.near_swap(chunks[k], k) for k in range(1, near)]
 
     gram_terms, turned = gram_part(near, gathered)
     gram_own = tree_sum(
@@ -353,18 +424,19 @@
     )
     gram_other = lax.ppermute(gram_own, "col", [(i, i ^ 1) for i in range(groups.cols)])
 
-    cross_terms = cross_part(groups, turned, chunks)
+    cross_terms = cross_part(groups, turned, tiles)
     summed = tree_sum(
         [cross_terms[0]] + [groups.far_swap(cross_terms[k], k) for k in range(1, far)]
     )
 
     upper_factor, inverse_t = cholesky_pair(gram_own, gram_other)
     shard = jnp.dot(inverse_t, summed, precision=HIGHEST).astype(jnp.bfloat16)
-    slots = gather_slots(groups, shard)
+    firsts, rests = gather_slots(groups, shard)
+    rows = gathered[: panel.shape[0], :].astype(jnp.float32)
     basis = lax.dot_general(
-        gathered[: panel.shape[0], :].astype(jnp.float32), inverse_t, (((1,), (1,)), ((), ())), precision=HIGHEST
+        rows, inverse_t, (((1,), (1,)), ((), ())), precision=HIGHEST
     ).astype(jnp.bfloat16)
-    coupling, updated = update(groups, basis, masked, slots)
+    coupling, updated = update(groups, basis, chunks, firsts, rests)
     return (upper_factor, coupling, updated)
 
 

time: 65.2 us -> 58.6 us (0.90)
  waiting for transfers between devices: 18.2 us -> 14.9 us
  Pallas kernels: 14.2 us -> 11.1 us
  starting transfers between devices: 26.8 us -> 28.8 us
  other arithmetic: 1.37 us -> 0.04 us
  local copies, waits for them, and re-layouts: 0.86 us -> 0.05 us
    pallas_call x1, Pallas kernels: 11 us -> 7.31 us  [cholesky_pair(): pl.pallas_call(factor_kernel, out_shape=[out, out], in_specs=[VMEM] * 2,...]
    ppermute x18 -> x21, waiting for transfers between devices: 17 us -> 13.6 us  [swap(): lax.ppermute(value, 'row', [(i, i ^ offset) for i in range(self.rows)])]
    ppermute x18 -> x21, starting transfers between devices: 26.7 us -> 28.7 us  [swap(): lax.ppermute(value, 'row', [(i, i ^ offset) for i in range(self.rows)])]
    mul x2 -> x0, other arithmetic: 1.3 us -> none  [local(): tiles * tile_mask.astype(jnp.bfloat16)[:, None, :, None]]
    pallas_call x0 -> x1, Pallas kernels: none -> 1.25 us  [masked_chunks(): pl.pallas_call(functools.partial(chunk_kernel, groups.near), out_shape=[o...]
    unnamed x6 -> x4, local copies, waits for them, and re-layouts: 0.74 us -> 0.04 us
  transfers between devices with their start and end apart: 19 -> 22, of which waited for: 7 -> 9; matrix products, arithmetic and copies ran while one was open for 3% -> 1% of each run, Pallas kernels for 18% -> 16%
where the time goes in v4:
time: 58.6 us; the launch traced here: 58.5 us
  starting transfers between devices  28.8 us (49%)
  waiting for transfers between devices  14.9 us (25%)
  Pallas kernels  11.1 us (19%)
  blocking collectives  2.18 us (4%)
  between operations  0.74 us (1%)
  matrix products  0.71 us (1%)
    ppermute x21, starting transfers between devices, swap(): lax.ppermute(value, 'row', [(i, i ^ offset) for i in range(self.rows)])  28.7 us
    ppermute x21, waiting for transfers between devices, swap(): lax.ppermute(value, 'row', [(i, i ^ offset) for i in range(self.rows)])  13.6 us
    pallas_call x1, Pallas kernels, cholesky_pair(): pl.pallas_call(factor_kernel, out_shape=[out, out], in_specs=[VMEM] * 2,...  7.31 us
    all_gather x1, blocking collectives, local(): gathered = lax.all_gather(stacked, 'col', axis=1, tiled=True)  2.18 us
    pallas_call x1, Pallas kernels, update(): pl.pallas_call(functools.partial(update_kernel, near, far), out_shape=[ja...  1.69 us
    pallas_call x1, Pallas kernels, masked_chunks(): pl.pallas_call(functools.partial(chunk_kernel, groups.near), out_shape=[o...  1.25 us
    ppermute x1, waiting for transfers between devices, local(): lax.ppermute(gram_own, 'col', [(i, i ^ 1) for i in range(groups.cols)])  1.25 us
  transfers between devices with their start and end apart: 22, of which 9 were waited for; matrix products, arithmetic and copies ran while one was open for 1% of the time, Pallas kernels for 16%

profile of v4, /device:TPU:0, one launch (start us, length us, event | category | flops | bytes accessed | tf_op | source)
XLA Modules:
  0.0 58.5 jit_solution(3002499970295942395)
XLA Ops:
  0.6 0.0 copy-start
  0.6 3.0 %collective-permute-start.1 = (bf16[256,128]{1,0:T(8,128)(2,1)}, bf16[256,128]{1,0:T(8,128)(2,1)S(1)}, u32[]{:S(2)}, u32[]{:S(2)}) collective-permute-start(bf16[256,128]{1,0:T(8,128)(2,1)} %param.3), channel_id=1, source_target_pairs={{0,4},{2,6},{4,0},{6,2},{8,12},{10,14},{12,8},{14,10},{16,20},{18,... | collective-permute-start | bytes 196616 | tf_op jit(solution)/shard_map/ppermute | solution.py:45
  3.7 1.5 %collective-permute-start = (bf16[256,128]{1,0:T(8,128)(2,1)}, bf16[256,128]{1,0:T(8,128)(2,1)S(1)}, u32[]{:S(2)}, u32[]{:S(2)}) collective-permute-start(bf16[256,128]{1,0:T(8,128)(2,1)} %param.3), channel_id=1, source_target_pairs={{0,2},{2,0},{4,6},{6,4},{8,10},{10,8},{12,14},{14,12},{16,18},{18,... | collective-permute-start | bytes 196616 | tf_op jit(solution)/shard_map/ppermute | solution.py:45
  5.2 0.0 collective-permute-start.2
  5.2 1.3 %chunks.1 = (bf16[256,512]{1,0:T(8,128)(2,1)S(1)}, bf16[256,512]{1,0:T(8,128)(2,1)S(1)}, bf16[256,512]{1,0:T(8,128)(2,1)S(1)}, bf16[256,512]{1,0:T(8,128)(2,1)S(1)}) custom-call(s32[1,8]{1,0:T(1,128)} %mask_hbm.1, bf16[256,2048]{1,0:T(8,128)(2,1)} %trailing_hbm.1), custom_call_target="tpu_custom_call" | custom-call | tf_op jit(solution)/shard_map/chunks/pallas_call | solution.py:306
  6.5 2.0 %collective-permute-start.7 = (bf16[256,512]{1,0:T(8,128)(2,1)S(1)}, bf16[256,512]{1,0:T(8,128)(2,1)S(1)}, u32[]{:S(2)}, u32[]{:S(2)}) collective-permute-start(bf16[256,512]{1,0:T(8,128)(2,1)S(1)} %get-tuple-element.23.refs_1_), channel_id=1, source_target_pairs={{0,2},{2,0},{4,6},{6,4},{8,10},{10,8},{12,14},{14,12},{16,18},{18,... | collective-permute-start | bytes 786440 | tf_op jit(solution)/shard_map/ppermute | solution.py:45
  8.5 1.5 %collective-permute-start.8 = (bf16[256,512]{1,0:T(8,128)(2,1)S(1)}, bf16[256,512]{1,0:T(8,128)(2,1)S(1)}, u32[]{:S(2)}, u32[]{:S(2)}) collective-permute-start(bf16[256,512]{1,0:T(8,128)(2,1)S(1)} %get-tuple-element.24.refs_2_), channel_id=1, source_target_pairs={{0,4},{2,6},{4,0},{6,2},{8,12},{10,14},{12,8},{14,10},{16,20},{18,... | collective-permute-start | bytes 786440 | tf_op jit(solution)/shard_map/ppermute | solution.py:45
  10.0 0.0 collective-permute-done.1
  10.0 0.0 collective-permute-start.9
  10.0 0.0 collective-permute-done
  10.0 1.2 %collective-permute-done.2 = bf16[256,128]{1,0:T(8,128)(2,1)S(1)} collective-permute-done((bf16[256,128]{1,0:T(8,128)(2,1)}, bf16[256,128]{1,0:T(8,128)(2,1)S(1)}, u32[]{:S(2)}, u32[]{:S(2)}) %collective-permute-start.2) | collective-permute-done | bytes 65568 | tf_op jit(solution)/shard_map/ppermute | solution.py:45
  11.2 0.0 copy-done
  11.3 2.2 %all_gather.3.panel_ref = bf16[1024,256]{1,0:T(8,128)(2,1)S(1)} all-gather(bf16[1024,128]{1,0:T(8,128)(2,1)S(1)} %pad_maximum_fusion), channel_id=1, replica_groups=mesh['row'=16,'col'=2] {'col'}, dimensions={1}, use_global_device_ids=true | all-gather | bytes 786432 | tf_op jit(solution)/shard_map/all_gather | solution.py:416
  13.5 0.4 gram_part.1
  13.8 3.7 %collective-permute-start.5 = (f32[136,128]{1,0:T(8,128)S(1)}, f32[136,128]{1,0:T(8,128)S(1)}, u32[]{:S(2)}, u32[]{:S(2)}) collective-permute-start(f32[136,128]{1,0:T(8,128)S(1)} %get-tuple-element.19), channel_id=1, source_target_pairs={{0,24},{2,26},{4,28},{6,30},{8,16},{10,18},{12,20},{14,22},{16,8},... | collective-permute-start | bytes 208904 | tf_op jit(solution)/shard_map/ppermute | solution.py:45
  17.5 0.0 collective-permute-start.4
  17.5 0.0 collective-permute-done.7.refs_1_
  17.5 0.8 %collective-permute-start.3 = (f32[136,128]{1,0:T(8,128)S(1)}, f32[136,128]{1,0:T(8,128)S(1)}, u32[]{:S(2)}, u32[]{:S(2)}) collective-permute-start(f32[136,128]{1,0:T(8,128)S(1)} %get-tuple-element.19), channel_id=1, source_target_pairs={{0,8},{2,10},{4,12},{6,14},{8,0},{10,2},{12,4},{14,6},{16,24},{18,... | collective-permute-start | bytes 208904 | tf_op jit(solution)/shard_map/ppermute | solution.py:45
  18.3 3.4 %collective-permute-done.8.refs_2_ = bf16[256,512]{1,0:T(8,128)(2,1)S(1)} collective-permute-done((bf16[256,512]{1,0:T(8,128)(2,1)S(1)}, bf16[256,512]{1,0:T(8,128)(2,1)S(1)}, u32[]{:S(2)}, u32[]{:S(2)}) %collective-permute-start.8) | collective-permute-done | bytes 262176 | tf_op jit(solution)/shard_map/ppermute | solution.py:45
  21.7 0.0 collective-permute-done.9.refs_3_
  21.7 0.5 cross_part.1
  22.2 1.6 %collective-permute-start.10 = (f32[256,128]{1,0:T(8,128)S(1)}, f32[256,128]{1,0:T(8,128)S(1)}, u32[]{:S(2)}, u32[]{:S(2)}) collective-permute-start(f32[256,128]{1,0:T(8,128)S(1)} %get-tuple-element.28), channel_id=1, source_target_pairs={{0,8},{2,10},{4,12},{6,14},{8,0},{10,2},{12,4},{14,6},{16,24},{18,... | collective-permute-start | bytes 393224 | tf_op jit(solution)/shard_map/ppermute | solution.py:45
  23.9 2.6 %collective-permute-start.11 = (f32[256,128]{1,0:T(8,128)S(1)}, f32[256,128]{1,0:T(8,128)S(1)}, u32[]{:S(2)}, u32[]{:S(2)}) collective-permute-start(f32[256,128]{1,0:T(8,128)S(1)} %get-tuple-element.29), channel_id=1, source_target_pairs={{0,16},{2,18},{4,20},{6,22},{8,24},{10,26},{12,28},{14,30},{16,0},... | collective-permute-start | bytes 393224 | tf_op jit(solution)/shard_map/ppermute | solution.py:45
  26.5 0.0 collective-permute-done.5
  26.5 0.2 collective-permute-start.12
  26.7 0.0 collective-permute-done.4
  26.7 0.0 collective-permute-done.3
  26.7 0.1 collective-permute-start.6
  26.8 1.2 %collective-permute-done.6.other_ref = f32[136,128]{1,0:T(8,128)S(1)} collective-permute-done((f32[136,128]{1,0:T(8,128)S(1)}, f32[136,128]{1,0:T(8,128)S(1)}, u32[]{:S(2)}, u32[]{:S(2)}) %collective-permute-start.6) | collective-permute-done | bytes 69664 | tf_op jit(solution)/shard_map/ppermute | solution.py:425
  28.0 7.3 %factor.1 = (f32[256,256]{1,0:T(8,128)}, f32[256,256]{1,0:T(8,128)S(1)}) custom-call(f32[136,128]{1,0:T(8,128)S(1)} %add_add_fusion.own_ref, f32[136,128]{1,0:T(8,128)S(1)} %collective-permute-done.6.other_ref), custom_call_target="tpu_custom_call" | custom-call | flops 134217728 | bytes 3145728 | tf_op jit(solution)/shard_map/factor/pallas_call | solution.py:191
  35.3 0.0 collective-permute-done.10
  35.3 0.1 collective-permute-done.11
  35.5 0.0 collective-permute-done.12
  35.5 0.4 convolution_convert_fusion.1.refs_4_
  35.9 3.1 %collective-permute-start.13 = (bf16[256,128]{1,0:T(8,128)(2,1)S(1)}, bf16[256,128]{1,0:T(8,128)(2,1)S(1)}, u32[]{:S(2)}, u32[]{:S(2)}) collective-permute-start(bf16[256,128]{1,0:T(8,128)(2,1)S(1)} %convolution_convert_fusion.1.refs_4_), channel_id=1, source_target_pairs={{0,16},{2,18},{4,20},{6,22},{8,24},{10,26},{12,28},{14,30},{16,0},... | collective-permute-start | bytes 196616 | tf_op jit(solution)/shard_map/ppermute | solution.py:45
  38.9 1.0 %collective-permute-start.17 = (bf16[256,128]{1,0:T(8,128)(2,1)S(1)}, bf16[256,128]{1,0:T(8,128)(2,1)S(1)}, u32[]{:S(2)}, u32[]{:S(2)}) collective-permute-start(bf16[256,128]{1,0:T(8,128)(2,1)S(1)} %convolution_convert_fusion.1.refs_4_), channel_id=1, source_target_pairs={{0,8},{2,10},{4,12},{6,14},{8,0},{10,2},{12,4},{14,6},{16,24},{18,... | collective-permute-start | bytes 196616 | tf_op jit(solution)/shard_map/ppermute | solution.py:45
  40.0 0.5 collective-permute-start.18
  40.5 1.4 %collective-permute-done.13 = bf16[256,128]{1,0:T(8,128)(2,1)S(1)} collective-permute-done((bf16[256,128]{1,0:T(8,128)(2,1)S(1)}, bf16[256,128]{1,0:T(8,128)(2,1)S(1)}, u32[]{:S(2)}, u32[]{:S(2)}) %collective-permute-start.13) | collective-permute-done | bytes 65568 | tf_op jit(solution)/shard_map/ppermute | solution.py:45
  41.9 0.8 %collective-permute-start.16 = (bf16[256,128]{1,0:T(8,128)(2,1)S(1)}, bf16[256,128]{1,0:T(8,128)(2,1)S(1)}, u32[]{:S(2)}, u32[]{:S(2)}) collective-permute-start(bf16[256,128]{1,0:T(8,128)(2,1)S(1)} %convolution_convert_fusion.1.refs_4_), channel_id=1, source_target_pairs={{0,6},{2,4},{4,2},{6,0},{8,14},{10,12},{12,10},{14,8},{16,22},{18,... | collective-permute-start | bytes 196616 | tf_op jit(solution)/shard_map/ppermute | solution.py:45
  42.7 1.3 %collective-permute-start.15 = (bf16[256,128]{1,0:T(8,128)(2,1)S(1)}, bf16[256,128]{1,0:T(8,128)(2,1)S(1)}, u32[]{:S(2)}, u32[]{:S(2)}) collective-permute-start(bf16[256,128]{1,0:T(8,128)(2,1)S(1)} %convolution_convert_fusion.1.refs_4_), channel_id=1, source_target_pairs={{0,4},{2,6},{4,0},{6,2},{8,12},{10,14},{12,8},{14,10},{16,20},{18,... | collective-permute-start | bytes 196616 | tf_op jit(solution)/shard_map/ppermute | solution.py:45
  44.0 1.4 %collective-permute-start.14 = (bf16[256,128]{1,0:T(8,128)(2,1)S(1)}, bf16[256,128]{1,0:T(8,128)(2,1)S(1)}, u32[]{:S(2)}, u32[]{:S(2)}) collective-permute-start(bf16[256,128]{1,0:T(8,128)(2,1)S(1)} %convolution_convert_fusion.1.refs_4_), channel_id=1, source_target_pairs={{0,2},{2,0},{4,6},{6,4},{8,10},{10,8},{12,14},{14,12},{16,18},{18,... | collective-permute-start | bytes 196616 | tf_op jit(solution)/shard_map/ppermute | solution.py:45
  45.4 0.0 collective-permute-done.17
  45.5 0.6 %collective-permute-done.18 = bf16[256,128]{1,0:T(8,128)(2,1)S(1)} collective-permute-done((bf16[256,128]{1,0:T(8,128)(2,1)S(1)}, bf16[256,128]{1,0:T(8,128)(2,1)S(1)}, u32[]{:S(2)}, u32[]{:S(2)}) %collective-permute-start.18) | collective-permute-done | bytes 65568 | tf_op jit(solution)/shard_map/ppermute | solution.py:45
  46.1 1.0 %collective-permute-start.21 = (bf16[256,384]{1,0:T(8,128)(2,1)S(1)}, bf16[256,384]{1,0:T(8,128)(2,1)S(1)}, u32[]{:S(2)}, u32[]{:S(2)}) collective-permute-start(bf16[256,384]{1,0:T(8,128)(2,1)S(1)} %constant_dynamic-update-slice_fusion.refs_8_), channel_id=1, source_target_pairs={{0,6},{2,4},{4,2},{6,0},{8,14},{10,12},{12,10},{14,8},{16,22},{18,... | collective-permute-start | bytes 589832 | tf_op jit(solution)/shard_map/ppermute | solution.py:45
  47.0 1.1 %collective-permute-start.20 = (bf16[256,384]{1,0:T(8,128)(2,1)S(1)}, bf16[256,384]{1,0:T(8,128)(2,1)S(1)}, u32[]{:S(2)}, u32[]{:S(2)}) collective-permute-start(bf16[256,384]{1,0:T(8,128)(2,1)S(1)} %constant_dynamic-update-slice_fusion.refs_8_), channel_id=1, source_target_pairs={{0,4},{2,6},{4,0},{6,2},{8,12},{10,14},{12,8},{14,10},{16,20},{18,... | collective-permute-start | bytes 589832 | tf_op jit(solution)/shard_map/ppermute | solution.py:45
  48.2 0.0 collective-permute-done.16.refs_7_
  48.2 1.5 %collective-permute-start.19 = (bf16[256,384]{1,0:T(8,128)(2,1)S(1)}, bf16[256,384]{1,0:T(8,128)(2,1)S(1)}, u32[]{:S(2)}, u32[]{:S(2)}) collective-permute-start(bf16[256,384]{1,0:T(8,128)(2,1)S(1)} %constant_dynamic-update-slice_fusion.refs_8_), channel_id=1, source_target_pairs={{0,2},{2,0},{4,6},{6,4},{8,10},{10,8},{12,14},{14,12},{16,18},{18,... | collective-permute-start | bytes 589832 | tf_op jit(solution)/shard_map/ppermute | solution.py:45
  49.7 0.3 convolution_convert_fusion.basis_ref
  50.0 0.0 collective-permute-done.15.refs_6_
  50.0 0.0 collective-permute-done.14.refs_5_
  50.0 4.8 %collective-permute-done.21.refs_11_ = bf16[256,384]{1,0:T(8,128)(2,1)S(1)} collective-permute-done((bf16[256,384]{1,0:T(8,128)(2,1)S(1)}, bf16[256,384]{1,0:T(8,128)(2,1)S(1)}, u32[]{:S(2)}, u32[]{:S(2)}) %collective-permute-start.21) | collective-permute-done | bytes 196640 | tf_op jit(solution)/shard_map/ppermute | solution.py:45
  54.8 1.5 %collective-permute-done.20.refs_10_ = bf16[256,384]{1,0:T(8,128)(2,1)S(1)} collective-permute-done((bf16[256,384]{1,0:T(8,128)(2,1)S(1)}, bf16[256,384]{1,0:T(8,128)(2,1)S(1)}, u32[]{:S(2)}, u32[]{:S(2)}) %collective-permute-start.20) | collective-permute-done | bytes 196640 | tf_op jit(solution)/shard_map/ppermute | solution.py:45
  56.3 0.4 collective-permute-done.19.refs_9_
  56.8 1.7 %update.1 = (bf16[256,2048]{1,0:T(8,128)(2,1)}, bf16[256,2048]{1,0:T(8,128)(2,1)}) custom-call(bf16[256,256]{1,0:T(8,128)(2,1)S(1)} %convolution_convert_fusion.basis_ref, bf16[256,512]{1,0:T(8,128)(2,1)S(1)} %get-tuple-element.22.refs_0_, bf16[256,512]{1,0:T(8,128)(2,1)S(1)} %get-tuple-element.23.refs_1_, bf16[256,512]{1,0:T(8,128)(2,1)S(1)} %get-tuple-element.24.refs_2_, ...), custom_call_target="tpu_custom_call" | custom-call | tf_op jit(solution)/shard_map/update/pallas_call | solution.py:367
  (5 shorter events, 0.1 us)
Async XLA Ops:
  0.6 10.6 %copy-start = (bf16[256,128]{1,0:T(8,128)(2,1)S(1)}, bf16[256,128]{1,0:T(8,128)(2,1)}, u32[]{:S(2)}) copy-start(bf16[256,128]{1,0:T(8,128)(2,1)} %param.3) | copy-start | bytes 196612
  0.6 9.3 %collective-permute-start.1 = (bf16[256,128]{1,0:T(8,128)(2,1)}, bf16[256,128]{1,0:T(8,128)(2,1)S(1)}, u32[]{:S(2)}, u32[]{:S(2)}) collective-permute-start(bf16[256,128]{1,0:T(8,128)(2,1)} %param.3), channel_id=1, source_target_pairs={{0,4},{2,6},{4,0},{6,2},{8,12},{10,14},{12,8},{14,10},{16,20},{18,... | collective-permute-start | bytes 196616 | tf_op jit(solution)/shard_map/ppermute | solution.py:45
  3.7 6.4 %collective-permute-start = (bf16[256,128]{1,0:T(8,128)(2,1)}, bf16[256,128]{1,0:T(8,128)(2,1)S(1)}, u32[]{:S(2)}, u32[]{:S(2)}) collective-permute-start(bf16[256,128]{1,0:T(8,128)(2,1)} %param.3), channel_id=1, source_target_pairs={{0,2},{2,0},{4,6},{6,4},{8,10},{10,8},{12,14},{14,12},{16,18},{18,... | collective-permute-start | bytes 196616 | tf_op jit(solution)/shard_map/ppermute | solution.py:45
  5.2 6.1 %collective-permute-start.2 = (bf16[256,128]{1,0:T(8,128)(2,1)}, bf16[256,128]{1,0:T(8,128)(2,1)S(1)}, u32[]{:S(2)}, u32[]{:S(2)}) collective-permute-start(bf16[256,128]{1,0:T(8,128)(2,1)} %param.3), channel_id=1, source_target_pairs={{0,6},{2,4},{4,2},{6,0},{8,14},{10,12},{12,10},{14,8},{16,22},{18,... | collective-permute-start | bytes 196616 | tf_op jit(solution)/shard_map/ppermute | solution.py:45
  6.5 11.0 %collective-permute-start.7 = (bf16[256,512]{1,0:T(8,128)(2,1)S(1)}, bf16[256,512]{1,0:T(8,128)(2,1)S(1)}, u32[]{:S(2)}, u32[]{:S(2)}) collective-permute-start(bf16[256,512]{1,0:T(8,128)(2,1)S(1)} %get-tuple-element.23.refs_1_), channel_id=1, source_target_pairs={{0,2},{2,0},{4,6},{6,4},{8,10},{10,8},{12,14},{14,12},{16,18},{18,... | collective-permute-start | bytes 786440 | tf_op jit(solution)/shard_map/ppermute | solution.py:45
  8.5 13.2 %collective-permute-start.8 = (bf16[256,512]{1,0:T(8,128)(2,1)S(1)}, bf16[256,512]{1,0:T(8,128)(2,1)S(1)}, u32[]{:S(2)}, u32[]{:S(2)}) collective-permute-start(bf16[256,512]{1,0:T(8,128)(2,1)S(1)} %get-tuple-element.24.refs_2_), channel_id=1, source_target_pairs={{0,4},{2,6},{4,0},{6,2},{8,12},{10,14},{12,8},{14,10},{16,20},{18,... | collective-permute-start | bytes 786440 | tf_op jit(solution)/shard_map/ppermute | solution.py:45
  10.0 11.7 %collective-permute-start.9 = (bf16[256,512]{1,0:T(8,128)(2,1)S(1)}, bf16[256,512]{1,0:T(8,128)(2,1)S(1)}, u32[]{:S(2)}, u32[]{:S(2)}) collective-permute-start(bf16[256,512]{1,0:T(8,128)(2,1)S(1)} %get-tuple-element.25.refs_3_), channel_id=1, source_target_pairs={{0,6},{2,4},{4,2},{6,0},{8,14},{10,12},{12,10},{14,8},{16,22},{18,... | collective-permute-start | bytes 786440 | tf_op jit(solution)/shard_map/ppermute | solution.py:45
  13.8 12.6 %collective-permute-start.5 = (f32[136,128]{1,0:T(8,128)S(1)}, f32[136,128]{1,0:T(8,128)S(1)}, u32[]{:S(2)}, u32[]{:S(2)}) collective-permute-start(f32[136,128]{1,0:T(8,128)S(1)} %get-tuple-element.19), channel_id=1, source_target_pairs={{0,24},{2,26},{4,28},{6,30},{8,16},{10,18},{12,20},{14,22},{16,8},... | collective-permute-start | bytes 208904 | tf_op jit(solution)/shard_map/ppermute | solution.py:45
  17.5 9.2 %collective-permute-start.4 = (f32[136,128]{1,0:T(8,128)S(1)}, f32[136,128]{1,0:T(8,128)S(1)}, u32[]{:S(2)}, u32[]{:S(2)}) collective-permute-start(f32[136,128]{1,0:T(8,128)S(1)} %get-tuple-element.19), channel_id=1, source_target_pairs={{0,16},{2,18},{4,20},{6,22},{8,24},{10,26},{12,28},{14,30},{16,0},... | collective-permute-start | bytes 208904 | tf_op jit(solution)/shard_map/ppermute | solution.py:45
  17.5 9.2 %collective-permute-start.3 = (f32[136,128]{1,0:T(8,128)S(1)}, f32[136,128]{1,0:T(8,128)S(1)}, u32[]{:S(2)}, u32[]{:S(2)}) collective-permute-start(f32[136,128]{1,0:T(8,128)S(1)} %get-tuple-element.19), channel_id=1, source_target_pairs={{0,8},{2,10},{4,12},{6,14},{8,0},{10,2},{12,4},{14,6},{16,24},{18,... | collective-permute-start | bytes 208904 | tf_op jit(solution)/shard_map/ppermute | solution.py:45
  22.2 13.1 %collective-permute-start.10 = (f32[256,128]{1,0:T(8,128)S(1)}, f32[256,128]{1,0:T(8,128)S(1)}, u32[]{:S(2)}, u32[]{:S(2)}) collective-permute-start(f32[256,128]{1,0:T(8,128)S(1)} %get-tuple-element.28), channel_id=1, source_target_pairs={{0,8},{2,10},{4,12},{6,14},{8,0},{10,2},{12,4},{14,6},{16,24},{18,... | collective-permute-start | bytes 393224 | tf_op jit(solution)/shard_map/ppermute | solution.py:45
  23.9 11.6 %collective-permute-start.11 = (f32[256,128]{1,0:T(8,128)S(1)}, f32[256,128]{1,0:T(8,128)S(1)}, u32[]{:S(2)}, u32[]{:S(2)}) collective-permute-start(f32[256,128]{1,0:T(8,128)S(1)} %get-tuple-element.29), channel_id=1, source_target_pairs={{0,16},{2,18},{4,20},{6,22},{8,24},{10,26},{12,28},{14,30},{16,0},... | collective-permute-start | bytes 393224 | tf_op jit(solution)/shard_map/ppermute | solution.py:45
  26.5 9.0 %collective-permute-start.12 = (f32[256,128]{1,0:T(8,128)S(1)}, f32[256,128]{1,0:T(8,128)S(1)}, u32[]{:S(2)}, u32[]{:S(2)}) collective-permute-start(f32[256,128]{1,0:T(8,128)S(1)} %get-tuple-element.30), channel_id=1, source_target_pairs={{0,24},{2,26},{4,28},{6,30},{8,16},{10,18},{12,20},{14,22},{16,8},... | collective-permute-start | bytes 393224 | tf_op jit(solution)/shard_map/ppermute | solution.py:45
  26.7 1.3 %collective-permute-start.6 = (f32[136,128]{1,0:T(8,128)S(1)}, f32[136,128]{1,0:T(8,128)S(1)}, u32[]{:S(2)}, u32[]{:S(2)}) collective-permute-start(f32[136,128]{1,0:T(8,128)S(1)} %add_add_fusion.own_ref), channel_id=1, source_target_pairs={{0,1},{1,0},{2,3},{3,2},{4,5},{5,4},{6,7},{7,6},{8,9},{9,8},{10,11... | collective-permute-start | bytes 208904 | tf_op jit(solution)/shard_map/ppermute | solution.py:425
  35.9 6.1 %collective-permute-start.13 = (bf16[256,128]{1,0:T(8,128)(2,1)S(1)}, bf16[256,128]{1,0:T(8,128)(2,1)S(1)}, u32[]{:S(2)}, u32[]{:S(2)}) collective-permute-start(bf16[256,128]{1,0:T(8,128)(2,1)S(1)} %convolution_convert_fusion.1.refs_4_), channel_id=1, source_target_pairs={{0,16},{2,18},{4,20},{6,22},{8,24},{10,26},{12,28},{14,30},{16,0},... | collective-permute-start | bytes 196616 | tf_op jit(solution)/shard_map/ppermute | solution.py:45
  38.9 6.5 %collective-permute-start.17 = (bf16[256,128]{1,0:T(8,128)(2,1)S(1)}, bf16[256,128]{1,0:T(8,128)(2,1)S(1)}, u32[]{:S(2)}, u32[]{:S(2)}) collective-permute-start(bf16[256,128]{1,0:T(8,128)(2,1)S(1)} %convolution_convert_fusion.1.refs_4_), channel_id=1, source_target_pairs={{0,8},{2,10},{4,12},{6,14},{8,0},{10,2},{12,4},{14,6},{16,24},{18,... | collective-permute-start | bytes 196616 | tf_op jit(solution)/shard_map/ppermute | solution.py:45
  40.0 6.1 %collective-permute-start.18 = (bf16[256,128]{1,0:T(8,128)(2,1)S(1)}, bf16[256,128]{1,0:T(8,128)(2,1)S(1)}, u32[]{:S(2)}, u32[]{:S(2)}) collective-permute-start(bf16[256,128]{1,0:T(8,128)(2,1)S(1)} %convolution_convert_fusion.1.refs_4_), channel_id=1, source_target_pairs={{0,24},{2,26},{4,28},{6,30},{8,16},{10,18},{12,20},{14,22},{16,8},... | collective-permute-start | bytes 196616 | tf_op jit(solution)/shard_map/ppermute | solution.py:45
  41.9 6.3 %collective-permute-start.16 = (bf16[256,128]{1,0:T(8,128)(2,1)S(1)}, bf16[256,128]{1,0:T(8,128)(2,1)S(1)}, u32[]{:S(2)}, u32[]{:S(2)}) collective-permute-start(bf16[256,128]{1,0:T(8,128)(2,1)S(1)} %convolution_convert_fusion.1.refs_4_), channel_id=1, source_target_pairs={{0,6},{2,4},{4,2},{6,0},{8,14},{10,12},{12,10},{14,8},{16,22},{18,... | collective-permute-start | bytes 196616 | tf_op jit(solution)/shard_map/ppermute | solution.py:45
  42.7 7.3 %collective-permute-start.15 = (bf16[256,128]{1,0:T(8,128)(2,1)S(1)}, bf16[256,128]{1,0:T(8,128)(2,1)S(1)}, u32[]{:S(2)}, u32[]{:S(2)}) collective-permute-start(bf16[256,128]{1,0:T(8,128)(2,1)S(1)} %convolution_convert_fusion.1.refs_4_), channel_id=1, source_target_pairs={{0,4},{2,6},{4,0},{6,2},{8,12},{10,14},{12,8},{14,10},{16,20},{18,... | collective-permute-start | bytes 196616 | tf_op jit(solution)/shard_map/ppermute | solution.py:45
  44.0 5.9 %collective-permute-start.14 = (bf16[256,128]{1,0:T(8,128)(2,1)S(1)}, bf16[256,128]{1,0:T(8,128)(2,1)S(1)}, u32[]{:S(2)}, u32[]{:S(2)}) collective-permute-start(bf16[256,128]{1,0:T(8,128)(2,1)S(1)} %convolution_convert_fusion.1.refs_4_), channel_id=1, source_target_pairs={{0,2},{2,0},{4,6},{6,4},{8,10},{10,8},{12,14},{14,12},{16,18},{18,... | collective-permute-start | bytes 196616 | tf_op jit(solution)/shard_map/ppermute | solution.py:45
  46.1 8.7 %collective-permute-start.21 = (bf16[256,384]{1,0:T(8,128)(2,1)S(1)}, bf16[256,384]{1,0:T(8,128)(2,1)S(1)}, u32[]{:S(2)}, u32[]{:S(2)}) collective-permute-start(bf16[256,384]{1,0:T(8,128)(2,1)S(1)} %constant_dynamic-update-slice_fusion.refs_8_), channel_id=1, source_target_pairs={{0,6},{2,4},{4,2},{6,0},{8,14},{10,12},{12,10},{14,8},{16,22},{18,... | collective-permute-start | bytes 589832 | tf_op jit(solution)/shard_map/ppermute | solution.py:45
  47.0 9.3 %collective-permute-start.20 = (bf16[256,384]{1,0:T(8,128)(2,1)S(1)}, bf16[256,384]{1,0:T(8,128)(2,1)S(1)}, u32[]{:S(2)}, u32[]{:S(2)}) collective-permute-start(bf16[256,384]{1,0:T(8,128)(2,1)S(1)} %constant_dynamic-update-slice_fusion.refs_8_), channel_id=1, source_target_pairs={{0,4},{2,6},{4,0},{6,2},{8,12},{10,14},{12,8},{14,10},{16,20},{18,... | collective-permute-start | bytes 589832 | tf_op jit(solution)/shard_map/ppermute | solution.py:45
  48.2 8.6 %collective-permute-start.19 = (bf16[256,384]{1,0:T(8,128)(2,1)S(1)}, bf16[256,384]{1,0:T(8,128)(2,1)S(1)}, u32[]{:S(2)}, u32[]{:S(2)}) collective-permute-start(bf16[256,384]{1,0:T(8,128)(2,1)S(1)} %constant_dynamic-update-slice_fusion.refs_8_), channel_id=1, source_target_pairs={{0,2},{2,0},{4,6},{6,4},{8,10},{10,8},{12,14},{14,12},{16,18},{18,... | collective-permute-start | bytes 589832 | tf_op jit(solution)/shard_map/ppermute | solution.py:45

commit v5 on v4

--- a/solution.py
+++ b/solution.py
@@ -321,12 +321,12 @@
     )
 
 
-def update_kernel(near, far, basis_ref, *refs):
-    chunks, firsts, rests = refs[:near], refs[near : 2 * near], refs[2 * near : 3 * near]
-    coupling_ref, updated_ref, work, sems = refs[3 * near :]
+def update_kernel(near, far, held, basis_ref, *refs):
+    count = len(held)
+    chunks, parts = refs[:count], refs[count : 2 * count]
+    coupling_ref, updated_ref, work, sems = refs[-4:]
     index = lax.axis_index("row")
     near_index, far_index = lax.rem(index, near), lax.div(index, near)
-    width = firsts[0].shape[1]
     copies = []
 
     def send(source, target, cols):
@@ -334,69 +334,92 @@
         copy.start()
         copies.append(copy)
 
-    for i in range(near):
-        for k in range(far):
-            source = firsts[i] if k == 0 else rests[i].at[:, (k - 1) * width : k * width]
-            start = ((near_index ^ i) * far + (far_index ^ k)) * width
-            send(source, coupling_ref, pl.ds(pl.multiple_of(start, width), width))
-    for i in range(near):
-        for part in (firsts, rests):
-            removed = jnp.dot(basis_ref[...], part[i][...], preferred_element_type=jnp.float32)
-            for k in range(part[i].shape[1] // width):
-                slot = k if part is firsts else k + 1
-                inner = (far_index ^ slot) * width
-                left = chunks[i][:, pl.ds(pl.multiple_of(inner, width), width)]
-                place = (i * far + slot) * width
-                result = left.astype(jnp.float32) - removed[:, k * width : (k + 1) * width]
-                work[:, place : place + width] = result.astype(work.dtype)
-                start = (near_index ^ i) * far * width + inner
-                cols = pl.ds(pl.multiple_of(start, width), width)
-                send(work.at[:, place : place + width], updated_ref, cols)
+    place = 0
+    for (offset, slots), chunk, part in zip(held, chunks, parts):
+        width = part.shape[1] // len(slots)
+        for k, slot in enumerate(slots):
+            start = ((near_index ^ offset) * far + (far_index ^ slot)) * width
+            cols = pl.ds(pl.multiple_of(start, width), width)
+            send(part.at[:, k * width : (k + 1) * width], coupling_ref, cols)
+    for (offset, slots), chunk, part in zip(held, chunks, parts):
+        width = part.shape[1] // len(slots)
+        removed = jnp.dot(basis_ref[...], part[...], preferred_element_type=jnp.float32)
+        for k, slot in enumerate(slots):
+            inner = (far_index ^ slot) * width
+            left = chunk[:, pl.ds(pl.multiple_of(inner, width), width)].astype(jnp.float32)
+            result = left - removed[:, k * width : (k + 1) * width]
+            work[:, place : place + width] = result.astype(work.dtype)
+            start = (near_index ^ offset) * far * width + inner
+            cols = pl.ds(pl.multiple_of(start, width), width)
+            send(work.at[:, place : place + width], updated_ref, cols)
+            place += width
     for copy in copies:
         copy.wait()
 
 
-def update(groups, basis, chunks, firsts, rests):
+def update_part(groups, basis, chunks, held, parts, outs):
     near, far = groups.near, groups.far
-    rows, width = chunks[0].shape
-    cols = width * near
+    rows, chunk = chunks[0].shape
+    cols = chunk * near
+    pieces = sum(len(slots) for _, slots in held)
     dtype = chunks[0].dtype
-    if (width // far) % 128:
-        return update_plain(groups, basis, chunks, firsts, rests)
+    count = 1 + 2 * len(held)
     hbm = pl.BlockSpec(memory_space=pltpu.HBM)
     return pl.pallas_call(
-        functools.partial(update_kernel, near, far),
+        functools.partial(update_kernel, near, far, held),
         out_shape=[
-            jax.ShapeDtypeStruct((firsts[0].shape[0], cols), dtype),
+            jax.ShapeDtypeStruct((parts[0].shape[0], cols), dtype),
             jax.ShapeDtypeStruct((rows, cols), dtype),
         ],
-        in_specs=[VMEM] * (1 + 3 * near),
+        in_specs=[VMEM] * count + [hbm] * len(outs),
         out_specs=[hbm] * 2,
+        input_output_aliases={count + i: i for i in range(len(outs))},
         scratch_shapes=[
-            pltpu.VMEM((rows, cols), dtype),
-            pltpu.SemaphoreType.DMA((2 * near * far,)),
+            pltpu.VMEM((rows, pieces * (chunk // far)), dtype),
+            pltpu.SemaphoreType.DMA((2 * pieces,)),
         ],
         compiler_params=PARAMS,
+        cost_estimate=pl.CostEstimate(
+            flops=2 * rows * parts[0].shape[0] * pieces * (chunk // far),
+            bytes_accessed=16 * rows * pieces * (chunk // far),
+            transcendentals=0,
+        ),
         name="update",
-    )(basis, *chunks, *firsts, *rests)
+    )(basis, *[chunks[offset] for offset, _ in held], *parts, *outs)
+
+
+def update(groups, basis, chunks, firsts, rests):
+    near = groups.near
+    if (chunks[0].shape[1] // groups.far) % 128:
+        return update_plain(groups, basis, chunks, firsts, rests)
+    early, late = far_slots(groups)
+    held = [(0, early), (0, late)] + [(i, early) for i in range(1, near)]
+    outs = update_part(groups, basis, chunks, held, [firsts[0], rests[0], *firsts[1:]], [])
+    held = [(i, late) for i in range(1, near)]
+    return update_part(groups, basis, chunks, held, rests[1:], outs)
 
 
 def update_plain(groups, basis, chunks, firsts, rests):
     near, far = groups.near, groups.far
     rows, chunk = chunks[0].shape
-    width = firsts[0].shape[1]
+    width = chunk // far
+    early, late = far_slots(groups)
     coupling = jnp.zeros((firsts[0].shape[0], chunk * near), firsts[0].dtype)
     masked = jnp.zeros((rows, chunk * near), chunks[0].dtype)
     for i in range(near):
         base = (groups.near_index() ^ i) * chunk
         masked = lax.dynamic_update_slice_in_dim(masked, chunks[i], base, 1)
-        slot = jnp.concatenate([firsts[i], rests[i]], axis=1)
-        for k in range(far):
-            start = base + (groups.far_index() ^ k) * width
-            part = slot[:, k * width : (k + 1) * width]
+        slots = jnp.concatenate([firsts[i], rests[i]], axis=1)
+        for k, slot in enumerate([*early, *late]):
+            start = base + (groups.far_index() ^ slot) * width
+            part = slots[:, k * width : (k + 1) * width]
             coupling = lax.dynamic_update_slice_in_dim(coupling, part, start, 1)
     removed = jnp.dot(basis, coupling, preferred_element_type=jnp.float32)
     return coupling, (masked.astype(jnp.float32) - removed).astype(masked.dtype)
+
+
+def far_slots(groups):
+    return [0], list(range(1, groups.far))
 
 
 def gather_slots(groups, shard):

time: 58.6 us -> 58.1 us (level)
  waiting for transfers between devices: 14.9 us -> 13.7 us
  Pallas kernels: 11.1 us -> 11.8 us
    ppermute x21, waiting for transfers between devices: 13.6 us -> 12.5 us  [swap(): lax.ppermute(value, 'row', [(i, i ^ offset) for i in range(self.rows)])]
    pallas_call x1 -> x2, Pallas kernels: 1.69 us -> 2.33 us  [update_part(): pl.pallas_call(functools.partial(update_kernel, near, far, held), out_sha...]
  transfers between devices with their start and end apart: 22 -> 22, of which waited for: 9 -> 9; matrix products, arithmetic and copies ran while one was open for 1% -> 1% of each run, Pallas kernels for 16% -> 18%
where the time goes in v5:
time: 58.1 us; the launch traced here: 58 us
  starting transfers between devices  28.8 us (50%)
  waiting for transfers between devices  13.7 us (24%)
  Pallas kernels  11.8 us (20%)
  blocking collectives  2.18 us (4%)
  between operations  0.75 us (1%)
  matrix products  0.71 us (1%)
    ppermute x21, starting transfers between devices, swap(): lax.ppermute(value, 'row', [(i, i ^ offset) for i in range(self.rows)])  28.7 us
    ppermute x21, waiting for transfers between devices, swap(): lax.ppermute(value, 'row', [(i, i ^ offset) for i in range(self.rows)])  12.5 us
    pallas_call x1, Pallas kernels, cholesky_pair(): pl.pallas_call(factor_kernel, out_shape=[out, out], in_specs=[VMEM] * 2,...  7.31 us
    pallas_call x2, Pallas kernels, update_part(): pl.pallas_call(functools.partial(update_kernel, near, far, held), out_sha...  2.33 us
    all_gather x1, blocking collectives, local(): gathered = lax.all_gather(stacked, 'col', axis=1, tiled=True)  2.18 us
    pallas_call x1, Pallas kernels, masked_chunks(): pl.pallas_call(functools.partial(chunk_kernel, groups.near), out_shape=[o...  1.25 us
    ppermute x1, waiting for transfers between devices, local(): lax.ppermute(gram_own, 'col', [(i, i ^ 1) for i in range(groups.cols)])  1.25 us
  transfers between devices with their start and end apart: 22, of which 9 were waited for; matrix products, arithmetic and copies ran while one was open for 1% of the time, Pallas kernels for 18%

profile of v5, /device:TPU:0, one launch (start us, length us, event | category | flops | bytes accessed | tf_op | source)
XLA Modules:
  0.0 58.0 jit_solution(12190792088621140503)
XLA Ops:
  0.6 0.0 copy-start
  0.6 3.0 %collective-permute-start.1 = (bf16[256,128]{1,0:T(8,128)(2,1)}, bf16[256,128]{1,0:T(8,128)(2,1)S(1)}, u32[]{:S(2)}, u32[]{:S(2)}) collective-permute-start(bf16[256,128]{1,0:T(8,128)(2,1)} %param.3), channel_id=1, source_target_pairs={{0,4},{2,6},{4,0},{6,2},{8,12},{10,14},{12,8},{14,10},{16,20},{18,... | collective-permute-start | bytes 196616 | tf_op jit(solution)/shard_map/ppermute | solution.py:45
  3.7 1.5 %collective-permute-start = (bf16[256,128]{1,0:T(8,128)(2,1)}, bf16[256,128]{1,0:T(8,128)(2,1)S(1)}, u32[]{:S(2)}, u32[]{:S(2)}) collective-permute-start(bf16[256,128]{1,0:T(8,128)(2,1)} %param.3), channel_id=1, source_target_pairs={{0,2},{2,0},{4,6},{6,4},{8,10},{10,8},{12,14},{14,12},{16,18},{18,... | collective-permute-start | bytes 196616 | tf_op jit(solution)/shard_map/ppermute | solution.py:45
  5.2 0.0 collective-permute-start.2
  5.2 1.3 %chunks.1 = (bf16[256,512]{1,0:T(8,128)(2,1)S(1)}, bf16[256,512]{1,0:T(8,128)(2,1)S(1)}, bf16[256,512]{1,0:T(8,128)(2,1)S(1)}, bf16[256,512]{1,0:T(8,128)(2,1)S(1)}) custom-call(s32[1,8]{1,0:T(1,128)} %mask_hbm.1, bf16[256,2048]{1,0:T(8,128)(2,1)} %trailing_hbm.1), custom_call_target="tpu_custom_call" | custom-call | tf_op jit(solution)/shard_map/chunks/pallas_call | solution.py:306
  6.5 2.0 %collective-permute-start.7 = (bf16[256,512]{1,0:T(8,128)(2,1)S(1)}, bf16[256,512]{1,0:T(8,128)(2,1)S(1)}, u32[]{:S(2)}, u32[]{:S(2)}) collective-permute-start(bf16[256,512]{1,0:T(8,128)(2,1)S(1)} %get-tuple-element.24.refs_2_.refs_0_), channel_id=1, source_target_pairs={{0,2},{2,0},{4,6},{6,4},{8,10},{10,8},{12,14},{14,12},{16,18},{18,... | collective-permute-start | bytes 786440 | tf_op jit(solution)/shard_map/ppermute | solution.py:45
  8.5 1.5 %collective-permute-start.8 = (bf16[256,512]{1,0:T(8,128)(2,1)S(1)}, bf16[256,512]{1,0:T(8,128)(2,1)S(1)}, u32[]{:S(2)}, u32[]{:S(2)}) collective-permute-start(bf16[256,512]{1,0:T(8,128)(2,1)S(1)} %get-tuple-element.25.refs_3_.refs_1_), channel_id=1, source_target_pairs={{0,4},{2,6},{4,0},{6,2},{8,12},{10,14},{12,8},{14,10},{16,20},{18,... | collective-permute-start | bytes 786440 | tf_op jit(solution)/shard_map/ppermute | solution.py:45
  10.0 0.0 collective-permute-done.1
  10.0 0.0 collective-permute-start.9
  10.0 0.0 collective-permute-done
  10.0 1.2 %collective-permute-done.2 = bf16[256,128]{1,0:T(8,128)(2,1)S(1)} collective-permute-done((bf16[256,128]{1,0:T(8,128)(2,1)}, bf16[256,128]{1,0:T(8,128)(2,1)S(1)}, u32[]{:S(2)}, u32[]{:S(2)}) %collective-permute-start.2) | collective-permute-done | bytes 65568 | tf_op jit(solution)/shard_map/ppermute | solution.py:45
  11.2 0.0 copy-done
  11.3 2.2 %all_gather.3.panel_ref = bf16[1024,256]{1,0:T(8,128)(2,1)S(1)} all-gather(bf16[1024,128]{1,0:T(8,128)(2,1)S(1)} %pad_maximum_fusion), channel_id=1, replica_groups=mesh['row'=16,'col'=2] {'col'}, dimensions={1}, use_global_device_ids=true | all-gather | bytes 786432 | tf_op jit(solution)/shard_map/all_gather | solution.py:439
  13.5 0.4 gram_part.1
  13.8 3.7 %collective-permute-start.5 = (f32[136,128]{1,0:T(8,128)S(1)}, f32[136,128]{1,0:T(8,128)S(1)}, u32[]{:S(2)}, u32[]{:S(2)}) collective-permute-start(f32[136,128]{1,0:T(8,128)S(1)} %get-tuple-element.21), channel_id=1, source_target_pairs={{0,24},{2,26},{4,28},{6,30},{8,16},{10,18},{12,20},{14,22},{16,8},... | collective-permute-start | bytes 208904 | tf_op jit(solution)/shard_map/ppermute | solution.py:45
  17.5 0.0 collective-permute-start.4
  17.5 0.0 collective-permute-done.7.refs_1_
  17.5 0.8 %collective-permute-start.3 = (f32[136,128]{1,0:T(8,128)S(1)}, f32[136,128]{1,0:T(8,128)S(1)}, u32[]{:S(2)}, u32[]{:S(2)}) collective-permute-start(f32[136,128]{1,0:T(8,128)S(1)} %get-tuple-element.21), channel_id=1, source_target_pairs={{0,8},{2,10},{4,12},{6,14},{8,0},{10,2},{12,4},{14,6},{16,24},{18,... | collective-permute-start | bytes 208904 | tf_op jit(solution)/shard_map/ppermute | solution.py:45
  18.3 3.4 %collective-permute-done.8.refs_2_ = bf16[256,512]{1,0:T(8,128)(2,1)S(1)} collective-permute-done((bf16[256,512]{1,0:T(8,128)(2,1)S(1)}, bf16[256,512]{1,0:T(8,128)(2,1)S(1)}, u32[]{:S(2)}, u32[]{:S(2)}) %collective-permute-start.8) | collective-permute-done | bytes 262176 | tf_op jit(solution)/shard_map/ppermute | solution.py:45
  21.7 0.0 collective-permute-done.9.refs_3_
  21.7 0.5 cross_part.1
  22.2 1.6 %collective-permute-start.10 = (f32[256,128]{1,0:T(8,128)S(1)}, f32[256,128]{1,0:T(8,128)S(1)}, u32[]{:S(2)}, u32[]{:S(2)}) collective-permute-start(f32[256,128]{1,0:T(8,128)S(1)} %get-tuple-element.30), channel_id=1, source_target_pairs={{0,8},{2,10},{4,12},{6,14},{8,0},{10,2},{12,4},{14,6},{16,24},{18,... | collective-permute-start | bytes 393224 | tf_op jit(solution)/shard_map/ppermute | solution.py:45
  23.9 2.6 %collective-permute-start.11 = (f32[256,128]{1,0:T(8,128)S(1)}, f32[256,128]{1,0:T(8,128)S(1)}, u32[]{:S(2)}, u32[]{:S(2)}) collective-permute-start(f32[256,128]{1,0:T(8,128)S(1)} %get-tuple-element.31), channel_id=1, source_target_pairs={{0,16},{2,18},{4,20},{6,22},{8,24},{10,26},{12,28},{14,30},{16,0},... | collective-permute-start | bytes 393224 | tf_op jit(solution)/shard_map/ppermute | solution.py:45
  26.5 0.0 collective-permute-done.5
  26.5 0.2 collective-permute-start.12
  26.7 0.0 collective-permute-done.4
  26.7 0.0 collective-permute-done.3
  26.7 0.1 collective-permute-start.6
  26.8 1.2 %collective-permute-done.6.other_ref = f32[136,128]{1,0:T(8,128)S(1)} collective-permute-done((f32[136,128]{1,0:T(8,128)S(1)}, f32[136,128]{1,0:T(8,128)S(1)}, u32[]{:S(2)}, u32[]{:S(2)}) %collective-permute-start.6) | collective-permute-done | bytes 69664 | tf_op jit(solution)/shard_map/ppermute | solution.py:448
  28.0 7.3 %factor.1 = (f32[256,256]{1,0:T(8,128)}, f32[256,256]{1,0:T(8,128)S(1)}) custom-call(f32[136,128]{1,0:T(8,128)S(1)} %add_add_fusion.own_ref, f32[136,128]{1,0:T(8,128)S(1)} %collective-permute-done.6.other_ref), custom_call_target="tpu_custom_call" | custom-call | flops 134217728 | bytes 3145728 | tf_op jit(solution)/shard_map/factor/pallas_call | solution.py:191
  35.3 0.0 collective-permute-done.10
  35.3 0.1 collective-permute-done.11
  35.5 0.0 collective-permute-done.12
  35.5 0.4 convolution_convert_fusion.1.refs_5_
  35.9 3.1 %collective-permute-start.14 = (bf16[256,128]{1,0:T(8,128)(2,1)S(1)}, bf16[256,128]{1,0:T(8,128)(2,1)S(1)}, u32[]{:S(2)}, u32[]{:S(2)}) collective-permute-start(bf16[256,128]{1,0:T(8,128)(2,1)S(1)} %convolution_convert_fusion.1.refs_5_), channel_id=1, source_target_pairs={{0,16},{2,18},{4,20},{6,22},{8,24},{10,26},{12,28},{14,30},{16,0},... | collective-permute-start | bytes 196616 | tf_op jit(solution)/shard_map/ppermute | solution.py:45
  38.9 1.0 %collective-permute-start.13 = (bf16[256,128]{1,0:T(8,128)(2,1)S(1)}, bf16[256,128]{1,0:T(8,128)(2,1)S(1)}, u32[]{:S(2)}, u32[]{:S(2)}) collective-permute-start(bf16[256,128]{1,0:T(8,128)(2,1)S(1)} %convolution_convert_fusion.1.refs_5_), channel_id=1, source_target_pairs={{0,8},{2,10},{4,12},{6,14},{8,0},{10,2},{12,4},{14,6},{16,24},{18,... | collective-permute-start | bytes 196616 | tf_op jit(solution)/shard_map/ppermute | solution.py:45
  40.0 0.5 collective-permute-start.15
  40.5 1.4 %collective-permute-done.14 = bf16[256,128]{1,0:T(8,128)(2,1)S(1)} collective-permute-done((bf16[256,128]{1,0:T(8,128)(2,1)S(1)}, bf16[256,128]{1,0:T(8,128)(2,1)S(1)}, u32[]{:S(2)}, u32[]{:S(2)}) %collective-permute-start.14) | collective-permute-done | bytes 65568 | tf_op jit(solution)/shard_map/ppermute | solution.py:45
  41.9 0.8 %collective-permute-start.21 = (bf16[256,128]{1,0:T(8,128)(2,1)S(1)}, bf16[256,128]{1,0:T(8,128)(2,1)S(1)}, u32[]{:S(2)}, u32[]{:S(2)}) collective-permute-start(bf16[256,128]{1,0:T(8,128)(2,1)S(1)} %convolution_convert_fusion.1.refs_5_), channel_id=1, source_target_pairs={{0,6},{2,4},{4,2},{6,0},{8,14},{10,12},{12,10},{14,8},{16,22},{18,... | collective-permute-start | bytes 196616 | tf_op jit(solution)/shard_map/ppermute | solution.py:45
  42.7 1.3 %collective-permute-start.20 = (bf16[256,128]{1,0:T(8,128)(2,1)S(1)}, bf16[256,128]{1,0:T(8,128)(2,1)S(1)}, u32[]{:S(2)}, u32[]{:S(2)}) collective-permute-start(bf16[256,128]{1,0:T(8,128)(2,1)S(1)} %convolution_convert_fusion.1.refs_5_), channel_id=1, source_target_pairs={{0,4},{2,6},{4,0},{6,2},{8,12},{10,14},{12,8},{14,10},{16,20},{18,... | collective-permute-start | bytes 196616 | tf_op jit(solution)/shard_map/ppermute | solution.py:45
  44.0 1.4 %collective-permute-start.19 = (bf16[256,128]{1,0:T(8,128)(2,1)S(1)}, bf16[256,128]{1,0:T(8,128)(2,1)S(1)}, u32[]{:S(2)}, u32[]{:S(2)}) collective-permute-start(bf16[256,128]{1,0:T(8,128)(2,1)S(1)} %convolution_convert_fusion.1.refs_5_), channel_id=1, source_target_pairs={{0,2},{2,0},{4,6},{6,4},{8,10},{10,8},{12,14},{14,12},{16,18},{18,... | collective-permute-start | bytes 196616 | tf_op jit(solution)/shard_map/ppermute | solution.py:45
  45.4 0.0 collective-permute-done.13
  45.5 0.6 %collective-permute-done.15 = bf16[256,128]{1,0:T(8,128)(2,1)S(1)} collective-permute-done((bf16[256,128]{1,0:T(8,128)(2,1)S(1)}, bf16[256,128]{1,0:T(8,128)(2,1)S(1)}, u32[]{:S(2)}, u32[]{:S(2)}) %collective-permute-start.15) | collective-permute-done | bytes 65568 | tf_op jit(solution)/shard_map/ppermute | solution.py:45
  46.1 1.0 %collective-permute-start.18 = (bf16[256,384]{1,0:T(8,128)(2,1)S(1)}, bf16[256,384]{1,0:T(8,128)(2,1)S(1)}, u32[]{:S(2)}, u32[]{:S(2)}) collective-permute-start(bf16[256,384]{1,0:T(8,128)(2,1)S(1)} %constant_dynamic-update-slice_fusion.refs_6_), channel_id=1, source_target_pairs={{0,6},{2,4},{4,2},{6,0},{8,14},{10,12},{12,10},{14,8},{16,22},{18,... | collective-permute-start | bytes 589832 | tf_op jit(solution)/shard_map/ppermute | solution.py:45
  47.0 1.1 %collective-permute-start.17 = (bf16[256,384]{1,0:T(8,128)(2,1)S(1)}, bf16[256,384]{1,0:T(8,128)(2,1)S(1)}, u32[]{:S(2)}, u32[]{:S(2)}) collective-permute-start(bf16[256,384]{1,0:T(8,128)(2,1)S(1)} %constant_dynamic-update-slice_fusion.refs_6_), channel_id=1, source_target_pairs={{0,4},{2,6},{4,0},{6,2},{8,12},{10,14},{12,8},{14,10},{16,20},{18,... | collective-permute-start | bytes 589832 | tf_op jit(solution)/shard_map/ppermute | solution.py:45
  48.2 0.0 collective-permute-done.21.refs_9_
  48.2 1.5 %collective-permute-start.16 = (bf16[256,384]{1,0:T(8,128)(2,1)S(1)}, bf16[256,384]{1,0:T(8,128)(2,1)S(1)}, u32[]{:S(2)}, u32[]{:S(2)}) collective-permute-start(bf16[256,384]{1,0:T(8,128)(2,1)S(1)} %constant_dynamic-update-slice_fusion.refs_6_), channel_id=1, source_target_pairs={{0,2},{2,0},{4,6},{6,4},{8,10},{10,8},{12,14},{14,12},{16,18},{18,... | collective-permute-start | bytes 589832 | tf_op jit(solution)/shard_map/ppermute | solution.py:45
  49.7 0.3 convolution_convert_fusion.basis_ref
  50.0 0.0 collective-permute-done.20.refs_8_
  50.0 0.0 collective-permute-done.19.refs_7_
  50.0 1.1 %update.2 = (bf16[256,2048]{1,0:T(8,128)(2,1)}, bf16[256,2048]{1,0:T(8,128)(2,1)}) custom-call(bf16[256,256]{1,0:T(8,128)(2,1)S(1)} %convolution_convert_fusion.basis_ref, bf16[256,512]{1,0:T(8,128)(2,1)S(1)} %get-tuple-element.28.refs_0_.refs_1_, bf16[256,512]{1,0:T(8,128)(2,1)S(1)} %get-tuple-element.28.refs_0_.refs_1_, ...), custom_call_target="tpu_custom_call" | custom-call | flops 117440512 | bytes 3670016 | tf_op jit(solution)/shard_map/update/pallas_call | solution.py:368
  51.1 3.6 %collective-permute-done.18.refs_5_ = bf16[256,384]{1,0:T(8,128)(2,1)S(1)} collective-permute-done((bf16[256,384]{1,0:T(8,128)(2,1)S(1)}, bf16[256,384]{1,0:T(8,128)(2,1)S(1)}, u32[]{:S(2)}, u32[]{:S(2)}) %collective-permute-start.18) | collective-permute-done | bytes 196640 | tf_op jit(solution)/shard_map/ppermute | solution.py:45
  54.8 1.5 %collective-permute-done.17.refs_4_ = bf16[256,384]{1,0:T(8,128)(2,1)S(1)} collective-permute-done((bf16[256,384]{1,0:T(8,128)(2,1)S(1)}, bf16[256,384]{1,0:T(8,128)(2,1)S(1)}, u32[]{:S(2)}, u32[]{:S(2)}) %collective-permute-start.17) | collective-permute-done | bytes 196640 | tf_op jit(solution)/shard_map/ppermute | solution.py:45
  56.3 0.4 collective-permute-done.16.refs_3_
  56.8 1.2 %update.3 = (bf16[256,2048]{1,0:T(8,128)(2,1)}, bf16[256,2048]{1,0:T(8,128)(2,1)}) custom-call(bf16[256,256]{1,0:T(8,128)(2,1)S(1)} %convolution_convert_fusion.basis_ref, bf16[256,512]{1,0:T(8,128)(2,1)S(1)} %get-tuple-element.24.refs_2_.refs_0_, ...), custom_call_target="tpu_custom_call", output_to_operand_aliasing={{0}: (7, {}), {1}: (8, {})} | custom-call | flops 150994944 | bytes 4718592 | tf_op jit(solution)/shard_map/update/pallas_call | solution.py:368
  (5 shorter events, 0.1 us)
Async XLA Ops:
  0.6 10.6 %copy-start = (bf16[256,128]{1,0:T(8,128)(2,1)S(1)}, bf16[256,128]{1,0:T(8,128)(2,1)}, u32[]{:S(2)}) copy-start(bf16[256,128]{1,0:T(8,128)(2,1)} %param.3) | copy-start | bytes 196612
  0.6 9.3 %collective-permute-start.1 = (bf16[256,128]{1,0:T(8,128)(2,1)}, bf16[256,128]{1,0:T(8,128)(2,1)S(1)}, u32[]{:S(2)}, u32[]{:S(2)}) collective-permute-start(bf16[256,128]{1,0:T(8,128)(2,1)} %param.3), channel_id=1, source_target_pairs={{0,4},{2,6},{4,0},{6,2},{8,12},{10,14},{12,8},{14,10},{16,20},{18,... | collective-permute-start | bytes 196616 | tf_op jit(solution)/shard_map/ppermute | solution.py:45
  3.7 6.4 %collective-permute-start = (bf16[256,128]{1,0:T(8,128)(2,1)}, bf16[256,128]{1,0:T(8,128)(2,1)S(1)}, u32[]{:S(2)}, u32[]{:S(2)}) collective-permute-start(bf16[256,128]{1,0:T(8,128)(2,1)} %param.3), channel_id=1, source_target_pairs={{0,2},{2,0},{4,6},{6,4},{8,10},{10,8},{12,14},{14,12},{16,18},{18,... | collective-permute-start | bytes 196616 | tf_op jit(solution)/shard_map/ppermute | solution.py:45
  5.2 6.1 %collective-permute-start.2 = (bf16[256,128]{1,0:T(8,128)(2,1)}, bf16[256,128]{1,0:T(8,128)(2,1)S(1)}, u32[]{:S(2)}, u32[]{:S(2)}) collective-permute-start(bf16[256,128]{1,0:T(8,128)(2,1)} %param.3), channel_id=1, source_target_pairs={{0,6},{2,4},{4,2},{6,0},{8,14},{10,12},{12,10},{14,8},{16,22},{18,... | collective-permute-start | bytes 196616 | tf_op jit(solution)/shard_map/ppermute | solution.py:45
  6.5 11.0 %collective-permute-start.7 = (bf16[256,512]{1,0:T(8,128)(2,1)S(1)}, bf16[256,512]{1,0:T(8,128)(2,1)S(1)}, u32[]{:S(2)}, u32[]{:S(2)}) collective-permute-start(bf16[256,512]{1,0:T(8,128)(2,1)S(1)} %get-tuple-element.24.refs_2_.refs_0_), channel_id=1, source_target_pairs={{0,2},{2,0},{4,6},{6,4},{8,10},{10,8},{12,14},{14,12},{16,18},{18,... | collective-permute-start | bytes 786440 | tf_op jit(solution)/shard_map/ppermute | solution.py:45
  8.5 13.2 %collective-permute-start.8 = (bf16[256,512]{1,0:T(8,128)(2,1)S(1)}, bf16[256,512]{1,0:T(8,128)(2,1)S(1)}, u32[]{:S(2)}, u32[]{:S(2)}) collective-permute-start(bf16[256,512]{1,0:T(8,128)(2,1)S(1)} %get-tuple-element.25.refs_3_.refs_1_), channel_id=1, source_target_pairs={{0,4},{2,6},{4,0},{6,2},{8,12},{10,14},{12,8},{14,10},{16,20},{18,... | collective-permute-start | bytes 786440 | tf_op jit(solution)/shard_map/ppermute | solution.py:45
  10.0 11.7 %collective-permute-start.9 = (bf16[256,512]{1,0:T(8,128)(2,1)S(1)}, bf16[256,512]{1,0:T(8,128)(2,1)S(1)}, u32[]{:S(2)}, u32[]{:S(2)}) collective-permute-start(bf16[256,512]{1,0:T(8,128)(2,1)S(1)} %get-tuple-element.26.refs_4_.refs_2_), channel_id=1, source_target_pairs={{0,6},{2,4},{4,2},{6,0},{8,14},{10,12},{12,10},{14,8},{16,22},{18,... | collective-permute-start | bytes 786440 | tf_op jit(solution)/shard_map/ppermute | solution.py:45
  13.8 12.6 %collective-permute-start.5 = (f32[136,128]{1,0:T(8,128)S(1)}, f32[136,128]{1,0:T(8,128)S(1)}, u32[]{:S(2)}, u32[]{:S(2)}) collective-permute-start(f32[136,128]{1,0:T(8,128)S(1)} %get-tuple-element.21), channel_id=1, source_target_pairs={{0,24},{2,26},{4,28},{6,30},{8,16},{10,18},{12,20},{14,22},{16,8},... | collective-permute-start | bytes 208904 | tf_op jit(solution)/shard_map/ppermute | solution.py:45
  17.5 9.2 %collective-permute-start.4 = (f32[136,128]{1,0:T(8,128)S(1)}, f32[136,128]{1,0:T(8,128)S(1)}, u32[]{:S(2)}, u32[]{:S(2)}) collective-permute-start(f32[136,128]{1,0:T(8,128)S(1)} %get-tuple-element.21), channel_id=1, source_target_pairs={{0,16},{2,18},{4,20},{6,22},{8,24},{10,26},{12,28},{14,30},{16,0},... | collective-permute-start | bytes 208904 | tf_op jit(solution)/shard_map/ppermute | solution.py:45
  17.5 9.2 %collective-permute-start.3 = (f32[136,128]{1,0:T(8,128)S(1)}, f32[136,128]{1,0:T(8,128)S(1)}, u32[]{:S(2)}, u32[]{:S(2)}) collective-permute-start(f32[136,128]{1,0:T(8,128)S(1)} %get-tuple-element.21), channel_id=1, source_target_pairs={{0,8},{2,10},{4,12},{6,14},{8,0},{10,2},{12,4},{14,6},{16,24},{18,... | collective-permute-start | bytes 208904 | tf_op jit(solution)/shard_map/ppermute | solution.py:45
  22.2 13.1 %collective-permute-start.10 = (f32[256,128]{1,0:T(8,128)S(1)}, f32[256,128]{1,0:T(8,128)S(1)}, u32[]{:S(2)}, u32[]{:S(2)}) collective-permute-start(f32[256,128]{1,0:T(8,128)S(1)} %get-tuple-element.30), channel_id=1, source_target_pairs={{0,8},{2,10},{4,12},{6,14},{8,0},{10,2},{12,4},{14,6},{16,24},{18,... | collective-permute-start | bytes 393224 | tf_op jit(solution)/shard_map/ppermute | solution.py:45
  23.9 11.6 %collective-permute-start.11 = (f32[256,128]{1,0:T(8,128)S(1)}, f32[256,128]{1,0:T(8,128)S(1)}, u32[]{:S(2)}, u32[]{:S(2)}) collective-permute-start(f32[256,128]{1,0:T(8,128)S(1)} %get-tuple-element.31), channel_id=1, source_target_pairs={{0,16},{2,18},{4,20},{6,22},{8,24},{10,26},{12,28},{14,30},{16,0},... | collective-permute-start | bytes 393224 | tf_op jit(solution)/shard_map/ppermute | solution.py:45
  26.5 9.0 %collective-permute-start.12 = (f32[256,128]{1,0:T(8,128)S(1)}, f32[256,128]{1,0:T(8,128)S(1)}, u32[]{:S(2)}, u32[]{:S(2)}) collective-permute-start(f32[256,128]{1,0:T(8,128)S(1)} %get-tuple-element.32), channel_id=1, source_target_pairs={{0,24},{2,26},{4,28},{6,30},{8,16},{10,18},{12,20},{14,22},{16,8},... | collective-permute-start | bytes 393224 | tf_op jit(solution)/shard_map/ppermute | solution.py:45
  26.7 1.3 %collective-permute-start.6 = (f32[136,128]{1,0:T(8,128)S(1)}, f32[136,128]{1,0:T(8,128)S(1)}, u32[]{:S(2)}, u32[]{:S(2)}) collective-permute-start(f32[136,128]{1,0:T(8,128)S(1)} %add_add_fusion.own_ref), channel_id=1, source_target_pairs={{0,1},{1,0},{2,3},{3,2},{4,5},{5,4},{6,7},{7,6},{8,9},{9,8},{10,11... | collective-permute-start | bytes 208904 | tf_op jit(solution)/shard_map/ppermute | solution.py:448
  35.9 6.1 %collective-permute-start.14 = (bf16[256,128]{1,0:T(8,128)(2,1)S(1)}, bf16[256,128]{1,0:T(8,128)(2,1)S(1)}, u32[]{:S(2)}, u32[]{:S(2)}) collective-permute-start(bf16[256,128]{1,0:T(8,128)(2,1)S(1)} %convolution_convert_fusion.1.refs_5_), channel_id=1, source_target_pairs={{0,16},{2,18},{4,20},{6,22},{8,24},{10,26},{12,28},{14,30},{16,0},... | collective-permute-start | bytes 196616 | tf_op jit(solution)/shard_map/ppermute | solution.py:45
  38.9 6.5 %collective-permute-start.13 = (bf16[256,128]{1,0:T(8,128)(2,1)S(1)}, bf16[256,128]{1,0:T(8,128)(2,1)S(1)}, u32[]{:S(2)}, u32[]{:S(2)}) collective-permute-start(bf16[256,128]{1,0:T(8,128)(2,1)S(1)} %convolution_convert_fusion.1.refs_5_), channel_id=1, source_target_pairs={{0,8},{2,10},{4,12},{6,14},{8,0},{10,2},{12,4},{14,6},{16,24},{18,... | collective-permute-start | bytes 196616 | tf_op jit(solution)/shard_map/ppermute | solution.py:45
  40.0 6.1 %collective-permute-start.15 = (bf16[256,128]{1,0:T(8,128)(2,1)S(1)}, bf16[256,128]{1,0:T(8,128)(2,1)S(1)}, u32[]{:S(2)}, u32[]{:S(2)}) collective-permute-start(bf16[256,128]{1,0:T(8,128)(2,1)S(1)} %convolution_convert_fusion.1.refs_5_), channel_id=1, source_target_pairs={{0,24},{2,26},{4,28},{6,30},{8,16},{10,18},{12,20},{14,22},{16,8},... | collective-permute-start | bytes 196616 | tf_op jit(solution)/shard_map/ppermute | solution.py:45
  41.9 6.3 %collective-permute-start.21 = (bf16[256,128]{1,0:T(8,128)(2,1)S(1)}, bf16[256,128]{1,0:T(8,128)(2,1)S(1)}, u32[]{:S(2)}, u32[]{:S(2)}) collective-permute-start(bf16[256,128]{1,0:T(8,128)(2,1)S(1)} %convolution_convert_fusion.1.refs_5_), channel_id=1, source_target_pairs={{0,6},{2,4},{4,2},{6,0},{8,14},{10,12},{12,10},{14,8},{16,22},{18,... | collective-permute-start | bytes 196616 | tf_op jit(solution)/shard_map/ppermute | solution.py:45
  42.7 7.3 %collective-permute-start.20 = (bf16[256,128]{1,0:T(8,128)(2,1)S(1)}, bf16[256,128]{1,0:T(8,128)(2,1)S(1)}, u32[]{:S(2)}, u32[]{:S(2)}) collective-permute-start(bf16[256,128]{1,0:T(8,128)(2,1)S(1)} %convolution_convert_fusion.1.refs_5_), channel_id=1, source_target_pairs={{0,4},{2,6},{4,0},{6,2},{8,12},{10,14},{12,8},{14,10},{16,20},{18,... | collective-permute-start | bytes 196616 | tf_op jit(solution)/shard_map/ppermute | solution.py:45
  44.0 5.9 %collective-permute-start.19 = (bf16[256,128]{1,0:T(8,128)(2,1)S(1)}, bf16[256,128]{1,0:T(8,128)(2,1)S(1)}, u32[]{:S(2)}, u32[]{:S(2)}) collective-permute-start(bf16[256,128]{1,0:T(8,128)(2,1)S(1)} %convolution_convert_fusion.1.refs_5_), channel_id=1, source_target_pairs={{0,2},{2,0},{4,6},{6,4},{8,10},{10,8},{12,14},{14,12},{16,18},{18,... | collective-permute-start | bytes 196616 | tf_op jit(solution)/shard_map/ppermute | solution.py:45
  46.1 8.7 %collective-permute-start.18 = (bf16[256,384]{1,0:T(8,128)(2,1)S(1)}, bf16[256,384]{1,0:T(8,128)(2,1)S(1)}, u32[]{:S(2)}, u32[]{:S(2)}) collective-permute-start(bf16[256,384]{1,0:T(8,128)(2,1)S(1)} %constant_dynamic-update-slice_fusion.refs_6_), channel_id=1, source_target_pairs={{0,6},{2,4},{4,2},{6,0},{8,14},{10,12},{12,10},{14,8},{16,22},{18,... | collective-permute-start | bytes 589832 | tf_op jit(solution)/shard_map/ppermute | solution.py:45
  47.0 9.3 %collective-permute-start.17 = (bf16[256,384]{1,0:T(8,128)(2,1)S(1)}, bf16[256,384]{1,0:T(8,128)(2,1)S(1)}, u32[]{:S(2)}, u32[]{:S(2)}) collective-permute-start(bf16[256,384]{1,0:T(8,128)(2,1)S(1)} %constant_dynamic-update-slice_fusion.refs_6_), channel_id=1, source_target_pairs={{0,4},{2,6},{4,0},{6,2},{8,12},{10,14},{12,8},{14,10},{16,20},{18,... | collective-permute-start | bytes 589832 | tf_op jit(solution)/shard_map/ppermute | solution.py:45
  48.2 8.6 %collective-permute-start.16 = (bf16[256,384]{1,0:T(8,128)(2,1)S(1)}, bf16[256,384]{1,0:T(8,128)(2,1)S(1)}, u32[]{:S(2)}, u32[]{:S(2)}) collective-permute-start(bf16[256,384]{1,0:T(8,128)(2,1)S(1)} %constant_dynamic-update-slice_fusion.refs_6_), channel_id=1, source_target_pairs={{0,2},{2,0},{4,6},{6,4},{8,10},{10,8},{12,14},{14,12},{16,18},{18,... | collective-permute-start | bytes 589832 | tf_op jit(solution)/shard_map/ppermute | solution.py:45

commit v6 on v5

--- a/solution.py
+++ b/solution.py
@@ -337,12 +337,6 @@
     place = 0
     for (offset, slots), chunk, part in zip(held, chunks, parts):
         width = part.shape[1] // len(slots)
-        for k, slot in enumerate(slots):
-            start = ((near_index ^ offset) * far + (far_index ^ slot)) * width
-            cols = pl.ds(pl.multiple_of(start, width), width)
-            send(part.at[:, k * width : (k + 1) * width], coupling_ref, cols)
-    for (offset, slots), chunk, part in zip(held, chunks, parts):
-        width = part.shape[1] // len(slots)
         removed = jnp.dot(basis_ref[...], part[...], preferred_element_type=jnp.float32)
         for k, slot in enumerate(slots):
             inner = (far_index ^ slot) * width
@@ -352,6 +346,7 @@
             start = (near_index ^ offset) * far * width + inner
             cols = pl.ds(pl.multiple_of(start, width), width)
             send(work.at[:, place : place + width], updated_ref, cols)
+            send(part.at[:, k * width : (k + 1) * width], coupling_ref, cols)
             place += width
     for copy in copies:
         copy.wait()

time: 58.1 us -> 58.3 us (level)
  no operation moved by 1% of the time
where the time goes in v6:
time: 58.3 us; the launch traced here: 58.2 us
  starting transfers between devices  28.8 us (49%)
  waiting for transfers between devices  13.6 us (23%)
  Pallas kernels  12 us (21%)
  blocking collectives  2.18 us (4%)
  between operations  0.75 us (1%)
  matrix products  0.71 us (1%)
    ppermute x21, starting transfers between devices, swap(): lax.ppermute(value, 'row', [(i, i ^ offset) for i in range(self.rows)])  28.7 us
    ppermute x21, waiting for transfers between devices, swap(): lax.ppermute(value, 'row', [(i, i ^ offset) for i in range(self.rows)])  12.4 us
    pallas_call x1, Pallas kernels, cholesky_pair(): pl.pallas_call(factor_kernel, out_shape=[out, out], in_specs=[VMEM] * 2,...  7.31 us
    pallas_call x2, Pallas kernels, update_part(): pl.pallas_call(functools.partial(update_kernel, near, far, held), out_sha...  2.62 us
    all_gather x1, blocking collectives, local(): gathered = lax.all_gather(stacked, 'col', axis=1, tiled=True)  2.18 us
    pallas_call x1, Pallas kernels, masked_chunks(): pl.pallas_call(functools.partial(chunk_kernel, groups.near), out_shape=[o...  1.25 us
    ppermute x1, waiting for transfers between devices, local(): lax.ppermute(gram_own, 'col', [(i, i ^ 1) for i in range(groups.cols)])  1.25 us
  transfers between devices with their start and end apart: 22, of which 9 were waited for; matrix products, arithmetic and copies ran while one was open for 1% of the time, Pallas kernels for 18%

profile of v6, /device:TPU:0, one launch (start us, length us, event | category | flops | bytes accessed | tf_op | source)
XLA Modules:
  0.0 58.2 jit_solution(6320433157111950148)
XLA Ops:
  0.6 0.0 copy-start
  0.6 3.0 %collective-permute-start.1 = (bf16[256,128]{1,0:T(8,128)(2,1)}, bf16[256,128]{1,0:T(8,128)(2,1)S(1)}, u32[]{:S(2)}, u32[]{:S(2)}) collective-permute-start(bf16[256,128]{1,0:T(8,128)(2,1)} %param.3), channel_id=1, source_target_pairs={{0,4},{2,6},{4,0},{6,2},{8,12},{10,14},{12,8},{14,10},{16,20},{18,... | collective-permute-start | bytes 196616 | tf_op jit(solution)/shard_map/ppermute | solution.py:45
  3.7 1.5 %collective-permute-start = (bf16[256,128]{1,0:T(8,128)(2,1)}, bf16[256,128]{1,0:T(8,128)(2,1)S(1)}, u32[]{:S(2)}, u32[]{:S(2)}) collective-permute-start(bf16[256,128]{1,0:T(8,128)(2,1)} %param.3), channel_id=1, source_target_pairs={{0,2},{2,0},{4,6},{6,4},{8,10},{10,8},{12,14},{14,12},{16,18},{18,... | collective-permute-start | bytes 196616 | tf_op jit(solution)/shard_map/ppermute | solution.py:45
  5.2 0.0 collective-permute-start.2
  5.2 1.3 %chunks.1 = (bf16[256,512]{1,0:T(8,128)(2,1)S(1)}, bf16[256,512]{1,0:T(8,128)(2,1)S(1)}, bf16[256,512]{1,0:T(8,128)(2,1)S(1)}, bf16[256,512]{1,0:T(8,128)(2,1)S(1)}) custom-call(s32[1,8]{1,0:T(1,128)} %mask_hbm.1, bf16[256,2048]{1,0:T(8,128)(2,1)} %trailing_hbm.1), custom_call_target="tpu_custom_call" | custom-call | tf_op jit(solution)/shard_map/chunks/pallas_call | solution.py:306
  6.5 2.0 %collective-permute-start.7 = (bf16[256,512]{1,0:T(8,128)(2,1)S(1)}, bf16[256,512]{1,0:T(8,128)(2,1)S(1)}, u32[]{:S(2)}, u32[]{:S(2)}) collective-permute-start(bf16[256,512]{1,0:T(8,128)(2,1)S(1)} %get-tuple-element.24.refs_2_.refs_0_), channel_id=1, source_target_pairs={{0,2},{2,0},{4,6},{6,4},{8,10},{10,8},{12,14},{14,12},{16,18},{18,... | collective-permute-start | bytes 786440 | tf_op jit(solution)/shard_map/ppermute | solution.py:45
  8.5 1.5 %collective-permute-start.8 = (bf16[256,512]{1,0:T(8,128)(2,1)S(1)}, bf16[256,512]{1,0:T(8,128)(2,1)S(1)}, u32[]{:S(2)}, u32[]{:S(2)}) collective-permute-start(bf16[256,512]{1,0:T(8,128)(2,1)S(1)} %get-tuple-element.25.refs_3_.refs_1_), channel_id=1, source_target_pairs={{0,4},{2,6},{4,0},{6,2},{8,12},{10,14},{12,8},{14,10},{16,20},{18,... | collective-permute-start | bytes 786440 | tf_op jit(solution)/shard_map/ppermute | solution.py:45
  10.0 0.0 collective-permute-done.1
  10.0 0.0 collective-permute-start.9
  10.0 0.0 collective-permute-done
  10.0 1.2 %collective-permute-done.2 = bf16[256,128]{1,0:T(8,128)(2,1)S(1)} collective-permute-done((bf16[256,128]{1,0:T(8,128)(2,1)}, bf16[256,128]{1,0:T(8,128)(2,1)S(1)}, u32[]{:S(2)}, u32[]{:S(2)}) %collective-permute-start.2) | collective-permute-done | bytes 65568 | tf_op jit(solution)/shard_map/ppermute | solution.py:45
  11.2 0.0 copy-done
  11.3 2.2 %all_gather.3.panel_ref = bf16[1024,256]{1,0:T(8,128)(2,1)S(1)} all-gather(bf16[1024,128]{1,0:T(8,128)(2,1)S(1)} %pad_maximum_fusion), channel_id=1, replica_groups=mesh['row'=16,'col'=2] {'col'}, dimensions={1}, use_global_device_ids=true | all-gather | bytes 786432 | tf_op jit(solution)/shard_map/all_gather | solution.py:434
  13.5 0.4 gram_part.1
  13.8 3.7 %collective-permute-start.5 = (f32[136,128]{1,0:T(8,128)S(1)}, f32[136,128]{1,0:T(8,128)S(1)}, u32[]{:S(2)}, u32[]{:S(2)}) collective-permute-start(f32[136,128]{1,0:T(8,128)S(1)} %get-tuple-element.21), channel_id=1, source_target_pairs={{0,24},{2,26},{4,28},{6,30},{8,16},{10,18},{12,20},{14,22},{16,8},... | collective-permute-start | bytes 208904 | tf_op jit(solution)/shard_map/ppermute | solution.py:45
  17.5 0.0 collective-permute-start.4
  17.5 0.0 collective-permute-done.7.refs_1_
  17.5 0.8 %collective-permute-start.3 = (f32[136,128]{1,0:T(8,128)S(1)}, f32[136,128]{1,0:T(8,128)S(1)}, u32[]{:S(2)}, u32[]{:S(2)}) collective-permute-start(f32[136,128]{1,0:T(8,128)S(1)} %get-tuple-element.21), channel_id=1, source_target_pairs={{0,8},{2,10},{4,12},{6,14},{8,0},{10,2},{12,4},{14,6},{16,24},{18,... | collective-permute-start | bytes 208904 | tf_op jit(solution)/shard_map/ppermute | solution.py:45
  18.3 3.4 %collective-permute-done.8.refs_2_ = bf16[256,512]{1,0:T(8,128)(2,1)S(1)} collective-permute-done((bf16[256,512]{1,0:T(8,128)(2,1)S(1)}, bf16[256,512]{1,0:T(8,128)(2,1)S(1)}, u32[]{:S(2)}, u32[]{:S(2)}) %collective-permute-start.8) | collective-permute-done | bytes 262176 | tf_op jit(solution)/shard_map/ppermute | solution.py:45
  21.7 0.0 collective-permute-done.9.refs_3_
  21.7 0.5 cross_part.1
  22.2 1.6 %collective-permute-start.10 = (f32[256,128]{1,0:T(8,128)S(1)}, f32[256,128]{1,0:T(8,128)S(1)}, u32[]{:S(2)}, u32[]{:S(2)}) collective-permute-start(f32[256,128]{1,0:T(8,128)S(1)} %get-tuple-element.30), channel_id=1, source_target_pairs={{0,8},{2,10},{4,12},{6,14},{8,0},{10,2},{12,4},{14,6},{16,24},{18,... | collective-permute-start | bytes 393224 | tf_op jit(solution)/shard_map/ppermute | solution.py:45
  23.9 2.6 %collective-permute-start.11 = (f32[256,128]{1,0:T(8,128)S(1)}, f32[256,128]{1,0:T(8,128)S(1)}, u32[]{:S(2)}, u32[]{:S(2)}) collective-permute-start(f32[256,128]{1,0:T(8,128)S(1)} %get-tuple-element.31), channel_id=1, source_target_pairs={{0,16},{2,18},{4,20},{6,22},{8,24},{10,26},{12,28},{14,30},{16,0},... | collective-permute-start | bytes 393224 | tf_op jit(solution)/shard_map/ppermute | solution.py:45
  26.5 0.0 collective-permute-done.5
  26.5 0.2 collective-permute-start.12
  26.7 0.0 collective-permute-done.4
  26.7 0.0 collective-permute-done.3
  26.7 0.1 collective-permute-start.6
  26.8 1.2 %collective-permute-done.6.other_ref = f32[136,128]{1,0:T(8,128)S(1)} collective-permute-done((f32[136,128]{1,0:T(8,128)S(1)}, f32[136,128]{1,0:T(8,128)S(1)}, u32[]{:S(2)}, u32[]{:S(2)}) %collective-permute-start.6) | collective-permute-done | bytes 69664 | tf_op jit(solution)/shard_map/ppermute | solution.py:443
  28.0 7.3 %factor.1 = (f32[256,256]{1,0:T(8,128)}, f32[256,256]{1,0:T(8,128)S(1)}) custom-call(f32[136,128]{1,0:T(8,128)S(1)} %add_add_fusion.own_ref, f32[136,128]{1,0:T(8,128)S(1)} %collective-permute-done.6.other_ref), custom_call_target="tpu_custom_call" | custom-call | flops 134217728 | bytes 3145728 | tf_op jit(solution)/shard_map/factor/pallas_call | solution.py:191
  35.3 0.0 collective-permute-done.10
  35.3 0.1 collective-permute-done.11
  35.5 0.0 collective-permute-done.12
  35.5 0.4 convolution_convert_fusion.1.refs_5_
  35.9 3.1 %collective-permute-start.14 = (bf16[256,128]{1,0:T(8,128)(2,1)S(1)}, bf16[256,128]{1,0:T(8,128)(2,1)S(1)}, u32[]{:S(2)}, u32[]{:S(2)}) collective-permute-start(bf16[256,128]{1,0:T(8,128)(2,1)S(1)} %convolution_convert_fusion.1.refs_5_), channel_id=1, source_target_pairs={{0,16},{2,18},{4,20},{6,22},{8,24},{10,26},{12,28},{14,30},{16,0},... | collective-permute-start | bytes 196616 | tf_op jit(solution)/shard_map/ppermute | solution.py:45
  38.9 1.0 %collective-permute-start.13 = (bf16[256,128]{1,0:T(8,128)(2,1)S(1)}, bf16[256,128]{1,0:T(8,128)(2,1)S(1)}, u32[]{:S(2)}, u32[]{:S(2)}) collective-permute-start(bf16[256,128]{1,0:T(8,128)(2,1)S(1)} %convolution_convert_fusion.1.refs_5_), channel_id=1, source_target_pairs={{0,8},{2,10},{4,12},{6,14},{8,0},{10,2},{12,4},{14,6},{16,24},{18,... | collective-permute-start | bytes 196616 | tf_op jit(solution)/shard_map/ppermute | solution.py:45
  40.0 0.5 collective-permute-start.15
  40.5 1.4 %collective-permute-done.14 = bf16[256,128]{1,0:T(8,128)(2,1)S(1)} collective-permute-done((bf16[256,128]{1,0:T(8,128)(2,1)S(1)}, bf16[256,128]{1,0:T(8,128)(2,1)S(1)}, u32[]{:S(2)}, u32[]{:S(2)}) %collective-permute-start.14) | collective-permute-done | bytes 65568 | tf_op jit(solution)/shard_map/ppermute | solution.py:45
  41.9 0.8 %collective-permute-start.21 = (bf16[256,128]{1,0:T(8,128)(2,1)S(1)}, bf16[256,128]{1,0:T(8,128)(2,1)S(1)}, u32[]{:S(2)}, u32[]{:S(2)}) collective-permute-start(bf16[256,128]{1,0:T(8,128)(2,1)S(1)} %convolution_convert_fusion.1.refs_5_), channel_id=1, source_target_pairs={{0,6},{2,4},{4,2},{6,0},{8,14},{10,12},{12,10},{14,8},{16,22},{18,... | collective-permute-start | bytes 196616 | tf_op jit(solution)/shard_map/ppermute | solution.py:45
  42.7 1.3 %collective-permute-start.20 = (bf16[256,128]{1,0:T(8,128)(2,1)S(1)}, bf16[256,128]{1,0:T(8,128)(2,1)S(1)}, u32[]{:S(2)}, u32[]{:S(2)}) collective-permute-start(bf16[256,128]{1,0:T(8,128)(2,1)S(1)} %convolution_convert_fusion.1.refs_5_), channel_id=1, source_target_pairs={{0,4},{2,6},{4,0},{6,2},{8,12},{10,14},{12,8},{14,10},{16,20},{18,... | collective-permute-start | bytes 196616 | tf_op jit(solution)/shard_map/ppermute | solution.py:45
  44.0 1.4 %collective-permute-start.19 = (bf16[256,128]{1,0:T(8,128)(2,1)S(1)}, bf16[256,128]{1,0:T(8,128)(2,1)S(1)}, u32[]{:S(2)}, u32[]{:S(2)}) collective-permute-start(bf16[256,128]{1,0:T(8,128)(2,1)S(1)} %convolution_convert_fusion.1.refs_5_), channel_id=1, source_target_pairs={{0,2},{2,0},{4,6},{6,4},{8,10},{10,8},{12,14},{14,12},{16,18},{18,... | collective-permute-start | bytes 196616 | tf_op jit(solution)/shard_map/ppermute | solution.py:45
  45.4 0.0 collective-permute-done.13
  45.5 0.6 %collective-permute-done.15 = bf16[256,128]{1,0:T(8,128)(2,1)S(1)} collective-permute-done((bf16[256,128]{1,0:T(8,128)(2,1)S(1)}, bf16[256,128]{1,0:T(8,128)(2,1)S(1)}, u32[]{:S(2)}, u32[]{:S(2)}) %collective-permute-start.15) | collective-permute-done | bytes 65568 | tf_op jit(solution)/shard_map/ppermute | solution.py:45
  46.1 1.0 %collective-permute-start.18 = (bf16[256,384]{1,0:T(8,128)(2,1)S(1)}, bf16[256,384]{1,0:T(8,128)(2,1)S(1)}, u32[]{:S(2)}, u32[]{:S(2)}) collective-permute-start(bf16[256,384]{1,0:T(8,128)(2,1)S(1)} %constant_dynamic-update-slice_fusion.refs_6_), channel_id=1, source_target_pairs={{0,6},{2,4},{4,2},{6,0},{8,14},{10,12},{12,10},{14,8},{16,22},{18,... | collective-permute-start | bytes 589832 | tf_op jit(solution)/shard_map/ppermute | solution.py:45
  47.0 1.1 %collective-permute-start.17 = (bf16[256,384]{1,0:T(8,128)(2,1)S(1)}, bf16[256,384]{1,0:T(8,128)(2,1)S(1)}, u32[]{:S(2)}, u32[]{:S(2)}) collective-permute-start(bf16[256,384]{1,0:T(8,128)(2,1)S(1)} %constant_dynamic-update-slice_fusion.refs_6_), channel_id=1, source_target_pairs={{0,4},{2,6},{4,0},{6,2},{8,12},{10,14},{12,8},{14,10},{16,20},{18,... | collective-permute-start | bytes 589832 | tf_op jit(solution)/shard_map/ppermute | solution.py:45
  48.2 0.0 collective-permute-done.21.refs_9_
  48.2 1.5 %collective-permute-start.16 = (bf16[256,384]{1,0:T(8,128)(2,1)S(1)}, bf16[256,384]{1,0:T(8,128)(2,1)S(1)}, u32[]{:S(2)}, u32[]{:S(2)}) collective-permute-start(bf16[256,384]{1,0:T(8,128)(2,1)S(1)} %constant_dynamic-update-slice_fusion.refs_6_), channel_id=1, source_target_pairs={{0,2},{2,0},{4,6},{6,4},{8,10},{10,8},{12,14},{14,12},{16,18},{18,... | collective-permute-start | bytes 589832 | tf_op jit(solution)/shard_map/ppermute | solution.py:45
  49.7 0.3 convolution_convert_fusion.basis_ref
  50.0 0.0 collective-permute-done.20.refs_8_
  50.0 0.0 collective-permute-done.19.refs_7_
  50.0 1.2 %update.2 = (bf16[256,2048]{1,0:T(8,128)(2,1)}, bf16[256,2048]{1,0:T(8,128)(2,1)}) custom-call(bf16[256,256]{1,0:T(8,128)(2,1)S(1)} %convolution_convert_fusion.basis_ref, bf16[256,512]{1,0:T(8,128)(2,1)S(1)} %get-tuple-element.28.refs_0_.refs_1_, bf16[256,512]{1,0:T(8,128)(2,1)S(1)} %get-tuple-element.28.refs_0_.refs_1_, ...), custom_call_target="tpu_custom_call" | custom-call | flops 117440512 | bytes 3670016 | tf_op jit(solution)/shard_map/update/pallas_call | solution.py:363
  51.3 3.5 %collective-permute-done.18.refs_5_ = bf16[256,384]{1,0:T(8,128)(2,1)S(1)} collective-permute-done((bf16[256,384]{1,0:T(8,128)(2,1)S(1)}, bf16[256,384]{1,0:T(8,128)(2,1)S(1)}, u32[]{:S(2)}, u32[]{:S(2)}) %collective-permute-start.18) | collective-permute-done | bytes 196640 | tf_op jit(solution)/shard_map/ppermute | solution.py:45
  54.8 1.5 %collective-permute-done.17.refs_4_ = bf16[256,384]{1,0:T(8,128)(2,1)S(1)} collective-permute-done((bf16[256,384]{1,0:T(8,128)(2,1)S(1)}, bf16[256,384]{1,0:T(8,128)(2,1)S(1)}, u32[]{:S(2)}, u32[]{:S(2)}) %collective-permute-start.17) | collective-permute-done | bytes 196640 | tf_op jit(solution)/shard_map/ppermute | solution.py:45
  56.3 0.4 collective-permute-done.16.refs_3_
  56.8 1.4 %update.3 = (bf16[256,2048]{1,0:T(8,128)(2,1)}, bf16[256,2048]{1,0:T(8,128)(2,1)}) custom-call(bf16[256,256]{1,0:T(8,128)(2,1)S(1)} %convolution_convert_fusion.basis_ref, bf16[256,512]{1,0:T(8,128)(2,1)S(1)} %get-tuple-element.24.refs_2_.refs_0_, ...), custom_call_target="tpu_custom_call", output_to_operand_aliasing={{0}: (7, {}), {1}: (8, {})} | custom-call | flops 150994944 | bytes 4718592 | tf_op jit(solution)/shard_map/update/pallas_call | solution.py:363
  (5 shorter events, 0.1 us)
Async XLA Ops:
  0.6 10.6 %copy-start = (bf16[256,128]{1,0:T(8,128)(2,1)S(1)}, bf16[256,128]{1,0:T(8,128)(2,1)}, u32[]{:S(2)}) copy-start(bf16[256,128]{1,0:T(8,128)(2,1)} %param.3) | copy-start | bytes 196612
  0.6 9.3 %collective-permute-start.1 = (bf16[256,128]{1,0:T(8,128)(2,1)}, bf16[256,128]{1,0:T(8,128)(2,1)S(1)}, u32[]{:S(2)}, u32[]{:S(2)}) collective-permute-start(bf16[256,128]{1,0:T(8,128)(2,1)} %param.3), channel_id=1, source_target_pairs={{0,4},{2,6},{4,0},{6,2},{8,12},{10,14},{12,8},{14,10},{16,20},{18,... | collective-permute-start | bytes 196616 | tf_op jit(solution)/shard_map/ppermute | solution.py:45
  3.7 6.4 %collective-permute-start = (bf16[256,128]{1,0:T(8,128)(2,1)}, bf16[256,128]{1,0:T(8,128)(2,1)S(1)}, u32[]{:S(2)}, u32[]{:S(2)}) collective-permute-start(bf16[256,128]{1,0:T(8,128)(2,1)} %param.3), channel_id=1, source_target_pairs={{0,2},{2,0},{4,6},{6,4},{8,10},{10,8},{12,14},{14,12},{16,18},{18,... | collective-permute-start | bytes 196616 | tf_op jit(solution)/shard_map/ppermute | solution.py:45
  5.2 6.1 %collective-permute-start.2 = (bf16[256,128]{1,0:T(8,128)(2,1)}, bf16[256,128]{1,0:T(8,128)(2,1)S(1)}, u32[]{:S(2)}, u32[]{:S(2)}) collective-permute-start(bf16[256,128]{1,0:T(8,128)(2,1)} %param.3), channel_id=1, source_target_pairs={{0,6},{2,4},{4,2},{6,0},{8,14},{10,12},{12,10},{14,8},{16,22},{18,... | collective-permute-start | bytes 196616 | tf_op jit(solution)/shard_map/ppermute | solution.py:45
  6.5 11.0 %collective-permute-start.7 = (bf16[256,512]{1,0:T(8,128)(2,1)S(1)}, bf16[256,512]{1,0:T(8,128)(2,1)S(1)}, u32[]{:S(2)}, u32[]{:S(2)}) collective-permute-start(bf16[256,512]{1,0:T(8,128)(2,1)S(1)} %get-tuple-element.24.refs_2_.refs_0_), channel_id=1, source_target_pairs={{0,2},{2,0},{4,6},{6,4},{8,10},{10,8},{12,14},{14,12},{16,18},{18,... | collective-permute-start | bytes 786440 | tf_op jit(solution)/shard_map/ppermute | solution.py:45
  8.5 13.2 %collective-permute-start.8 = (bf16[256,512]{1,0:T(8,128)(2,1)S(1)}, bf16[256,512]{1,0:T(8,128)(2,1)S(1)}, u32[]{:S(2)}, u32[]{:S(2)}) collective-permute-start(bf16[256,512]{1,0:T(8,128)(2,1)S(1)} %get-tuple-element.25.refs_3_.refs_1_), channel_id=1, source_target_pairs={{0,4},{2,6},{4,0},{6,2},{8,12},{10,14},{12,8},{14,10},{16,20},{18,... | collective-permute-start | bytes 786440 | tf_op jit(solution)/shard_map/ppermute | solution.py:45
  10.0 11.7 %collective-permute-start.9 = (bf16[256,512]{1,0:T(8,128)(2,1)S(1)}, bf16[256,512]{1,0:T(8,128)(2,1)S(1)}, u32[]{:S(2)}, u32[]{:S(2)}) collective-permute-start(bf16[256,512]{1,0:T(8,128)(2,1)S(1)} %get-tuple-element.26.refs_4_.refs_2_), channel_id=1, source_target_pairs={{0,6},{2,4},{4,2},{6,0},{8,14},{10,12},{12,10},{14,8},{16,22},{18,... | collective-permute-start | bytes 786440 | tf_op jit(solution)/shard_map/ppermute | solution.py:45
  13.8 12.6 %collective-permute-start.5 = (f32[136,128]{1,0:T(8,128)S(1)}, f32[136,128]{1,0:T(8,128)S(1)}, u32[]{:S(2)}, u32[]{:S(2)}) collective-permute-start(f32[136,128]{1,0:T(8,128)S(1)} %get-tuple-element.21), channel_id=1, source_target_pairs={{0,24},{2,26},{4,28},{6,30},{8,16},{10,18},{12,20},{14,22},{16,8},... | collective-permute-start | bytes 208904 | tf_op jit(solution)/shard_map/ppermute | solution.py:45
  17.5 9.2 %collective-permute-start.4 = (f32[136,128]{1,0:T(8,128)S(1)}, f32[136,128]{1,0:T(8,128)S(1)}, u32[]{:S(2)}, u32[]{:S(2)}) collective-permute-start(f32[136,128]{1,0:T(8,128)S(1)} %get-tuple-element.21), channel_id=1, source_target_pairs={{0,16},{2,18},{4,20},{6,22},{8,24},{10,26},{12,28},{14,30},{16,0},... | collective-permute-start | bytes 208904 | tf_op jit(solution)/shard_map/ppermute | solution.py:45
  17.5 9.2 %collective-permute-start.3 = (f32[136,128]{1,0:T(8,128)S(1)}, f32[136,128]{1,0:T(8,128)S(1)}, u32[]{:S(2)}, u32[]{:S(2)}) collective-permute-start(f32[136,128]{1,0:T(8,128)S(1)} %get-tuple-element.21), channel_id=1, source_target_pairs={{0,8},{2,10},{4,12},{6,14},{8,0},{10,2},{12,4},{14,6},{16,24},{18,... | collective-permute-start | bytes 208904 | tf_op jit(solution)/shard_map/ppermute | solution.py:45
  22.2 13.1 %collective-permute-start.10 = (f32[256,128]{1,0:T(8,128)S(1)}, f32[256,128]{1,0:T(8,128)S(1)}, u32[]{:S(2)}, u32[]{:S(2)}) collective-permute-start(f32[256,128]{1,0:T(8,128)S(1)} %get-tuple-element.30), channel_id=1, source_target_pairs={{0,8},{2,10},{4,12},{6,14},{8,0},{10,2},{12,4},{14,6},{16,24},{18,... | collective-permute-start | bytes 393224 | tf_op jit(solution)/shard_map/ppermute | solution.py:45
  23.9 11.6 %collective-permute-start.11 = (f32[256,128]{1,0:T(8,128)S(1)}, f32[256,128]{1,0:T(8,128)S(1)}, u32[]{:S(2)}, u32[]{:S(2)}) collective-permute-start(f32[256,128]{1,0:T(8,128)S(1)} %get-tuple-element.31), channel_id=1, source_target_pairs={{0,16},{2,18},{4,20},{6,22},{8,24},{10,26},{12,28},{14,30},{16,0},... | collective-permute-start | bytes 393224 | tf_op jit(solution)/shard_map/ppermute | solution.py:45
  26.5 9.0 %collective-permute-start.12 = (f32[256,128]{1,0:T(8,128)S(1)}, f32[256,128]{1,0:T(8,128)S(1)}, u32[]{:S(2)}, u32[]{:S(2)}) collective-permute-start(f32[256,128]{1,0:T(8,128)S(1)} %get-tuple-element.32), channel_id=1, source_target_pairs={{0,24},{2,26},{4,28},{6,30},{8,16},{10,18},{12,20},{14,22},{16,8},... | collective-permute-start | bytes 393224 | tf_op jit(solution)/shard_map/ppermute | solution.py:45
  26.7 1.3 %collective-permute-start.6 = (f32[136,128]{1,0:T(8,128)S(1)}, f32[136,128]{1,0:T(8,128)S(1)}, u32[]{:S(2)}, u32[]{:S(2)}) collective-permute-start(f32[136,128]{1,0:T(8,128)S(1)} %add_add_fusion.own_ref), channel_id=1, source_target_pairs={{0,1},{1,0},{2,3},{3,2},{4,5},{5,4},{6,7},{7,6},{8,9},{9,8},{10,11... | collective-permute-start | bytes 208904 | tf_op jit(solution)/shard_map/ppermute | solution.py:443
  35.9 6.1 %collective-permute-start.14 = (bf16[256,128]{1,0:T(8,128)(2,1)S(1)}, bf16[256,128]{1,0:T(8,128)(2,1)S(1)}, u32[]{:S(2)}, u32[]{:S(2)}) collective-permute-start(bf16[256,128]{1,0:T(8,128)(2,1)S(1)} %convolution_convert_fusion.1.refs_5_), channel_id=1, source_target_pairs={{0,16},{2,18},{4,20},{6,22},{8,24},{10,26},{12,28},{14,30},{16,0},... | collective-permute-start | bytes 196616 | tf_op jit(solution)/shard_map/ppermute | solution.py:45
  38.9 6.5 %collective-permute-start.13 = (bf16[256,128]{1,0:T(8,128)(2,1)S(1)}, bf16[256,128]{1,0:T(8,128)(2,1)S(1)}, u32[]{:S(2)}, u32[]{:S(2)}) collective-permute-start(bf16[256,128]{1,0:T(8,128)(2,1)S(1)} %convolution_convert_fusion.1.refs_5_), channel_id=1, source_target_pairs={{0,8},{2,10},{4,12},{6,14},{8,0},{10,2},{12,4},{14,6},{16,24},{18,... | collective-permute-start | bytes 196616 | tf_op jit(solution)/shard_map/ppermute | solution.py:45
  40.0 6.1 %collective-permute-start.15 = (bf16[256,128]{1,0:T(8,128)(2,1)S(1)}, bf16[256,128]{1,0:T(8,128)(2,1)S(1)}, u32[]{:S(2)}, u32[]{:S(2)}) collective-permute-start(bf16[256,128]{1,0:T(8,128)(2,1)S(1)} %convolution_convert_fusion.1.refs_5_), channel_id=1, source_target_pairs={{0,24},{2,26},{4,28},{6,30},{8,16},{10,18},{12,20},{14,22},{16,8},... | collective-permute-start | bytes 196616 | tf_op jit(solution)/shard_map/ppermute | solution.py:45
  41.9 6.3 %collective-permute-start.21 = (bf16[256,128]{1,0:T(8,128)(2,1)S(1)}, bf16[256,128]{1,0:T(8,128)(2,1)S(1)}, u32[]{:S(2)}, u32[]{:S(2)}) collective-permute-start(bf16[256,128]{1,0:T(8,128)(2,1)S(1)} %convolution_convert_fusion.1.refs_5_), channel_id=1, source_target_pairs={{0,6},{2,4},{4,2},{6,0},{8,14},{10,12},{12,10},{14,8},{16,22},{18,... | collective-permute-start | bytes 196616 | tf_op jit(solution)/shard_map/ppermute | solution.py:45
  42.7 7.3 %collective-permute-start.20 = (bf16[256,128]{1,0:T(8,128)(2,1)S(1)}, bf16[256,128]{1,0:T(8,128)(2,1)S(1)}, u32[]{:S(2)}, u32[]{:S(2)}) collective-permute-start(bf16[256,128]{1,0:T(8,128)(2,1)S(1)} %convolution_convert_fusion.1.refs_5_), channel_id=1, source_target_pairs={{0,4},{2,6},{4,0},{6,2},{8,12},{10,14},{12,8},{14,10},{16,20},{18,... | collective-permute-start | bytes 196616 | tf_op jit(solution)/shard_map/ppermute | solution.py:45
  44.0 5.9 %collective-permute-start.19 = (bf16[256,128]{1,0:T(8,128)(2,1)S(1)}, bf16[256,128]{1,0:T(8,128)(2,1)S(1)}, u32[]{:S(2)}, u32[]{:S(2)}) collective-permute-start(bf16[256,128]{1,0:T(8,128)(2,1)S(1)} %convolution_convert_fusion.1.refs_5_), channel_id=1, source_target_pairs={{0,2},{2,0},{4,6},{6,4},{8,10},{10,8},{12,14},{14,12},{16,18},{18,... | collective-permute-start | bytes 196616 | tf_op jit(solution)/shard_map/ppermute | solution.py:45
  46.1 8.7 %collective-permute-start.18 = (bf16[256,384]{1,0:T(8,128)(2,1)S(1)}, bf16[256,384]{1,0:T(8,128)(2,1)S(1)}, u32[]{:S(2)}, u32[]{:S(2)}) collective-permute-start(bf16[256,384]{1,0:T(8,128)(2,1)S(1)} %constant_dynamic-update-slice_fusion.refs_6_), channel_id=1, source_target_pairs={{0,6},{2,4},{4,2},{6,0},{8,14},{10,12},{12,10},{14,8},{16,22},{18,... | collective-permute-start | bytes 589832 | tf_op jit(solution)/shard_map/ppermute | solution.py:45
  47.0 9.3 %collective-permute-start.17 = (bf16[256,384]{1,0:T(8,128)(2,1)S(1)}, bf16[256,384]{1,0:T(8,128)(2,1)S(1)}, u32[]{:S(2)}, u32[]{:S(2)}) collective-permute-start(bf16[256,384]{1,0:T(8,128)(2,1)S(1)} %constant_dynamic-update-slice_fusion.refs_6_), channel_id=1, source_target_pairs={{0,4},{2,6},{4,0},{6,2},{8,12},{10,14},{12,8},{14,10},{16,20},{18,... | collective-permute-start | bytes 589832 | tf_op jit(solution)/shard_map/ppermute | solution.py:45
  48.2 8.6 %collective-permute-start.16 = (bf16[256,384]{1,0:T(8,128)(2,1)S(1)}, bf16[256,384]{1,0:T(8,128)(2,1)S(1)}, u32[]{:S(2)}, u32[]{:S(2)}) collective-permute-start(bf16[256,384]{1,0:T(8,128)(2,1)S(1)} %constant_dynamic-update-slice_fusion.refs_6_), channel_id=1, source_target_pairs={{0,2},{2,0},{4,6},{6,4},{8,10},{10,8},{12,14},{14,12},{16,18},{18,... | collective-permute-start | bytes 589832 | tf_op jit(solution)/shard_map/ppermute | solution.py:45
